TPU v7x, 32 devices: a whole 2x2x4 slice. The times are simulated.
32 devices in a mesh: groups: 2 (over y), depth: 4 (over z), tm: 2 (over x), tile: 2 (over core).
Axes of the slice: x: 2, y: 2, z: 4, core: 2. Of those that a mesh axis runs over, the one named last changes fastest.
Arguments:
- volume: bfloat16 [8, 8, 64, 2048], P(('groups', 'tm'), 'depth', 'tile'), parts along dimension 0, may hold values from 0.099609375 to 3
- background: float32 [16, 64, 2048], P(('groups', 'depth'), 'tile'), parts along dimension 0, may hold values from 0.05 to 1
- measured: bfloat16 [8, 64, 2048], P(('groups', 'tm'), 'tile'), parts along dimension 0, may hold values from 0.29882812 to 5
- psf: bfloat16 [8, 9, 16, 17], P('depth'), may hold values from 8.1539154e-05 to 0.0016326904
Outputs:
- new_volume: bfloat16 [8, 8, 64, 2048], P(('groups', 'tm'), 'depth', 'tile'), parts along dimension 0
- new_background: float32 [16, 64, 2048], P(('groups', 'depth'), 'tile'), parts along dimension 0
There are 2 independent parts, one for each index of `groups`. A program takes and returns all parts, laid end to end along the dimension named above; an argument that names none is the same for every part. Nothing has to cross between parts.
All inputs are finite; a program needn't handle non-finite values.
Results may differ from a plain program's by a relative error of at most 0.0018.
Values may be sent and summed in bfloat16 or wider, within the bound.
No kernel may reach another device: no remote copies, remote signals or barrier semaphores. Data moves between devices by JAX's collectives and lax.ppermute only.
A program may use at most 64 MiB of HBM per device.

v0:
```python
import math

import jax
import jax.numpy as jnp
from jax import lax
from jax.sharding import PartitionSpec as P


def padded_2(block, sides, width):
    for axis, dim in sides:
        count = lax.axis_size(axis)
        forward = [(i, i + 1) for i in range(count - 1)]
        backward = [(target, source) for source, target in forward]
        low = lax.ppermute(
            lax.slice_in_dim(block, block.shape[dim] - width, None, axis=dim), axis, forward
        )
        high = lax.ppermute(lax.slice_in_dim(block, 0, width, axis=dim), axis, backward)
        block = jnp.concatenate([low, block, high], axis=dim)
    return block


def band_tables(psf, block):
    depth_count = psf.shape[0]
    tap_count = psf.shape[1]
    pitch_cols = psf.shape[2]
    kernel_width = psf.shape[3]
    col_reach = (kernel_width - 1) // 2
    tiled = jnp.tile(psf, (1, 1, block // pitch_cols, 1))
    side = jnp.arange(3, dtype=jnp.int32)[:, None, None] - 1
    row_pos = jnp.arange(block, dtype=jnp.int32)[None, :, None]
    col_pos = jnp.arange(block, dtype=jnp.int32)[None, None, :]
    fwd_offset = col_pos - row_pos - block * side + col_reach
    bwd_offset = row_pos - col_pos + block * side + col_reach
    forward = jnp.zeros((depth_count, tap_count, 3, block, block), jnp.bfloat16)
    backward = jnp.zeros((depth_count, tap_count, 3, block, block), jnp.bfloat16)
    for column in range(kernel_width):
        forward = jnp.where(fwd_offset == column, tiled[:, :, None, :, column, None], forward)
        backward = jnp.where(bwd_offset == column, tiled[:, :, None, None, :, column], backward)
    forward = forward.reshape(depth_count, tap_count, 3 * block, block)
    backward = backward.reshape(depth_count, tap_count, 3 * block, block)
    return (forward, backward)


def with_neighbours(values, block):
    leading = values.shape[:-1]
    blocks = values.reshape(leading + (values.shape[-1] // block, block))
    padded = jnp.pad(blocks, [(0, 0)] * len(leading) + [(1, 1), (0, 0)])
    return jnp.concatenate([padded[..., :-2, :], padded[..., 1:-1, :], padded[..., 2:, :]], axis=-1)


def body(volume, background, measured, psf):
    tap_count = psf.shape[1]
    half_reach = (tap_count - 1) // 2
    pitch_cols = psf.shape[2]
    frame_here = volume.shape[0]
    depth_here = volume.shape[1]
    row_count = volume.shape[2]
    col_count = volume.shape[3]
    block = math.gcd(col_count, 128)
    block_count = col_count // block
    forward, backward = band_tables(psf, block)
    emitters = (volume.astype(jnp.float32) + background[None]).astype(jnp.bfloat16)
    padded = padded_2(emitters, (("tile", 2),), half_reach)
    spread = with_neighbours(padded, block)
    partial_value = jnp.zeros((frame_here, row_count, block_count, block), jnp.float32)
    for offset in range(tap_count):
        window = lax.slice_in_dim(spread, offset, offset + row_count, axis=2)
        partial_value = partial_value + jnp.einsum(
            "fdrjc,dce->frje", window, forward[:, offset], preferred_element_type=jnp.float32
        )
    partial_value = partial_value.reshape(frame_here, row_count, col_count)
    sensor = lax.psum(partial_value, "depth")
    ratio_image = (measured.astype(jnp.float32) / sensor).astype(jnp.bfloat16)
    ratio_pad = padded_2(ratio_image, (("tile", 1),), half_reach)
    ratio_spread = with_neighbours(ratio_pad, block)
    backprojected = jnp.zeros((frame_here, depth_here, row_count, block_count, block), jnp.float32)
    for offset in range(tap_count):
        start_row = tap_count - 1 - offset
        window = lax.slice_in_dim(ratio_spread, start_row, start_row + row_count, axis=1)
        backprojected = backprojected + jnp.einsum(
            "frje,dec->fdrjc", window, backward[:, offset], preferred_element_type=jnp.float32
        )
    backprojected = backprojected.reshape(frame_here, depth_here, row_count, col_count)
    weight = jnp.tile(jnp.sum(psf, axis=(1, 3), dtype=jnp.float32), (1, col_count // pitch_cols))
    new_volume = (volume.astype(jnp.float32) * backprojected / weight[None, :, None, :]).astype(
        jnp.bfloat16
    )
    frame_local = jnp.sum(backprojected, axis=0)
    frame_count = frame_here * lax.axis_size("tm")
    frame_total = lax.psum(frame_local, "tm")
    new_background = background * frame_total / (frame_count * weight[:, None, :])
    return (new_volume, new_background)


def solution(mesh):
    placed = (
        P(("groups", "tm"), "depth", "tile", None),
        P(("groups", "depth"), "tile", None),
        P(("groups", "tm"), "tile", None),
        P("depth", None, None, None),
    )
    return jax.shard_map(
        body,
        mesh=mesh,
        in_specs=placed,
        out_specs=(
            P(("groups", "tm"), "depth", "tile", None),
            P(("groups", "depth"), "tile", None),
        ),
        check_vma=False,
    )
```

profile of v0, /device:TPU:0, one launch (start us, length us, event | category | flops | bytes accessed | tf_op | source)
XLA Modules:
  0.0 129.8 jit_solution(13692091582985638470)
XLA Ops:
  7.2 1.3 fusion.9
  8.6 1.3 collective-permute-start.1
  9.9 3.0 %collective-permute-start = (bf16[2,2,4,2048]{3,2,1,0:T(4,128)(2,1)S(1)}, bf16[2,2,4,2048]{3,2,1,0:T(4,128)(2,1)S(1)}, u32[]{:S(2)}, u32[]{:S(2)}) collective-permute-start(bf16[2,2,4,2048]{3,2,1,0:T(4,128)(2,1)S(1)} %get-tuple-element.4), channel_id=1, source_target_pairs={{0,1},{2,3},{4,5},{6,7},{8,9},{10,11},{12,13},{14,15},{16,17},{18,... | collective-permute-start | bytes 196616 | tf_op jit(solution)/shard_map/ppermute | solution.py:14
  13.3 0.6 tile.18
  14.9 1.2 fusion.48
  16.0 16.6 %select_select_fusion = bf16[2,9,384,128]{3,2,0,1:T(8,128)(2,1)S(1)} fusion(pred[384,128]{1,0:T(8,128)(4,1)S(1)} %get-tuple-element.76, pred[384,128]{1,0:T(8,128)(4,1)S(1)} %get-tuple-element.75, pred[384,128]{1,0:T(8,128)(4,1)S(1)} %get-tuple-element.74, pred[384,128]{1,0:T(8,128)(4,1)S(1)} %get-tuple-element.73, ...), kind=kLoop, calls=%fused_computation.1 | loop fusion | flops 15040512 | bytes 2840064 | tf_op jit(solution)/shard_map/jit(_where)/select_n | solution.py:37
  34.1 0.6 convolution_bitcast_fusion.1
  35.3 0.6 convolution_bitcast_fusion.3
  37.0 0.6 convolution_bitcast_fusion.6
  37.6 0.6 convolution_bitcast_fusion.7
  38.1 0.6 fusion.8
  38.8 0.9 reshape.231
  39.9 3.9 %select_select_fusion.1 = bf16[2,9,384,128]{3,2,0,1:T(8,128)(2,1)S(1)} fusion(pred[384,128]{1,0:T(8,128)(4,1)S(1)} %get-tuple-element.28, pred[384,128]{1,0:T(8,128)(4,1)S(1)} %get-tuple-element.29, pred[384,128]{1,0:T(8,128)(4,1)S(1)} %get-tuple-element.30, pred[384,128]{1,0:T(8,128)(4,1)S(1)} %get-tuple-element.31, ...), kind=kLoop, calls=%fused_computation.2 | loop fusion | flops 15040512 | bytes 2683392 | tf_op jit(solution)/shard_map/jit(_where)/select_n | solution.py:38
  43.8 37.0 %all-reduce.5.cloned.1.call-done = f32[2,32,2048]{2,1,0:T(8,128)} async-done(((f32[2,32,2048]{2,1,0:T(8,128)}), f32[2,32,2048]{2,1,0:T(8,128)}) %all-reduce.5.cloned.1.call-update) | async-done | bytes 524304 | tf_op jit(solution)/shard_map/psum | solution.py:72
  80.8 1.1 divide_convert_fusion
  82.0 1.3 collective-permute-start.3
  83.3 3.0 %collective-permute-start.2 = (bf16[2,4,2048]{2,1,0:T(4,128)(2,1)S(1)}, bf16[2,4,2048]{2,1,0:T(4,128)(2,1)S(1)}, u32[]{:S(2)}, u32[]{:S(2)}) collective-permute-start(bf16[2,4,2048]{2,1,0:T(4,128)(2,1)S(1)} %get-tuple-element.8), channel_id=1, source_target_pairs={{0,1},{2,3},{4,5},{6,7},{8,9},{10,11},{12,13},{14,15},{16,17},{18,... | collective-permute-start | bytes 98312 | tf_op jit(solution)/shard_map/ppermute | solution.py:14
  86.6 0.6 collective-permute-done.2
  91.5 0.8 copy_bitcast_fusion
  92.3 1.6 %copy.22 = f32[2,2,32,16,128]{4,3,2,1,0:T(8,128)} copy(f32[2,2,32,16,128]{4,2,3,0,1:T(8,128)S(1)} %get-tuple-element.79) | data formatting | bytes 2097152 | tf_op jit(solution)/shard_map/add | solution.py:80
  93.9 1.4 %reshape.233 = f32[2,2,32,2048]{3,2,1,0:T(8,128)S(1)} reshape(f32[2,2,32,16,128]{4,3,2,1,0:T(8,128)} %copy.22) | data formatting | bytes 2097152 | tf_op jit(solution)/shard_map/reshape | solution.py:83
  95.4 0.9 fusion.11
  96.3 24.7 %all-reduce.7.cloned.1.call-done = f32[2,32,2048]{2,1,0:T(8,128)} async-done(((f32[2,32,2048]{2,1,0:T(8,128)}), f32[2,32,2048]{2,1,0:T(8,128)}) %all-reduce.7.cloned.1.call-update) | async-done | bytes 524304 | tf_op jit(solution)/shard_map/psum | solution.py:90
  121.1 1.9 %multiply_divide_fusion = f32[2,32,2048]{2,1,0:T(8,128)} fusion(f32[2,32,2048]{2,1,0:T(8,128)S(1)} %copy-done, f32[2,32,2048]{2,1,0:T(8,128)} %all-reduce.7.cloned.1.call-done, f32[2,2048]{1,0:T(2,128)S(1)} %broadcast_multiply_fusion), kind=kLoop, calls=%fused_computation.49 | loop fusion | flops 262144 | bytes 1589248 | tf_op jit(solution)/shard_map/div | solution.py:91
  (80 shorter events, 9.1 us)
Async XLA Ops:
  7.2 5.9 %copy-start.2 = (bf16[2,9,16,17]{3,2,1,0:T(8,128)(2,1)S(1)}, bf16[2,9,16,17]{3,2,1,0:T(8,128)(2,1)}, u32[]{:S(2)}) copy-start(bf16[2,9,16,17]{3,2,1,0:T(8,128)(2,1)} %param.7) | copy-start | bytes 29380
  7.2 73.6 %all-reduce.5.cloned.1.call-start = ((), (), s32[]{:S(2)}) async-start(), calls=%async_computation | async-start | bytes 1048576 | tf_op jit(solution)/shard_map/psum | solution.py:72
  8.6 24.0 %collective-permute-start.1 = (bf16[2,2,4,2048]{3,2,1,0:T(4,128)(2,1)S(1)}, bf16[2,2,4,2048]{3,2,1,0:T(4,128)(2,1)S(1)}, u32[]{:S(2)}, u32[]{:S(2)}) collective-permute-start(bf16[2,2,4,2048]{3,2,1,0:T(4,128)(2,1)S(1)} %get-tuple-element.5), channel_id=1, source_target_pairs={{1,0},{3,2},{5,4},{7,6},{9,8},{11,10},{13,12},{15,14},{17,16},{19,... | collective-permute-start | bytes 196616 | tf_op jit(solution)/shard_map/ppermute | solution.py:17
  9.9 22.7 %collective-permute-start = (bf16[2,2,4,2048]{3,2,1,0:T(4,128)(2,1)S(1)}, bf16[2,2,4,2048]{3,2,1,0:T(4,128)(2,1)S(1)}, u32[]{:S(2)}, u32[]{:S(2)}) collective-permute-start(bf16[2,2,4,2048]{3,2,1,0:T(4,128)(2,1)S(1)} %get-tuple-element.4), channel_id=1, source_target_pairs={{0,1},{2,3},{4,5},{6,7},{8,9},{10,11},{12,13},{14,15},{16,17},{18,... | collective-permute-start | bytes 196616 | tf_op jit(solution)/shard_map/ppermute | solution.py:14
  39.6 41.2 %copy-start.3 = (bf16[2,32,2048]{2,1,0:T(8,128)(2,1)S(1)}, bf16[2,32,2048]{2,1,0:T(8,128)(2,1)}, u32[]{:S(2)}) copy-start(bf16[2,32,2048]{2,1,0:T(8,128)(2,1)} %param.6) | copy-start | bytes 786436
  39.7 81.4 %all-reduce.7.cloned.1.call-start = ((), (), s32[]{:S(2)}) async-start(), calls=%async_computation.1 | async-start | bytes 1048576 | tf_op jit(solution)/shard_map/psum | solution.py:90
  82.0 4.6 %collective-permute-start.3 = (bf16[2,4,2048]{2,1,0:T(4,128)(2,1)S(1)}, bf16[2,4,2048]{2,1,0:T(4,128)(2,1)S(1)}, u32[]{:S(2)}, u32[]{:S(2)}) collective-permute-start(bf16[2,4,2048]{2,1,0:T(4,128)(2,1)S(1)} %get-tuple-element.9), channel_id=1, source_target_pairs={{1,0},{3,2},{5,4},{7,6},{9,8},{11,10},{13,12},{15,14},{17,16},{19,... | collective-permute-start | bytes 98312 | tf_op jit(solution)/shard_map/ppermute | solution.py:17
  83.3 3.9 %collective-permute-start.2 = (bf16[2,4,2048]{2,1,0:T(4,128)(2,1)S(1)}, bf16[2,4,2048]{2,1,0:T(4,128)(2,1)S(1)}, u32[]{:S(2)}, u32[]{:S(2)}) collective-permute-start(bf16[2,4,2048]{2,1,0:T(4,128)(2,1)S(1)} %get-tuple-element.8), channel_id=1, source_target_pairs={{0,1},{2,3},{4,5},{6,7},{8,9},{10,11},{12,13},{14,15},{16,17},{18,... | collective-permute-start | bytes 98312 | tf_op jit(solution)/shard_map/ppermute | solution.py:14
  92.3 3.0 %copy-start.1 = (bf16[2,2,32,2048]{3,2,1,0:T(8,128)(2,1)S(1)}, bf16[2,2,32,2048]{3,2,1,0:T(8,128)(2,1)}, u32[]{:S(2)}) copy-start(bf16[2,2,32,2048]{3,2,1,0:T(8,128)(2,1)} %param.4) | copy-start | bytes 1572868
  93.9 27.2 %copy-start = (f32[2,32,2048]{2,1,0:T(8,128)S(1)}, f32[2,32,2048]{2,1,0:T(8,128)}, u32[]{:S(2)}) copy-start(f32[2,32,2048]{2,1,0:T(8,128)} %param.5) | copy-start | bytes 1572868
Sparse Core Ops, SparseCore 0:
  39.8 40.9 all-reduce.4
  92.4 28.5 all-reduce.6
where the time goes:
time: 130 us
  waiting for transfers between devices  62.4 us (48%)
  other arithmetic  27.5 us (21%)
  between operations  14.6 us (11%)
  matrix products  9.06 us (7%)
  starting transfers between devices  8.91 us (7%)
  local copies, waits for them, and re-layouts  7.37 us (6%)
    psum x1, waiting for transfers between devices, body(): sensor = lax.psum(partial_value, 'depth')  37 us
    psum x1, waiting for transfers between devices, body(): frame_total = lax.psum(frame_local, 'tm')  24.7 us
    select_n x1, other arithmetic, band_tables(): jnp.where(fwd_offset == column, tiled[:, :, None, :, column, None], forward)  16.6 us
    ppermute x2, starting transfers between devices, padded_2(): lax.ppermute(lax.slice_in_dim(block, block.shape[dim] - width, None, axis...  6.06 us
    dot_general x9, matrix products, body(): jnp.einsum('fdrjc,dce->frje', window, forward[:, offset], preferred_eleme...  5.2 us
    select_n x1, other arithmetic, band_tables(): jnp.where(bwd_offset == column, tiled[:, :, None, None, :, column], backw...  3.9 us
    dot_general x9, matrix products, body(): jnp.einsum('frje,dec->fdrjc', window, backward[:, offset], preferred_elem...  3.86 us
  transfers between devices with their start and end apart: 6, of which 3 were waited for; matrix products, arithmetic and copies ran while one was open for 21% of the time, Pallas kernels for 0%

commit v1 on v0

v1 whole, which is shorter than its diff:
```python
import functools

import jax
import jax.numpy as jnp
from jax import lax
from jax.experimental import pallas as pl
from jax.experimental.pallas import tpu as pltpu
from jax.sharding import PartitionSpec as P

LANES = 128
F32 = jnp.float32
BF16 = jnp.bfloat16


def rotated(base_ref, row, pitch):
    base = base_ref[pl.ds(row, pitch), :]
    return jnp.concatenate([base if g == 0 else pltpu.roll(base, pitch * g, 1) for g in range(LANES // pitch)], axis=0)


def fill_base(psf_ref, base_ref):
    depth, taps, pitch, width = psf_ref.shape
    reach = (width - 1) // 2
    base_ref[...] = jnp.zeros_like(base_ref)
    for d in range(depth):
        for t in range(taps):
            base_ref[pl.ds((d * taps + t) * pitch, pitch), pl.ds(0, width)] = psf_ref[d, t].astype(F32)
    for d in range(depth):
        for t in range(taps):
            rows = pl.ds((d * taps + t) * pitch, pitch)
            base_ref[rows, :] = pltpu.roll(base_ref[rows, :], LANES - reach, 1, stride=1, stride_axis=0)


def near_mask(width):
    reach = (width - 1) // 2
    row = lax.broadcasted_iota(jnp.int32, (LANES, LANES), 0)
    col = lax.broadcasted_iota(jnp.int32, (LANES, LANES), 1)
    return jnp.abs(row - col) <= reach


def forward_table_kernel(psf_ref, table_ref, base_ref):
    depth, taps, pitch, width = psf_ref.shape
    fill_base(psf_ref, base_ref)
    near = near_mask(width)
    for d in range(depth):
        for t in range(2 * table_ref.shape[1]):
            lanes = pl.ds((t % 2) * LANES, LANES)
            if t < taps:
                band = rotated(base_ref, (d * taps + t) * pitch, pitch)
                table_ref[d, t // 2, pl.ds(0, LANES), lanes] = jnp.where(near, band, 0.0).astype(BF16)
                table_ref[d, t // 2, pl.ds(LANES, LANES), lanes] = jnp.where(near, 0.0, band).astype(BF16)
            else:
                table_ref[d, t // 2, :, lanes] = jnp.zeros((2 * LANES, LANES), BF16)


def backward_table_kernel(psf_ref, measured_ref, got_ref, table_ref, inverse_ref, chunk_ref, base_ref, rows_ref):
    depth, taps, pitch, width = psf_ref.shape
    frames, row_count, col_count = measured_ref.shape
    blocks = col_count // LANES
    extra = got_ref.shape[1]
    chunk_rows = chunk_ref.shape[1]
    fill_base(psf_ref, base_ref)
    near = near_mask(width)
    for d in range(depth):
        total = jnp.zeros((1, LANES), F32)
        lanes = pl.ds(d * LANES, LANES)
        for t in range(taps):
            band = rotated(base_ref, (d * taps + t) * pitch, pitch).T
            total = total + jnp.sum(band, axis=0, keepdims=True)
            table_ref[t, pl.ds(0, LANES), lanes] = jnp.where(near, band, 0.0).astype(BF16)
            table_ref[t, pl.ds(LANES, LANES), lanes] = jnp.where(near, 0.0, band).astype(BF16)
        inverse_ref[d] = 1.0 / total
    tile = lax.axis_index("tile")
    place = lax.axis_index("depth")
    per_frame = rows_ref.shape[0] // frames
    rows_ref[...] = jnp.ones_like(rows_ref)
    for f in range(frames):
        own = f * per_frame + extra * blocks * tile
        other = f * per_frame + row_count * blocks * (1 - tile)
        for j in range(blocks):
            lanes = pl.ds(j * LANES, LANES)
            values = measured_ref[f, :, lanes].astype(F32)
            rows_ref[pl.ds(own + j, row_count, stride=blocks), :] = values
            values = got_ref[f, :, lanes].astype(F32)
            rows_ref[pl.ds(other + j, extra, stride=blocks), :] = values
        for r in range(chunk_rows):
            start = pl.multiple_of(f * per_frame + (place * chunk_rows + r) * blocks, blocks)
            chunk_ref[f, r] = rows_ref[pl.ds(start, blocks), :]


def with_edges(rows_ref, start, count, blocks, after_mask, before_mask):
    here = rows_ref[pl.ds(start, count), :]
    after = rows_ref[pl.ds(start + 1, count), :]
    before = rows_ref[pl.ds(start - 1, count), :]
    edges = jnp.where(after_mask, after, jnp.where(before_mask, before, 0.0))
    return here.astype(BF16), edges.astype(BF16)


def edge_masks(count, blocks):
    row = lax.rem(lax.broadcasted_iota(jnp.int32, (count, LANES), 0), blocks)
    lane = lax.broadcasted_iota(jnp.int32, (count, LANES), 1)
    after = jnp.logical_and(lane < LANES // 2, row < blocks - 1)
    before = jnp.logical_and(lane >= LANES // 2, row > 0)
    return after, before


PAD = 8


def sensor_kernel(chunks, volume_ref, background_ref, got_ref, table_ref, own_ref, *rest):
    sent_refs = rest[: chunks - 1]
    rows_ref, left_ref, sums_ref, whole_ref = rest[chunks - 1 :]
    frames, depth, row_count, col_count = volume_ref.shape
    blocks = col_count // LANES
    pairs = table_ref.shape[1]
    halo = got_ref.shape[2]
    half = halo // 2
    sensor_rows = row_count + half
    windows = sensor_rows + halo + 1
    span = windows * blocks
    tile = lax.axis_index("tile")
    place = lax.axis_index("depth")
    use_after, use_before = edge_masks(blocks, blocks)
    for f in range(frames):
        for d in range(depth):
            first = PAD + (f * depth + d) * span
            own = first + (half + half * tile) * blocks
            other = first + (row_count + half) * blocks * (1 - tile)
            empty = pl.multiple_of(first + (row_count + halo) * blocks * tile, 8)
            rows_ref[pl.ds(empty, half * blocks), :] = jnp.zeros((half * blocks, LANES), F32)
            rows_ref[pl.ds(first + (windows - 1) * blocks, blocks), :] = jnp.zeros((blocks, LANES), F32)
            for j in range(blocks):
                lanes = pl.ds(j * LANES, LANES)
                total = (volume_ref[f, d, :, lanes].astype(F32) + background_ref[d, :, lanes]).astype(BF16).astype(F32)
                rows_ref[pl.ds(own + j, row_count, stride=blocks), :] = total
                rows_ref[pl.ds(other + j, halo, stride=blocks), :] = got_ref[f, d, :, lanes].astype(F32)
            for r in range(windows):
                start = first + r * blocks
                here, edges = with_edges(rows_ref, start, blocks, blocks, use_after, use_before)
                left_ref[pl.ds(start - PAD, blocks), pl.ds(0, LANES)] = here
                left_ref[pl.ds(start - PAD, blocks), pl.ds(LANES, LANES)] = edges
    size = (sensor_rows + 1) * blocks
    chunk_rows = own_ref.shape[1]
    for f in range(frames):
        total = None
        for d in range(depth):
            for p in range(pairs):
                left = left_ref[pl.ds((f * depth + d) * span + 2 * p * blocks, size), :]
                product = jnp.dot(left, table_ref[d, p], preferred_element_type=F32)
                total = product if total is None else total + product
        sums_ref[...] = total
        count = sensor_rows * blocks
        whole_ref[f, pl.ds(0, count), :] = sums_ref[pl.ds(0, count), pl.ds(0, LANES)] + sums_ref[pl.ds(blocks, count), pl.ds(LANES, LANES)]
        if whole_ref.shape[1] > count:
            whole_ref[f, pl.ds(count, whole_ref.shape[1] - count), :] = jnp.ones((whole_ref.shape[1] - count, LANES), F32)
        for s in range(chunks):
            target = lax.rem(place + s, chunks)
            for r in range(chunk_rows):
                start = pl.multiple_of((target * chunk_rows + r) * blocks, blocks)
                values = whole_ref[f, pl.ds(start, blocks), :]
                if s == 0:
                    own_ref[f, r] = values
                else:
                    sent_refs[s - 1][f, r] = values.astype(BF16)


def spread_ratio(chunks, images, get, rows_ref, left_ref, row_count, half, blocks):
    tile = lax.axis_index("tile")
    place = lax.axis_index("depth")
    use_after, use_before = edge_masks(blocks, blocks)
    windows = row_count + 2 * half
    span = windows * blocks
    sensor_rows = row_count + half
    for f in range(images):
        first = PAD + f * max(windows, chunks * get.rows + half) * blocks
        empty = pl.multiple_of(first + sensor_rows * blocks * tile, 8)
        base = first + half * blocks * (1 - tile)
        for s in range(chunks):
            source = lax.rem(place + chunks - s, chunks)
            chunk_rows = get.rows
            for r in range(chunk_rows):
                start = pl.multiple_of(base + (source * chunk_rows + r) * blocks, 8)
                rows_ref[pl.ds(start, blocks), :] = get(s, f, r)
        rows_ref[pl.ds(empty, half * blocks), :] = jnp.zeros((half * blocks, LANES), F32)
        for r in range(windows):
            here, edges = with_edges(rows_ref, first + r * blocks, blocks, blocks, use_after, use_before)
            left_ref[pl.ds(f * span + r * blocks, blocks), pl.ds(0, LANES)] = here
            left_ref[pl.ds(f * span + r * blocks, blocks), pl.ds(LANES, LANES)] = edges


class Chunk:
    def __init__(self, rows, read):
        self.rows = rows
        self.read = read

    def __call__(self, s, f, r):
        return self.read(s, f, r)


def backproject(f, span, taps, row_count, blocks, left_ref, table_ref):
    total = None
    for t in range(taps):
        left = left_ref[pl.ds(f * span + (taps - 1 - t) * blocks, row_count * blocks), :]
        product = jnp.dot(left, table_ref[t], preferred_element_type=F32)
        total = product if total is None else total + product
    return total


def volume_kernel(chunks, half, *refs):
    ratio_refs = refs[:chunks]
    volume_ref, table_ref, inverse_ref, out_ref, rows_ref, left_ref, sums_ref = refs[chunks:]
    frames, depth, row_count, col_count = volume_ref.shape
    blocks = col_count // LANES
    taps = table_ref.shape[0]
    get = Chunk(ratio_refs[0].shape[1], lambda s, f, r: ratio_refs[s][f, r].astype(F32))
    spread_ratio(chunks, frames, get, rows_ref, left_ref, row_count, half, blocks)
    span = (row_count + 2 * half) * blocks
    for f in range(frames):
        total = backproject(f, span, taps, row_count, blocks, left_ref, table_ref)
        for d in range(depth):
            start = (f * depth + d) * row_count * blocks
            sums_ref[pl.ds(start, row_count * blocks), :] = total[:, d * LANES : (d + 1) * LANES]
            for j in range(blocks):
                lanes = pl.ds(j * LANES, LANES)
                back = sums_ref[pl.ds(start + j, row_count, stride=blocks), :]
                value = volume_ref[f, d, :, lanes].astype(F32) * back * inverse_ref[d]
                out_ref[f, d, :, lanes] = value.astype(BF16)


def background_kernel(chunks, half, scale, summed_ref, got_ref, background_ref, table_ref, inverse_ref, out_ref, rows_ref, left_ref, sums_ref):
    depth, row_count, col_count = background_ref.shape
    blocks = col_count // LANES
    taps = table_ref.shape[0]
    get = Chunk(summed_ref.shape[1], lambda s, f, r: summed_ref[s, r].astype(F32) + got_ref[s, r].astype(F32))
    spread_ratio(chunks, 1, get, rows_ref, left_ref, row_count, half, blocks)
    span = (row_count + 2 * half) * blocks
    total = backproject(0, span, taps, row_count, blocks, left_ref, table_ref)
    for d in range(depth):
        start = d * row_count * blocks
        sums_ref[pl.ds(start, row_count * blocks), :] = total[:, d * LANES : (d + 1) * LANES]
        for j in range(blocks):
            lanes = pl.ds(j * LANES, LANES)
            back = sums_ref[pl.ds(start + j, row_count, stride=blocks), :]
            out_ref[d, :, lanes] = background_ref[d, :, lanes] * back * (inverse_ref[d] * scale)


def whole(count):
    return [pl.BlockSpec(memory_space=pltpu.VMEM)] * count


def call(kernel, args, outs, scratch, flops):
    moved = sum(a.size * a.dtype.itemsize for a in args)
    return pl.pallas_call(
        kernel,
        out_shape=outs,
        in_specs=whole(len(args)),
        out_specs=jax.tree.map(lambda _: pl.BlockSpec(memory_space=pltpu.VMEM), outs),
        scratch_shapes=scratch,
        compiler_params=pltpu.CompilerParams(vmem_limit_bytes=40 * 2**20),
        cost_estimate=pl.CostEstimate(flops=flops, bytes_accessed=moved, transcendentals=0),
    )(*args)


def body(volume, background, measured, psf):
    frames, depth, row_count, col_count = volume.shape
    taps, pitch, width = psf.shape[1:]
    half = (taps - 1) // 2
    blocks = col_count // LANES
    pairs = (taps + 1) // 2
    chunks = lax.axis_size("depth")
    splits = lax.axis_size("tm")
    sensor_rows = row_count + half
    chunk_rows = -(-sensor_rows // chunks)
    shape = jax.ShapeDtypeStruct
    vmem = pltpu.VMEM

    tile = lax.axis_index("tile")
    swap = [(0, 1), (1, 0)]

    def edge(values, width, axis):
        size = values.shape[axis]
        return jnp.where(
            tile == 0,
            lax.slice_in_dim(values, size - width, size, axis=axis),
            lax.slice_in_dim(values, 0, width, axis=axis),
        )

    border = (edge(volume, 2 * half, 2).astype(F32) + edge(background, 2 * half, 1)[None]).astype(BF16)
    border = lax.ppermute(border, "tile", swap)
    measured_border = lax.ppermute(edge(measured, half, 1), "tile", swap)

    base = vmem((depth * taps * pitch, LANES), F32)
    forward = call(
        forward_table_kernel,
        (psf,),
        shape((depth, pairs, 2 * LANES, 2 * LANES), BF16),
        [base],
        2 * 10**8,
    )
    windows = sensor_rows + 2 * half + 1
    padded_rows = chunks * chunk_rows
    chunk = (frames, chunk_rows, blocks, LANES)
    parts = call(
        functools.partial(sensor_kernel, chunks),
        (volume, background, border, forward),
        (shape(chunk, F32),) + (shape(chunk, BF16),) * (chunks - 1),
        [
            vmem((frames * depth * windows * blocks + 2 * PAD, LANES), F32),
            vmem((frames * depth * windows * blocks, 2 * LANES), BF16),
            vmem(((sensor_rows + 1) * blocks, 2 * LANES), F32),
            vmem((frames, padded_rows * blocks, LANES), F32),
        ],
        2 * 10**9,
    )
    sensor = parts[0]
    moved = [
        lax.ppermute(parts[s], "depth", [(i, (i + s) % chunks) for i in range(chunks)])
        for s in range(1, chunks)
    ]
    backward, inverse, measured_chunk = call(
        backward_table_kernel,
        (psf, measured, measured_border),
        (
            shape((taps, 2 * LANES, depth * LANES), BF16),
            shape((depth, 1, LANES), F32),
            shape(chunk, F32),
        ),
        [base, vmem((frames * padded_rows * blocks, LANES), F32)],
        2 * 10**8,
    )
    for part in moved:
        sensor = sensor + part.astype(F32)
    ratio = (measured_chunk / sensor).astype(BF16)
    ratios = [ratio] + [
        lax.ppermute(ratio, "depth", [(i, (i + s) % chunks) for i in range(chunks)])
        for s in range(1, chunks)
    ]
    summed = jnp.stack([jnp.sum(r.astype(F32), axis=0) for r in ratios]).astype(BF16)
    if splits == 2:
        others = lax.ppermute(summed, "tm", swap)
    else:
        total = lax.psum(summed.astype(F32), "tm").astype(BF16)
        summed, others = total, jnp.zeros_like(total)
    window_rows = max(row_count + 2 * half, padded_rows + half) * blocks
    new_volume = call(
        functools.partial(volume_kernel, chunks, half),
        (*ratios, volume, backward, inverse),
        shape(volume.shape, BF16),
        [
            vmem((frames * window_rows + 2 * PAD, LANES), F32),
            vmem((frames * (row_count + 2 * half) * blocks, 2 * LANES), BF16),
            vmem((frames * depth * row_count * blocks, LANES), F32),
        ],
        2 * 10**9,
    )
    new_background = call(
        functools.partial(background_kernel, chunks, half, 1.0 / (frames * splits)),
        (summed, others, background, backward, inverse),
        shape(background.shape, F32),
        [
            vmem((window_rows + 2 * PAD, LANES), F32),
            vmem(((row_count + 2 * half) * blocks, 2 * LANES), BF16),
            vmem((depth * row_count * blocks, LANES), F32),
        ],
        10**9,
    )
    return new_volume, new_background


def solution(mesh):
    placed = (
        P(("groups", "tm"), "depth", "tile", None),
        P(("groups", "depth"), "tile", None),
        P(("groups", "tm"), "tile", None),
        P("depth", None, None, None),
    )
    return jax.shard_map(
        body,
        mesh=mesh,
        in_specs=placed,
        out_specs=(
            P(("groups", "tm"), "depth", "tile", None),
            P(("groups", "depth"), "tile", None),
        ),
        check_vma=False,
    )
```

time: 130 us -> 34.7 us (0.27)
  waiting for transfers between devices: 62.4 us -> 9.61 us
  other arithmetic: 27.5 us -> 2.25 us
  between operations: 14.6 us -> 0.76 us
  matrix products: 9.06 us -> 0 us
  Pallas kernels: 0 us -> 7.85 us
  local copies, waits for them, and re-layouts: 7.37 us -> 0.9 us
  starting transfers between devices: 8.91 us -> 13.1 us
    psum x2 -> x0, waiting for transfers between devices: 61.7 us -> none  [the longest x1 37 us: body(): sensor = lax.psum(partial_value, 'depth')]
    select_n x2, other arithmetic: 20.5 us -> 1.1 us  [edge(): jnp.where(tile == 0, lax.slice_in_dim(values, size - width, size, axis=ax...]
    dot_general x18 -> x0, matrix products: 9.06 us -> none  [the longest x9 5.2 us: body(): jnp.einsum('fdrjc,dce->frje', window, forward[:, offset], preferred_eleme...]
    ppermute x4 -> x9, waiting for transfers between devices: 0.6 us -> 9.61 us  [the longest x3 4.76 us: body(): lax.ppermute(ratio, 'depth', [(i, (i + s) % chunks) for i in range(chunks)])]
    pallas_call x0 -> x5, Pallas kernels: none -> 7.85 us  [call(): pl.pallas_call(kernel, out_shape=outs, in_specs=whole(len(args)), out_spe...]
    ppermute x4 -> x9, starting transfers between devices: 8.65 us -> 13.1 us  [the longest x3 6.64 us: body(): lax.ppermute(parts[s], 'depth', [(i, (i + s) % chunks) for i in range(chu...]
    convert_element_type x3 -> x1, other arithmetic: 3.37 us -> 1.02 us  [body(): (edge(volume, 2 * half, 2).astype(F32) + edge(background, 2 * half, 1)[No...]
    reshape x2 -> x0, local copies, waits for them, and re-layouts: 2.32 us -> none  [the longest x1 1.44 us: body(): backprojected.reshape(frame_here, depth_here, row_count, col_count)]
  transfers between devices with their start and end apart: 6 -> 9, of which waited for: 3 -> 7; matrix products, arithmetic and copies ran while one was open for 21% -> 0% of each run, Pallas kernels for 0% -> 11%
where the time goes in v1:
time: 34.7 us; the launch traced here: 34.5 us
  starting transfers between devices  13.1 us (38%)
  waiting for transfers between devices  9.61 us (28%)
  Pallas kernels  7.85 us (23%)
  other arithmetic  2.25 us (6%)
  local copies, waits for them, and re-layouts  0.9 us (3%)
  between operations  0.76 us (2%)
    pallas_call x5, Pallas kernels, call(): pl.pallas_call(kernel, out_shape=outs, in_specs=whole(len(args)), out_spe...  7.85 us
    ppermute x3, starting transfers between devices, body(): lax.ppermute(parts[s], 'depth', [(i, (i + s) % chunks) for i in range(chu...  6.64 us
    ppermute x3, waiting for transfers between devices, body(): lax.ppermute(ratio, 'depth', [(i, (i + s) % chunks) for i in range(chunks)])  4.76 us
    ppermute x3, starting transfers between devices, body(): lax.ppermute(ratio, 'depth', [(i, (i + s) % chunks) for i in range(chunks)])  4.31 us
    ppermute x3, waiting for transfers between devices, body(): lax.ppermute(parts[s], 'depth', [(i, (i + s) % chunks) for i in range(chu...  2.19 us
    ppermute x1, starting transfers between devices, body(): others = lax.ppermute(summed, 'tm', swap)  1.56 us
    ppermute x1, waiting for transfers between devices, body(): others = lax.ppermute(summed, 'tm', swap)  1.47 us
    ppermute x1, waiting for transfers between devices, body(): measured_border = lax.ppermute(edge(measured, half, 1), 'tile', swap)  1.19 us
  transfers between devices with their start and end apart: 9, of which 7 were waited for; matrix products, arithmetic and copies ran while one was open for 0% of the time, Pallas kernels for 11%

profile of v1, /device:TPU:0, one launch (start us, length us, event | category | flops | bytes accessed | tf_op | source)
XLA Modules:
  0.0 34.5 jit_solution(3843391906232477837)
XLA Ops:
  0.7 1.1 %slice_select_fusion = f32[2,8,2048]{2,1,0:T(8,128)S(1)} fusion(f32[2,32,2048]{2,1,0:T(8,128)} %background_ref.3, pred[]{:T(512)S(6)} %eq.2), kind=kLoop, calls=%fused_computation.3 | loop fusion | flops 32768 | bytes 393217 | tf_op jit(solution)/shard_map/jit(_where)/select_n | solution.py:281
  1.7 1.0 %add_convert_fusion = bf16[2,2,8,2048]{3,2,1,0:T(8,128)(2,1)S(1)} fusion(f32[2,8,2048]{2,1,0:T(8,128)S(1)} %slice_select_fusion, bf16[2,2,32,2048]{3,2,1,0:T(8,128)(2,1)} %refs_4_.1, pred[]{:T(512)S(6)} %eq.2), kind=kLoop, calls=%fused_computation | loop fusion | flops 262144 | bytes 524289 | tf_op jit(solution)/shard_map/convert_element_type | solution.py:287
  2.8 0.5 %collective-permute-start.1 = (bf16[2,2,8,2048]{3,2,1,0:T(8,128)(2,1)S(1)}, bf16[2,2,8,2048]{3,2,1,0:T(8,128)(2,1)S(1)}, u32[]{:S(2)}, u32[]{:S(2)}) collective-permute-start(bf16[2,2,8,2048]{3,2,1,0:T(8,128)(2,1)S(1)} %add_convert_fusion), channel_id=1, source_target_pairs={{0,1},{1,0},{2,3},{3,2},{4,5},{5,4},{6,7},{7,6},{8,9},{9,8},{10,11... | collective-permute-start | bytes 393224 | tf_op jit(solution)/shard_map/ppermute | solution.py:288
  3.3 0.9 %copy-done.2 = bf16[2,9,16,17]{3,2,1,0:T(8,128)(2,1)S(1)} copy-done((bf16[2,9,16,17]{3,2,1,0:T(8,128)(2,1)S(1)}, bf16[2,9,16,17]{3,2,1,0:T(8,128)(2,1)}, u32[]{:S(2)}) %copy-start.2) | copy-done | bytes 9816
  4.2 0.3 shard_map.60.table_ref
  4.5 2.2 %shard_map.61 = (f32[2,9,16,128]{3,2,1,0:T(8,128)S(1)}, bf16[2,9,16,128]{3,2,1,0:T(8,128)(2,1)S(1)}, bf16[2,9,16,128]{3,2,1,0:T(8,128)(2,1)S(1)}, bf16[2,9,16,128]{3,2,1,0:T(8,128)(2,1)S(1)}) custom-call(bf16[2,2,32,2048]{3,2,1,0:T(8,128)(2,1)S(1)} %copy-done, f32[2,32,2048]{2,1,0:T(8,128)S(1)} %copy-done.1, ...), custom_call_target="tpu_custom_call" | custom-call | flops 2000000000 | bytes 2490368 | tf_op jit(solution)/shard_map/pallas_call | solution.py:252
  6.8 2.7 %collective-permute-start.2 = (bf16[2,9,16,128]{3,2,1,0:T(8,128)(2,1)S(1)}, bf16[2,9,16,128]{3,2,1,0:T(8,128)(2,1)S(1)}, u32[]{:S(2)}, u32[]{:S(2)}) collective-permute-start(bf16[2,9,16,128]{3,2,1,0:T(8,128)(2,1)S(1)} %get-tuple-element.11), channel_id=1, source_target_pairs={{0,4},{4,8},{8,12},{12,0},{1,5},{5,9},{9,13},{13,1},{2,6},{6,10},{... | collective-permute-start | bytes 221192 | tf_op jit(solution)/shard_map/ppermute | solution.py:316
  9.5 2.6 %collective-permute-start.3 = (bf16[2,9,16,128]{3,2,1,0:T(8,128)(2,1)S(1)}, bf16[2,9,16,128]{3,2,1,0:T(8,128)(2,1)S(1)}, u32[]{:S(2)}, u32[]{:S(2)}) collective-permute-start(bf16[2,9,16,128]{3,2,1,0:T(8,128)(2,1)S(1)} %get-tuple-element.12), channel_id=1, source_target_pairs={{0,8},{4,12},{8,0},{12,4},{1,9},{5,13},{9,1},{13,5},{2,10},{6,14},... | collective-permute-start | bytes 221192 | tf_op jit(solution)/shard_map/ppermute | solution.py:316
  12.1 1.3 %collective-permute-start.4 = (bf16[2,9,16,128]{3,2,1,0:T(8,128)(2,1)S(1)}, bf16[2,9,16,128]{3,2,1,0:T(8,128)(2,1)S(1)}, u32[]{:S(2)}, u32[]{:S(2)}) collective-permute-start(bf16[2,9,16,128]{3,2,1,0:T(8,128)(2,1)S(1)} %get-tuple-element.13), channel_id=1, source_target_pairs={{0,12},{4,0},{8,4},{12,8},{1,13},{5,1},{9,5},{13,9},{2,14},{6,2},{... | collective-permute-start | bytes 221192 | tf_op jit(solution)/shard_map/ppermute | solution.py:316
  13.5 0.1 collective-permute-start
  13.5 1.2 %collective-permute-done.got_ref = bf16[2,4,2048]{2,1,0:T(4,128)(2,1)S(1)} collective-permute-done((bf16[2,4,2048]{2,1,0:T(4,128)(2,1)S(1)}, bf16[2,4,2048]{2,1,0:T(4,128)(2,1)S(1)}, u32[]{:S(2)}, u32[]{:S(2)}) %collective-permute-start) | collective-permute-done | bytes 32800 | tf_op jit(solution)/shard_map/ppermute | solution.py:289
  14.7 1.0 %shard_map.59 = (bf16[9,256,256]{2,1,0:T(8,128)(2,1)S(1)}, f32[2,1,128]{2,1,0:T(1,128)S(1)}, f32[2,9,16,128]{3,2,1,0:T(8,128)S(1)}) custom-call(bf16[2,9,16,17]{3,2,1,0:T(8,128)(2,1)S(1)} %copy-done.2, bf16[2,32,2048]{2,1,0:T(8,128)(2,1)S(1)} %copy-done.3, bf16[2,4,2048]{2,1,0:T(4,128)(2,1)S(1)} %collective-permute-done.got_ref), custom_call_target="tpu_custom_call" | custom-call | flops 200000000 | bytes 304704 | tf_op jit(solution)/shard_map/pallas_call | solution.py:252
  15.7 1.9 %collective-permute-done.3 = bf16[2,9,16,128]{3,2,1,0:T(8,128)(2,1)S(1)} collective-permute-done((bf16[2,9,16,128]{3,2,1,0:T(8,128)(2,1)S(1)}, bf16[2,9,16,128]{3,2,1,0:T(8,128)(2,1)S(1)}, u32[]{:S(2)}, u32[]{:S(2)}) %collective-permute-start.3) | collective-permute-done | bytes 73760 | tf_op jit(solution)/shard_map/ppermute | solution.py:316
  17.7 0.2 collective-permute-done.4
  18.0 1.9 %collective-permute-start.5 = (bf16[2,9,16,128]{3,2,1,0:T(8,128)(2,1)S(1)}, bf16[2,9,16,128]{3,2,1,0:T(8,128)(2,1)S(1)}, u32[]{:S(2)}, u32[]{:S(2)}) collective-permute-start(bf16[2,9,16,128]{3,2,1,0:T(8,128)(2,1)S(1)} %get-tuple-element.17.refs_0_), channel_id=1, source_target_pairs={{0,4},{4,8},{8,12},{12,0},{1,5},{5,9},{9,13},{13,1},{2,6},{6,10},{... | collective-permute-start | bytes 221192 | tf_op jit(solution)/shard_map/ppermute | solution.py:334
  19.8 1.6 %collective-permute-start.6 = (bf16[2,9,16,128]{3,2,1,0:T(8,128)(2,1)S(1)}, bf16[2,9,16,128]{3,2,1,0:T(8,128)(2,1)S(1)}, u32[]{:S(2)}, u32[]{:S(2)}) collective-permute-start(bf16[2,9,16,128]{3,2,1,0:T(8,128)(2,1)S(1)} %get-tuple-element.17.refs_0_), channel_id=1, source_target_pairs={{0,8},{4,12},{8,0},{12,4},{1,9},{5,13},{9,1},{13,5},{2,10},{6,14},... | collective-permute-start | bytes 221192 | tf_op jit(solution)/shard_map/ppermute | solution.py:334
  21.4 0.8 %collective-permute-start.7 = (bf16[2,9,16,128]{3,2,1,0:T(8,128)(2,1)S(1)}, bf16[2,9,16,128]{3,2,1,0:T(8,128)(2,1)S(1)}, u32[]{:S(2)}, u32[]{:S(2)}) collective-permute-start(bf16[2,9,16,128]{3,2,1,0:T(8,128)(2,1)S(1)} %get-tuple-element.17.refs_0_), channel_id=1, source_target_pairs={{0,12},{4,0},{8,4},{12,8},{1,13},{5,1},{9,5},{13,9},{2,14},{6,2},{... | collective-permute-start | bytes 221192 | tf_op jit(solution)/shard_map/ppermute | solution.py:334
  22.3 2.5 %collective-permute-done.5.refs_1_ = bf16[2,9,16,128]{3,2,1,0:T(8,128)(2,1)S(1)} collective-permute-done((bf16[2,9,16,128]{3,2,1,0:T(8,128)(2,1)S(1)}, bf16[2,9,16,128]{3,2,1,0:T(8,128)(2,1)S(1)}, u32[]{:S(2)}, u32[]{:S(2)}) %collective-permute-start.5) | collective-permute-done | bytes 73760 | tf_op jit(solution)/shard_map/ppermute | solution.py:334
  24.8 2.2 %collective-permute-done.6.refs_2_ = bf16[2,9,16,128]{3,2,1,0:T(8,128)(2,1)S(1)} collective-permute-done((bf16[2,9,16,128]{3,2,1,0:T(8,128)(2,1)S(1)}, bf16[2,9,16,128]{3,2,1,0:T(8,128)(2,1)S(1)}, u32[]{:S(2)}, u32[]{:S(2)}) %collective-permute-start.6) | collective-permute-done | bytes 73760 | tf_op jit(solution)/shard_map/ppermute | solution.py:334
  27.0 0.1 collective-permute-done.7.refs_3_
  27.1 1.6 %collective-permute-start.8 = (bf16[4,9,16,128]{3,2,1,0:T(8,128)(2,1)S(1)}, bf16[4,9,16,128]{3,2,1,0:T(8,128)(2,1)S(1)}, u32[]{:S(2)}, u32[]{:S(2)}) collective-permute-start(bf16[4,9,16,128]{3,2,1,0:T(8,128)(2,1)S(1)} %pad_maximum_fusion.summed_ref), channel_id=1, source_target_pairs={{0,2},{2,0},{1,3},{3,1},{4,6},{6,4},{5,7},{7,5},{8,10},{10,8},{9,1... | collective-permute-start | bytes 442376 | tf_op jit(solution)/shard_map/ppermute | solution.py:339
  28.7 2.6 %shard_map.62 = bf16[2,2,32,2048]{3,2,1,0:T(8,128)(2,1)} custom-call(bf16[2,9,16,128]{3,2,1,0:T(8,128)(2,1)S(1)} %get-tuple-element.17.refs_0_, bf16[2,9,16,128]{3,2,1,0:T(8,128)(2,1)S(1)} %collective-permute-done.5.refs_1_, bf16[2,9,16,128]{3,2,1,0:T(8,128)(2,1)S(1)} %collective-permute-done.6.refs_2_, ...), custom_call_target="tpu_custom_call" | custom-call | flops 2000000000 | bytes 1999872 | tf_op jit(solution)/shard_map/pallas_call | solution.py:252
  31.3 1.5 %collective-permute-done.8.got_ref = bf16[4,9,16,128]{3,2,1,0:T(8,128)(2,1)S(1)} collective-permute-done((bf16[4,9,16,128]{3,2,1,0:T(8,128)(2,1)S(1)}, bf16[4,9,16,128]{3,2,1,0:T(8,128)(2,1)S(1)}, u32[]{:S(2)}, u32[]{:S(2)}) %collective-permute-start.8) | collective-permute-done | bytes 147488 | tf_op jit(solution)/shard_map/ppermute | solution.py:339
  32.8 1.7 %shard_map.63 = f32[2,32,2048]{2,1,0:T(8,128)} custom-call(bf16[4,9,16,128]{3,2,1,0:T(8,128)(2,1)S(1)} %pad_maximum_fusion.summed_ref, bf16[4,9,16,128]{3,2,1,0:T(8,128)(2,1)S(1)} %collective-permute-done.8.got_ref, f32[2,32,2048]{2,1,0:T(8,128)S(1)} %copy-done.1, bf16[9,256,256]{2,1,0:T(8,128)(2,1)S(1)} %get-tuple-element.14.refs_5_.table_ref, ...), custom_call_target="tpu_custom_call" | custom-call | flops 1000000000 | bytes 1999872 | tf_op jit(solution)/shard_map/pallas_call | solution.py:252
  (15 shorter events, 0.2 us)
Async XLA Ops:
  0.6 3.9 %copy-start.1 = (f32[2,32,2048]{2,1,0:T(8,128)S(1)}, f32[2,32,2048]{2,1,0:T(8,128)}, u32[]{:S(2)}) copy-start(f32[2,32,2048]{2,1,0:T(8,128)} %background_ref.3) | copy-start | bytes 1572868
  0.6 3.9 %copy-start = (bf16[2,2,32,2048]{3,2,1,0:T(8,128)(2,1)S(1)}, bf16[2,2,32,2048]{3,2,1,0:T(8,128)(2,1)}, u32[]{:S(2)}) copy-start(bf16[2,2,32,2048]{3,2,1,0:T(8,128)(2,1)} %refs_4_.1) | copy-start | bytes 1572868
  2.8 1.8 %collective-permute-start.1 = (bf16[2,2,8,2048]{3,2,1,0:T(8,128)(2,1)S(1)}, bf16[2,2,8,2048]{3,2,1,0:T(8,128)(2,1)S(1)}, u32[]{:S(2)}, u32[]{:S(2)}) collective-permute-start(bf16[2,2,8,2048]{3,2,1,0:T(8,128)(2,1)S(1)} %add_convert_fusion), channel_id=1, source_target_pairs={{0,1},{1,0},{2,3},{3,2},{4,5},{5,4},{6,7},{7,6},{8,9},{9,8},{10,11... | collective-permute-start | bytes 393224 | tf_op jit(solution)/shard_map/ppermute | solution.py:288
  3.3 0.9 %copy-start.2 = (bf16[2,9,16,17]{3,2,1,0:T(8,128)(2,1)S(1)}, bf16[2,9,16,17]{3,2,1,0:T(8,128)(2,1)}, u32[]{:S(2)}) copy-start(bf16[2,9,16,17]{3,2,1,0:T(8,128)(2,1)} %psf_ref.3) | copy-start | bytes 29380
  4.5 8.9 %copy-start.3 = (bf16[2,32,2048]{2,1,0:T(8,128)(2,1)S(1)}, bf16[2,32,2048]{2,1,0:T(8,128)(2,1)}, u32[]{:S(2)}) copy-start(bf16[2,32,2048]{2,1,0:T(8,128)(2,1)} %measured_ref.1) | copy-start | bytes 786436
  6.8 8.9 %collective-permute-start.2 = (bf16[2,9,16,128]{3,2,1,0:T(8,128)(2,1)S(1)}, bf16[2,9,16,128]{3,2,1,0:T(8,128)(2,1)S(1)}, u32[]{:S(2)}, u32[]{:S(2)}) collective-permute-start(bf16[2,9,16,128]{3,2,1,0:T(8,128)(2,1)S(1)} %get-tuple-element.11), channel_id=1, source_target_pairs={{0,4},{4,8},{8,12},{12,0},{1,5},{5,9},{9,13},{13,1},{2,6},{6,10},{... | collective-permute-start | bytes 221192 | tf_op jit(solution)/shard_map/ppermute | solution.py:316
  9.5 8.2 %collective-permute-start.3 = (bf16[2,9,16,128]{3,2,1,0:T(8,128)(2,1)S(1)}, bf16[2,9,16,128]{3,2,1,0:T(8,128)(2,1)S(1)}, u32[]{:S(2)}, u32[]{:S(2)}) collective-permute-start(bf16[2,9,16,128]{3,2,1,0:T(8,128)(2,1)S(1)} %get-tuple-element.12), channel_id=1, source_target_pairs={{0,8},{4,12},{8,0},{12,4},{1,9},{5,13},{9,1},{13,5},{2,10},{6,14},... | collective-permute-start | bytes 221192 | tf_op jit(solution)/shard_map/ppermute | solution.py:316
  12.1 5.8 %collective-permute-start.4 = (bf16[2,9,16,128]{3,2,1,0:T(8,128)(2,1)S(1)}, bf16[2,9,16,128]{3,2,1,0:T(8,128)(2,1)S(1)}, u32[]{:S(2)}, u32[]{:S(2)}) collective-permute-start(bf16[2,9,16,128]{3,2,1,0:T(8,128)(2,1)S(1)} %get-tuple-element.13), channel_id=1, source_target_pairs={{0,12},{4,0},{8,4},{12,8},{1,13},{5,1},{9,5},{13,9},{2,14},{6,2},{... | collective-permute-start | bytes 221192 | tf_op jit(solution)/shard_map/ppermute | solution.py:316
  13.5 1.3 %collective-permute-start = (bf16[2,4,2048]{2,1,0:T(4,128)(2,1)S(1)}, bf16[2,4,2048]{2,1,0:T(4,128)(2,1)S(1)}, u32[]{:S(2)}, u32[]{:S(2)}) collective-permute-start(bf16[2,4,2048]{2,1,0:T(4,128)(2,1)S(1)} %slice_select_fusion.1), channel_id=1, source_target_pairs={{0,1},{1,0},{2,3},{3,2},{4,5},{5,4},{6,7},{7,6},{8,9},{9,8},{10,11... | collective-permute-start | bytes 98312 | tf_op jit(solution)/shard_map/ppermute | solution.py:289
  18.0 6.8 %collective-permute-start.5 = (bf16[2,9,16,128]{3,2,1,0:T(8,128)(2,1)S(1)}, bf16[2,9,16,128]{3,2,1,0:T(8,128)(2,1)S(1)}, u32[]{:S(2)}, u32[]{:S(2)}) collective-permute-start(bf16[2,9,16,128]{3,2,1,0:T(8,128)(2,1)S(1)} %get-tuple-element.17.refs_0_), channel_id=1, source_target_pairs={{0,4},{4,8},{8,12},{12,0},{1,5},{5,9},{9,13},{13,1},{2,6},{6,10},{... | collective-permute-start | bytes 221192 | tf_op jit(solution)/shard_map/ppermute | solution.py:334
  19.8 7.1 %collective-permute-start.6 = (bf16[2,9,16,128]{3,2,1,0:T(8,128)(2,1)S(1)}, bf16[2,9,16,128]{3,2,1,0:T(8,128)(2,1)S(1)}, u32[]{:S(2)}, u32[]{:S(2)}) collective-permute-start(bf16[2,9,16,128]{3,2,1,0:T(8,128)(2,1)S(1)} %get-tuple-element.17.refs_0_), channel_id=1, source_target_pairs={{0,8},{4,12},{8,0},{12,4},{1,9},{5,13},{9,1},{13,5},{2,10},{6,14},... | collective-permute-start | bytes 221192 | tf_op jit(solution)/shard_map/ppermute | solution.py:334
  21.4 5.6 %collective-permute-start.7 = (bf16[2,9,16,128]{3,2,1,0:T(8,128)(2,1)S(1)}, bf16[2,9,16,128]{3,2,1,0:T(8,128)(2,1)S(1)}, u32[]{:S(2)}, u32[]{:S(2)}) collective-permute-start(bf16[2,9,16,128]{3,2,1,0:T(8,128)(2,1)S(1)} %get-tuple-element.17.refs_0_), channel_id=1, source_target_pairs={{0,12},{4,0},{8,4},{12,8},{1,13},{5,1},{9,5},{13,9},{2,14},{6,2},{... | collective-permute-start | bytes 221192 | tf_op jit(solution)/shard_map/ppermute | solution.py:334
  27.1 5.6 %collective-permute-start.8 = (bf16[4,9,16,128]{3,2,1,0:T(8,128)(2,1)S(1)}, bf16[4,9,16,128]{3,2,1,0:T(8,128)(2,1)S(1)}, u32[]{:S(2)}, u32[]{:S(2)}) collective-permute-start(bf16[4,9,16,128]{3,2,1,0:T(8,128)(2,1)S(1)} %pad_maximum_fusion.summed_ref), channel_id=1, source_target_pairs={{0,2},{2,0},{1,3},{3,1},{4,6},{6,4},{5,7},{7,5},{8,10},{10,8},{9,1... | collective-permute-start | bytes 442376 | tf_op jit(solution)/shard_map/ppermute | solution.py:339

commit v2 on v1

--- a/solution.py
+++ b/solution.py
@@ -35,6 +35,40 @@
     row = lax.broadcasted_iota(jnp.int32, (LANES, LANES), 0)
     col = lax.broadcasted_iota(jnp.int32, (LANES, LANES), 1)
     return jnp.abs(row - col) <= reach
+
+
+def border_kernel(volume_ref, background_ref, measured_ref, psf_ref, border_ref, table_ref, volume_edge, background_edge, sems):
+    frames, depth, row_count = volume_ref.shape[:3]
+    width = border_ref.shape[2]
+    tile = lax.axis_index("tile")
+
+    def copies(start):
+        rows = pl.ds(start, width)
+        return (
+            pltpu.make_async_copy(volume_ref.at[:, :, rows, :], volume_edge, sems.at[0]),
+            pltpu.make_async_copy(background_ref.at[:, rows, :], background_edge, sems.at[1]),
+            pltpu.make_async_copy(measured_ref.at[:, rows, :], border_ref.at[:, depth], sems.at[2]),
+        )
+
+    spread = pltpu.make_async_copy(psf_ref, table_ref, sems.at[3])
+
+    @pl.when(tile == 0)
+    def _():
+        for copy in copies(row_count - width):
+            copy.start()
+
+    @pl.when(tile != 0)
+    def _():
+        for copy in copies(0):
+            copy.start()
+
+    spread.start()
+    for copy in copies(0):
+        copy.wait()
+    for f in range(frames):
+        for d in range(depth):
+            border_ref[f, d] = (volume_edge[f, d].astype(F32) + background_edge[d]).astype(BF16)
+    spread.wait()
 
 
 def forward_table_kernel(psf_ref, table_ref, base_ref):
@@ -56,7 +90,8 @@
     depth, taps, pitch, width = psf_ref.shape
     frames, row_count, col_count = measured_ref.shape
     blocks = col_count // LANES
-    extra = got_ref.shape[1]
+    extra = (taps - 1) // 2
+    got_rows = got_ref.shape[2]
     chunk_rows = chunk_ref.shape[1]
     fill_base(psf_ref, base_ref)
     near = near_mask(width)
@@ -74,17 +109,18 @@
     per_frame = rows_ref.shape[0] // frames
     rows_ref[...] = jnp.ones_like(rows_ref)
     for f in range(frames):
-        own = f * per_frame + extra * blocks * tile
-        other = f * per_frame + row_count * blocks * (1 - tile)
+        start = f * per_frame + extra * blocks
+        own = start + extra * blocks * tile
+        other = start + (row_count * (1 - tile) - (got_rows - extra) * tile) * blocks
         for j in range(blocks):
             lanes = pl.ds(j * LANES, LANES)
             values = measured_ref[f, :, lanes].astype(F32)
             rows_ref[pl.ds(own + j, row_count, stride=blocks), :] = values
-            values = got_ref[f, :, lanes].astype(F32)
-            rows_ref[pl.ds(other + j, extra, stride=blocks), :] = values
+            values = got_ref[f, depth, :, lanes].astype(F32)
+            rows_ref[pl.ds(other + j, got_rows, stride=blocks), :] = values
         for r in range(chunk_rows):
-            start = pl.multiple_of(f * per_frame + (place * chunk_rows + r) * blocks, blocks)
-            chunk_ref[f, r] = rows_ref[pl.ds(start, blocks), :]
+            at = pl.multiple_of(start + (place * chunk_rows + r) * blocks, blocks)
+            chunk_ref[f, r] = rows_ref[pl.ds(at, blocks), :]
 
 
 def with_edges(rows_ref, start, count, blocks, after_mask, before_mask):
@@ -273,25 +309,25 @@
     shape = jax.ShapeDtypeStruct
     vmem = pltpu.VMEM
 
-    tile = lax.axis_index("tile")
     swap = [(0, 1), (1, 0)]
-
-    def edge(values, width, axis):
-        size = values.shape[axis]
-        return jnp.where(
-            tile == 0,
-            lax.slice_in_dim(values, size - width, size, axis=axis),
-            lax.slice_in_dim(values, 0, width, axis=axis),
-        )
-
-    border = (edge(volume, 2 * half, 2).astype(F32) + edge(background, 2 * half, 1)[None]).astype(BF16)
-    border = lax.ppermute(border, "tile", swap)
-    measured_border = lax.ppermute(edge(measured, half, 1), "tile", swap)
+    sent, table = pl.pallas_call(
+        border_kernel,
+        out_shape=(shape((frames, depth + 1, 2 * half, col_count), BF16), shape(psf.shape, BF16)),
+        in_specs=[pl.BlockSpec(memory_space=pltpu.HBM)] * 4,
+        out_specs=(pl.BlockSpec(memory_space=pltpu.VMEM),) * 2,
+        scratch_shapes=[
+            vmem((frames, depth, 2 * half, col_count), BF16),
+            vmem((depth, 2 * half, col_count), F32),
+            pltpu.SemaphoreType.DMA((4,)),
+        ],
+        compiler_params=pltpu.CompilerParams(vmem_limit_bytes=8 * 2**20),
+    )(*[pltpu.with_memory_space_constraint(a, pltpu.HBM) for a in (volume, background, measured, psf)])
+    border = lax.ppermute(sent, "tile", swap)
 
     base = vmem((depth * taps * pitch, LANES), F32)
     forward = call(
         forward_table_kernel,
-        (psf,),
+        (table,),
         shape((depth, pairs, 2 * LANES, 2 * LANES), BF16),
         [base],
         2 * 10**8,
@@ -318,13 +354,13 @@
     ]
     backward, inverse, measured_chunk = call(
         backward_table_kernel,
-        (psf, measured, measured_border),
+        (table, measured, border),
         (
             shape((taps, 2 * LANES, depth * LANES), BF16),
             shape((depth, 1, LANES), F32),
             shape(chunk, F32),
         ),
-        [base, vmem((frames * padded_rows * blocks, LANES), F32)],
+        [base, vmem((frames * (half + max(padded_rows, row_count + 2 * half)) * blocks, LANES), F32)],
         2 * 10**8,
     )
     for part in moved:

time: 34.7 us -> 34.7 us (level)
  waiting for transfers between devices: 9.61 us -> 11.9 us
  other arithmetic: 2.25 us -> 0.13 us
  Pallas kernels: 7.85 us -> 9.07 us
  local copies, waits for them, and re-layouts: 0.9 us -> 0.01 us
  starting transfers between devices: 13.1 us -> 12.6 us
    ppermute x3, waiting for transfers between devices: 4.76 us -> 6.76 us  [body(): lax.ppermute(ratio, 'depth', [(i, (i + s) % chunks) for i in range(chunks)])]
    pallas_call x0 -> x1, Pallas kernels: none -> 1.17 us  [body(): pl.pallas_call(border_kernel, out_shape=(shape((frames, depth + 1, 2 * ha...]
    select_n x2 -> x0, other arithmetic: 1.1 us -> none  [edge(): jnp.where(tile == 0, lax.slice_in_dim(values, size - width, size, axis=ax...]
    convert_element_type x1 -> x0, other arithmetic: 1.02 us -> none  [body(): (edge(volume, 2 * half, 2).astype(F32) + edge(background, 2 * half, 1)[No...]
    ppermute x3, waiting for transfers between devices: 2.19 us -> 3.09 us  [body(): lax.ppermute(parts[s], 'depth', [(i, (i + s) % chunks) for i in range(chu...]
    unnamed x8 -> x6, local copies, waits for them, and re-layouts: 0.9 us -> 0.01 us
    ppermute x3, starting transfers between devices: 4.31 us -> 3.62 us  [body(): lax.ppermute(ratio, 'depth', [(i, (i + s) % chunks) for i in range(chunks)])]
    ppermute x2 -> x1, waiting for transfers between devices: 1.2 us -> 0.71 us  [body(): border = lax.ppermute(sent, 'tile', swap)]
  transfers between devices with their start and end apart: 9 -> 8, of which waited for: 7 -> 6; matrix products, arithmetic and copies ran while one was open for 0% -> 0% of each run, Pallas kernels for 11% -> 12%
where the time goes in v2:
time: 34.7 us; the launch traced here: 34.5 us
  starting transfers between devices  12.6 us (36%)
  waiting for transfers between devices  11.9 us (34%)
  Pallas kernels  9.07 us (26%)
  between operations  0.73 us (2%)
    pallas_call x5, Pallas kernels, call(): pl.pallas_call(kernel, out_shape=outs, in_specs=whole(len(args)), out_spe...  7.9 us
    ppermute x3, starting transfers between devices, body(): lax.ppermute(parts[s], 'depth', [(i, (i + s) % chunks) for i in range(chu...  6.93 us
    ppermute x3, waiting for transfers between devices, body(): lax.ppermute(ratio, 'depth', [(i, (i + s) % chunks) for i in range(chunks)])  6.76 us
    ppermute x3, starting transfers between devices, body(): lax.ppermute(ratio, 'depth', [(i, (i + s) % chunks) for i in range(chunks)])  3.62 us
    ppermute x3, waiting for transfers between devices, body(): lax.ppermute(parts[s], 'depth', [(i, (i + s) % chunks) for i in range(chu...  3.09 us
    ppermute x1, starting transfers between devices, body(): others = lax.ppermute(summed, 'tm', swap)  1.56 us
    ppermute x1, waiting for transfers between devices, body(): others = lax.ppermute(summed, 'tm', swap)  1.37 us
    pallas_call x1, Pallas kernels, body(): pl.pallas_call(border_kernel, out_shape=(shape((frames, depth + 1, 2 * ha...  1.17 us
  transfers between devices with their start and end apart: 8, of which 6 were waited for; matrix products, arithmetic and copies ran while one was open for 0% of the time, Pallas kernels for 12%

profile of v2, /device:TPU:0, one launch (start us, length us, event | category | flops | bytes accessed | tf_op | source)
XLA Modules:
  0.0 34.5 jit_solution(8017218684936019698)
XLA Ops:
  0.6 1.2 %shard_map.59 = (bf16[2,3,8,2048]{3,2,1,0:T(8,128)(2,1)S(1)}, bf16[2,9,16,17]{3,2,1,0:T(8,128)(2,1)S(1)}) custom-call(bf16[2,2,32,2048]{3,2,1,0:T(8,128)(2,1)} %refs_4_.1, f32[2,32,2048]{2,1,0:T(8,128)} %background_ref.5, bf16[2,32,2048]{2,1,0:T(8,128)(2,1)} %measured_ref.3, bf16[2,9,16,17]{3,2,1,0:T(8,128)(2,1)} %psf_ref.1), custom_call_target="tpu_custom_call" | custom-call | tf_op jit(solution)/shard_map/pallas_call | solution.py:313
  1.8 0.5 %collective-permute-start = (bf16[2,3,8,2048]{3,2,1,0:T(8,128)(2,1)S(1)}, bf16[2,3,8,2048]{3,2,1,0:T(8,128)(2,1)S(1)}, u32[]{:S(2)}, u32[]{:S(2)}) collective-permute-start(bf16[2,3,8,2048]{3,2,1,0:T(8,128)(2,1)S(1)} %get-tuple-element.12), channel_id=1, source_target_pairs={{0,1},{1,0},{2,3},{3,2},{4,5},{5,4},{6,7},{7,6},{8,9},{9,8},{10,11... | collective-permute-start | bytes 589832 | tf_op jit(solution)/shard_map/ppermute | solution.py:325
  2.3 0.3 shard_map.61.table_ref
  2.7 0.0 copy-start.2
  2.7 0.7 %collective-permute-done.got_ref = bf16[2,3,8,2048]{3,2,1,0:T(8,128)(2,1)S(1)} collective-permute-done((bf16[2,3,8,2048]{3,2,1,0:T(8,128)(2,1)S(1)}, bf16[2,3,8,2048]{3,2,1,0:T(8,128)(2,1)S(1)}, u32[]{:S(2)}, u32[]{:S(2)}) %collective-permute-start) | collective-permute-done | bytes 196640 | tf_op jit(solution)/shard_map/ppermute | solution.py:325
  3.4 2.2 %shard_map.62 = (f32[2,9,16,128]{3,2,1,0:T(8,128)S(1)}, bf16[2,9,16,128]{3,2,1,0:T(8,128)(2,1)S(1)}, bf16[2,9,16,128]{3,2,1,0:T(8,128)(2,1)S(1)}, bf16[2,9,16,128]{3,2,1,0:T(8,128)(2,1)S(1)}) custom-call(bf16[2,2,32,2048]{3,2,1,0:T(8,128)(2,1)S(1)} %copy-done, f32[2,32,2048]{2,1,0:T(8,128)S(1)} %copy-done.1, ...), custom_call_target="tpu_custom_call" | custom-call | flops 2000000000 | bytes 2555904 | tf_op jit(solution)/shard_map/pallas_call | solution.py:288
  5.6 3.0 %collective-permute-start.1 = (bf16[2,9,16,128]{3,2,1,0:T(8,128)(2,1)S(1)}, bf16[2,9,16,128]{3,2,1,0:T(8,128)(2,1)S(1)}, u32[]{:S(2)}, u32[]{:S(2)}) collective-permute-start(bf16[2,9,16,128]{3,2,1,0:T(8,128)(2,1)S(1)} %get-tuple-element.15), channel_id=1, source_target_pairs={{0,4},{4,8},{8,12},{12,0},{1,5},{5,9},{9,13},{13,1},{2,6},{6,10},{... | collective-permute-start | bytes 221192 | tf_op jit(solution)/shard_map/ppermute | solution.py:352
  8.6 2.6 %collective-permute-start.2 = (bf16[2,9,16,128]{3,2,1,0:T(8,128)(2,1)S(1)}, bf16[2,9,16,128]{3,2,1,0:T(8,128)(2,1)S(1)}, u32[]{:S(2)}, u32[]{:S(2)}) collective-permute-start(bf16[2,9,16,128]{3,2,1,0:T(8,128)(2,1)S(1)} %get-tuple-element.16), channel_id=1, source_target_pairs={{0,8},{4,12},{8,0},{12,4},{1,9},{5,13},{9,1},{13,5},{2,10},{6,14},... | collective-permute-start | bytes 221192 | tf_op jit(solution)/shard_map/ppermute | solution.py:352
  11.2 1.4 %collective-permute-start.3 = (bf16[2,9,16,128]{3,2,1,0:T(8,128)(2,1)S(1)}, bf16[2,9,16,128]{3,2,1,0:T(8,128)(2,1)S(1)}, u32[]{:S(2)}, u32[]{:S(2)}) collective-permute-start(bf16[2,9,16,128]{3,2,1,0:T(8,128)(2,1)S(1)} %get-tuple-element.17), channel_id=1, source_target_pairs={{0,12},{4,0},{8,4},{12,8},{1,13},{5,1},{9,5},{13,9},{2,14},{6,2},{... | collective-permute-start | bytes 221192 | tf_op jit(solution)/shard_map/ppermute | solution.py:352
  12.6 1.0 %shard_map.60 = (bf16[9,256,256]{2,1,0:T(8,128)(2,1)S(1)}, f32[2,1,128]{2,1,0:T(1,128)S(1)}, f32[2,9,16,128]{3,2,1,0:T(8,128)S(1)}) custom-call(bf16[2,9,16,17]{3,2,1,0:T(8,128)(2,1)S(1)} %get-tuple-element.11.psf_ref, bf16[2,32,2048]{2,1,0:T(8,128)(2,1)S(1)} %copy-done.2, bf16[2,3,8,2048]{3,2,1,0:T(8,128)(2,1)S(1)} %collective-permute-done.got_ref), custom_call_target="tpu_custom_call" | custom-call | flops 200000000 | bytes 468544 | tf_op jit(solution)/shard_map/pallas_call | solution.py:288
  13.6 0.0 collective-permute-done.1
  13.6 2.9 %collective-permute-done.2 = bf16[2,9,16,128]{3,2,1,0:T(8,128)(2,1)S(1)} collective-permute-done((bf16[2,9,16,128]{3,2,1,0:T(8,128)(2,1)S(1)}, bf16[2,9,16,128]{3,2,1,0:T(8,128)(2,1)S(1)}, u32[]{:S(2)}, u32[]{:S(2)}) %collective-permute-start.2) | collective-permute-done | bytes 73760 | tf_op jit(solution)/shard_map/ppermute | solution.py:352
  16.5 0.2 collective-permute-done.3
  16.7 0.1 fusion
  16.8 3.0 %collective-permute-start.6 = (bf16[2,9,16,128]{3,2,1,0:T(8,128)(2,1)S(1)}, bf16[2,9,16,128]{3,2,1,0:T(8,128)(2,1)S(1)}, u32[]{:S(2)}, u32[]{:S(2)}) collective-permute-start(bf16[2,9,16,128]{3,2,1,0:T(8,128)(2,1)S(1)} %get-tuple-element.21.refs_0_), channel_id=1, source_target_pairs={{0,12},{4,0},{8,4},{12,8},{1,13},{5,1},{9,5},{13,9},{2,14},{6,2},{... | collective-permute-start | bytes 221192 | tf_op jit(solution)/shard_map/ppermute | solution.py:370
  19.8 0.4 %collective-permute-start.5 = (bf16[2,9,16,128]{3,2,1,0:T(8,128)(2,1)S(1)}, bf16[2,9,16,128]{3,2,1,0:T(8,128)(2,1)S(1)}, u32[]{:S(2)}, u32[]{:S(2)}) collective-permute-start(bf16[2,9,16,128]{3,2,1,0:T(8,128)(2,1)S(1)} %get-tuple-element.21.refs_0_), channel_id=1, source_target_pairs={{0,8},{4,12},{8,0},{12,4},{1,9},{5,13},{9,1},{13,5},{2,10},{6,14},... | collective-permute-start | bytes 221192 | tf_op jit(solution)/shard_map/ppermute | solution.py:370
  20.1 0.3 collective-permute-start.4
  20.4 2.1 %collective-permute-done.6.refs_3_ = bf16[2,9,16,128]{3,2,1,0:T(8,128)(2,1)S(1)} collective-permute-done((bf16[2,9,16,128]{3,2,1,0:T(8,128)(2,1)S(1)}, bf16[2,9,16,128]{3,2,1,0:T(8,128)(2,1)S(1)}, u32[]{:S(2)}, u32[]{:S(2)}) %collective-permute-start.6) | collective-permute-done | bytes 73760 | tf_op jit(solution)/shard_map/ppermute | solution.py:370
  22.5 4.7 %collective-permute-done.5.refs_2_ = bf16[2,9,16,128]{3,2,1,0:T(8,128)(2,1)S(1)} collective-permute-done((bf16[2,9,16,128]{3,2,1,0:T(8,128)(2,1)S(1)}, bf16[2,9,16,128]{3,2,1,0:T(8,128)(2,1)S(1)}, u32[]{:S(2)}, u32[]{:S(2)}) %collective-permute-start.5) | collective-permute-done | bytes 73760 | tf_op jit(solution)/shard_map/ppermute | solution.py:370
  27.2 0.0 collective-permute-done.4.refs_1_
  27.3 1.6 %collective-permute-start.7 = (bf16[4,9,16,128]{3,2,1,0:T(8,128)(2,1)S(1)}, bf16[4,9,16,128]{3,2,1,0:T(8,128)(2,1)S(1)}, u32[]{:S(2)}, u32[]{:S(2)}) collective-permute-start(bf16[4,9,16,128]{3,2,1,0:T(8,128)(2,1)S(1)} %pad_maximum_fusion.summed_ref), channel_id=1, source_target_pairs={{0,2},{2,0},{1,3},{3,1},{4,6},{6,4},{5,7},{7,5},{8,10},{10,8},{9,1... | collective-permute-start | bytes 442376 | tf_op jit(solution)/shard_map/ppermute | solution.py:375
  28.8 2.6 %shard_map.63 = bf16[2,2,32,2048]{3,2,1,0:T(8,128)(2,1)} custom-call(bf16[2,9,16,128]{3,2,1,0:T(8,128)(2,1)S(1)} %get-tuple-element.21.refs_0_, bf16[2,9,16,128]{3,2,1,0:T(8,128)(2,1)S(1)} %collective-permute-done.4.refs_1_, bf16[2,9,16,128]{3,2,1,0:T(8,128)(2,1)S(1)} %collective-permute-done.5.refs_2_, ...), custom_call_target="tpu_custom_call" | custom-call | flops 2000000000 | bytes 1999872 | tf_op jit(solution)/shard_map/pallas_call | solution.py:288
  31.4 1.4 %collective-permute-done.7.got_ref = bf16[4,9,16,128]{3,2,1,0:T(8,128)(2,1)S(1)} collective-permute-done((bf16[4,9,16,128]{3,2,1,0:T(8,128)(2,1)S(1)}, bf16[4,9,16,128]{3,2,1,0:T(8,128)(2,1)S(1)}, u32[]{:S(2)}, u32[]{:S(2)}) %collective-permute-start.7) | collective-permute-done | bytes 147488 | tf_op jit(solution)/shard_map/ppermute | solution.py:375
  32.8 1.7 %shard_map.64 = f32[2,32,2048]{2,1,0:T(8,128)} custom-call(bf16[4,9,16,128]{3,2,1,0:T(8,128)(2,1)S(1)} %pad_maximum_fusion.summed_ref, bf16[4,9,16,128]{3,2,1,0:T(8,128)(2,1)S(1)} %collective-permute-done.7.got_ref, f32[2,32,2048]{2,1,0:T(8,128)S(1)} %copy-done.1, bf16[9,256,256]{2,1,0:T(8,128)(2,1)S(1)} %get-tuple-element.18.refs_5_.table_ref, ...), custom_call_target="tpu_custom_call" | custom-call | flops 1000000000 | bytes 1999872 | tf_op jit(solution)/shard_map/pallas_call | solution.py:288
  (9 shorter events, 0.1 us)
Async XLA Ops:
  0.6 2.8 %copy-start.1 = (f32[2,32,2048]{2,1,0:T(8,128)S(1)}, f32[2,32,2048]{2,1,0:T(8,128)}, u32[]{:S(2)}) copy-start(f32[2,32,2048]{2,1,0:T(8,128)} %background_ref.5) | copy-start | bytes 1572868
  0.6 2.8 %copy-start = (bf16[2,2,32,2048]{3,2,1,0:T(8,128)(2,1)S(1)}, bf16[2,2,32,2048]{3,2,1,0:T(8,128)(2,1)}, u32[]{:S(2)}) copy-start(bf16[2,2,32,2048]{3,2,1,0:T(8,128)(2,1)} %refs_4_.1) | copy-start | bytes 1572868
  1.8 1.6 %collective-permute-start = (bf16[2,3,8,2048]{3,2,1,0:T(8,128)(2,1)S(1)}, bf16[2,3,8,2048]{3,2,1,0:T(8,128)(2,1)S(1)}, u32[]{:S(2)}, u32[]{:S(2)}) collective-permute-start(bf16[2,3,8,2048]{3,2,1,0:T(8,128)(2,1)S(1)} %get-tuple-element.12), channel_id=1, source_target_pairs={{0,1},{1,0},{2,3},{3,2},{4,5},{5,4},{6,7},{7,6},{8,9},{9,8},{10,11... | collective-permute-start | bytes 589832 | tf_op jit(solution)/shard_map/ppermute | solution.py:325
  2.7 9.9 %copy-start.2 = (bf16[2,32,2048]{2,1,0:T(8,128)(2,1)S(1)}, bf16[2,32,2048]{2,1,0:T(8,128)(2,1)}, u32[]{:S(2)}) copy-start(bf16[2,32,2048]{2,1,0:T(8,128)(2,1)} %measured_ref.3) | copy-start | bytes 786436
  5.6 8.0 %collective-permute-start.1 = (bf16[2,9,16,128]{3,2,1,0:T(8,128)(2,1)S(1)}, bf16[2,9,16,128]{3,2,1,0:T(8,128)(2,1)S(1)}, u32[]{:S(2)}, u32[]{:S(2)}) collective-permute-start(bf16[2,9,16,128]{3,2,1,0:T(8,128)(2,1)S(1)} %get-tuple-element.15), channel_id=1, source_target_pairs={{0,4},{4,8},{8,12},{12,0},{1,5},{5,9},{9,13},{13,1},{2,6},{6,10},{... | collective-permute-start | bytes 221192 | tf_op jit(solution)/shard_map/ppermute | solution.py:352
  8.6 7.8 %collective-permute-start.2 = (bf16[2,9,16,128]{3,2,1,0:T(8,128)(2,1)S(1)}, bf16[2,9,16,128]{3,2,1,0:T(8,128)(2,1)S(1)}, u32[]{:S(2)}, u32[]{:S(2)}) collective-permute-start(bf16[2,9,16,128]{3,2,1,0:T(8,128)(2,1)S(1)} %get-tuple-element.16), channel_id=1, source_target_pairs={{0,8},{4,12},{8,0},{12,4},{1,9},{5,13},{9,1},{13,5},{2,10},{6,14},... | collective-permute-start | bytes 221192 | tf_op jit(solution)/shard_map/ppermute | solution.py:352
  11.2 5.5 %collective-permute-start.3 = (bf16[2,9,16,128]{3,2,1,0:T(8,128)(2,1)S(1)}, bf16[2,9,16,128]{3,2,1,0:T(8,128)(2,1)S(1)}, u32[]{:S(2)}, u32[]{:S(2)}) collective-permute-start(bf16[2,9,16,128]{3,2,1,0:T(8,128)(2,1)S(1)} %get-tuple-element.17), channel_id=1, source_target_pairs={{0,12},{4,0},{8,4},{12,8},{1,13},{5,1},{9,5},{13,9},{2,14},{6,2},{... | collective-permute-start | bytes 221192 | tf_op jit(solution)/shard_map/ppermute | solution.py:352
  16.8 5.7 %collective-permute-start.6 = (bf16[2,9,16,128]{3,2,1,0:T(8,128)(2,1)S(1)}, bf16[2,9,16,128]{3,2,1,0:T(8,128)(2,1)S(1)}, u32[]{:S(2)}, u32[]{:S(2)}) collective-permute-start(bf16[2,9,16,128]{3,2,1,0:T(8,128)(2,1)S(1)} %get-tuple-element.21.refs_0_), channel_id=1, source_target_pairs={{0,12},{4,0},{8,4},{12,8},{1,13},{5,1},{9,5},{13,9},{2,14},{6,2},{... | collective-permute-start | bytes 221192 | tf_op jit(solution)/shard_map/ppermute | solution.py:370
  19.8 7.4 %collective-permute-start.5 = (bf16[2,9,16,128]{3,2,1,0:T(8,128)(2,1)S(1)}, bf16[2,9,16,128]{3,2,1,0:T(8,128)(2,1)S(1)}, u32[]{:S(2)}, u32[]{:S(2)}) collective-permute-start(bf16[2,9,16,128]{3,2,1,0:T(8,128)(2,1)S(1)} %get-tuple-element.21.refs_0_), channel_id=1, source_target_pairs={{0,8},{4,12},{8,0},{12,4},{1,9},{5,13},{9,1},{13,5},{2,10},{6,14},... | collective-permute-start | bytes 221192 | tf_op jit(solution)/shard_map/ppermute | solution.py:370
  20.1 7.1 %collective-permute-start.4 = (bf16[2,9,16,128]{3,2,1,0:T(8,128)(2,1)S(1)}, bf16[2,9,16,128]{3,2,1,0:T(8,128)(2,1)S(1)}, u32[]{:S(2)}, u32[]{:S(2)}) collective-permute-start(bf16[2,9,16,128]{3,2,1,0:T(8,128)(2,1)S(1)} %get-tuple-element.21.refs_0_), channel_id=1, source_target_pairs={{0,4},{4,8},{8,12},{12,0},{1,5},{5,9},{9,13},{13,1},{2,6},{6,10},{... | collective-permute-start | bytes 221192 | tf_op jit(solution)/shard_map/ppermute | solution.py:370
  27.3 5.5 %collective-permute-start.7 = (bf16[4,9,16,128]{3,2,1,0:T(8,128)(2,1)S(1)}, bf16[4,9,16,128]{3,2,1,0:T(8,128)(2,1)S(1)}, u32[]{:S(2)}, u32[]{:S(2)}) collective-permute-start(bf16[4,9,16,128]{3,2,1,0:T(8,128)(2,1)S(1)} %pad_maximum_fusion.summed_ref), channel_id=1, source_target_pairs={{0,2},{2,0},{1,3},{3,1},{4,6},{6,4},{5,7},{7,5},{8,10},{10,8},{9,1... | collective-permute-start | bytes 442376 | tf_op jit(solution)/shard_map/ppermute | solution.py:375

commit v3 on v2

--- a/solution.py
+++ b/solution.py
@@ -71,7 +71,7 @@
     spread.wait()
 
 
-def forward_table_kernel(psf_ref, table_ref, base_ref):
+def forward_table_kernel(psf_ref, volume_ref, background_ref, table_ref, left_ref, base_ref, rows_ref):
     depth, taps, pitch, width = psf_ref.shape
     fill_base(psf_ref, base_ref)
     near = near_mask(width)
@@ -84,6 +84,28 @@
                 table_ref[d, t // 2, pl.ds(LANES, LANES), lanes] = jnp.where(near, 0.0, band).astype(BF16)
             else:
                 table_ref[d, t // 2, :, lanes] = jnp.zeros((2 * LANES, LANES), BF16)
+    frames, depth, row_count, col_count = volume_ref.shape
+    blocks = col_count // LANES
+    half = (taps - 1) // 2
+    tile = lax.axis_index("tile")
+    masks = edge_masks(blocks, blocks)
+    span = left_ref.shape[0] // (frames * depth)
+    for f in range(frames):
+        for d in range(depth):
+            base = (f * depth + d) * row_count * blocks
+            for j in range(blocks):
+                lanes = pl.ds(j * LANES, LANES)
+                total = (volume_ref[f, d, :, lanes].astype(F32) + background_ref[d, :, lanes]).astype(BF16).astype(F32)
+                rows_ref[pl.ds(PAD + base + j, row_count, stride=blocks), :] = total
+            own = (f * depth + d) * span + (half + half * tile) * blocks
+            empty = pl.multiple_of((f * depth + d) * span + (row_count + 2 * half) * blocks * tile, blocks)
+            left_ref[pl.ds(empty, half * blocks), :] = jnp.zeros((half * blocks, 2 * LANES), BF16)
+            left_ref[pl.ds((f * depth + d + 1) * span - blocks, blocks), :] = jnp.zeros((blocks, 2 * LANES), BF16)
+            for r in range(row_count):
+                here, edges = with_edges(rows_ref, PAD + base + r * blocks, blocks, blocks, *masks)
+                rows = pl.ds(pl.multiple_of(own + r * blocks, blocks), blocks)
+                left_ref[rows, pl.ds(0, LANES)] = here
+                left_ref[rows, pl.ds(LANES, LANES)] = edges
 
 
 def backward_table_kernel(psf_ref, measured_ref, got_ref, table_ref, inverse_ref, chunk_ref, base_ref, rows_ref):
@@ -142,38 +164,30 @@
 PAD = 8
 
 
-def sensor_kernel(chunks, volume_ref, background_ref, got_ref, table_ref, own_ref, *rest):
+def sensor_kernel(chunks, row_count, half, given_ref, got_ref, table_ref, own_ref, *rest):
     sent_refs = rest[: chunks - 1]
-    rows_ref, left_ref, sums_ref, whole_ref = rest[chunks - 1 :]
-    frames, depth, row_count, col_count = volume_ref.shape
+    left_ref, rows_ref, sums_ref, whole_ref = rest[chunks - 1 :]
+    frames, layers, halo, col_count = got_ref.shape
+    depth = layers - 1
     blocks = col_count // LANES
     pairs = table_ref.shape[1]
-    halo = got_ref.shape[2]
-    half = halo // 2
     sensor_rows = row_count + half
-    windows = sensor_rows + halo + 1
-    span = windows * blocks
+    span = left_ref.shape[0] // (frames * depth)
     tile = lax.axis_index("tile")
     place = lax.axis_index("depth")
-    use_after, use_before = edge_masks(blocks, blocks)
+    masks = edge_masks(blocks, blocks)
     for f in range(frames):
         for d in range(depth):
-            first = PAD + (f * depth + d) * span
-            own = first + (half + half * tile) * blocks
-            other = first + (row_count + half) * blocks * (1 - tile)
-            empty = pl.multiple_of(first + (row_count + halo) * blocks * tile, 8)
-            rows_ref[pl.ds(empty, half * blocks), :] = jnp.zeros((half * blocks, LANES), F32)
-            rows_ref[pl.ds(first + (windows - 1) * blocks, blocks), :] = jnp.zeros((blocks, LANES), F32)
+            first = (f * depth + d) * halo * blocks
+            other = (f * depth + d) * span + (row_count + half) * blocks * (1 - tile)
             for j in range(blocks):
                 lanes = pl.ds(j * LANES, LANES)
-                total = (volume_ref[f, d, :, lanes].astype(F32) + background_ref[d, :, lanes]).astype(BF16).astype(F32)
-                rows_ref[pl.ds(own + j, row_count, stride=blocks), :] = total
-                rows_ref[pl.ds(other + j, halo, stride=blocks), :] = got_ref[f, d, :, lanes].astype(F32)
-            for r in range(windows):
-                start = first + r * blocks
-                here, edges = with_edges(rows_ref, start, blocks, blocks, use_after, use_before)
-                left_ref[pl.ds(start - PAD, blocks), pl.ds(0, LANES)] = here
-                left_ref[pl.ds(start - PAD, blocks), pl.ds(LANES, LANES)] = edges
+                rows_ref[pl.ds(PAD + first + j, halo, stride=blocks), :] = got_ref[f, d, :, lanes].astype(F32)
+            for r in range(halo):
+                here, edges = with_edges(rows_ref, PAD + first + r * blocks, blocks, blocks, *masks)
+                rows = pl.ds(pl.multiple_of(other + r * blocks, blocks), blocks)
+                left_ref[rows, pl.ds(0, LANES)] = here
+                left_ref[rows, pl.ds(LANES, LANES)] = edges
     size = (sensor_rows + 1) * blocks
     chunk_rows = own_ref.shape[1]
     for f in range(frames):
@@ -283,7 +297,7 @@
     return [pl.BlockSpec(memory_space=pltpu.VMEM)] * count
 
 
-def call(kernel, args, outs, scratch, flops):
+def call(kernel, args, outs, scratch, flops, aliases={}):
     moved = sum(a.size * a.dtype.itemsize for a in args)
     return pl.pallas_call(
         kernel,
@@ -291,6 +305,7 @@
         in_specs=whole(len(args)),
         out_specs=jax.tree.map(lambda _: pl.BlockSpec(memory_space=pltpu.VMEM), outs),
         scratch_shapes=scratch,
+        input_output_aliases=aliases,
         compiler_params=pltpu.CompilerParams(vmem_limit_bytes=40 * 2**20),
         cost_estimate=pl.CostEstimate(flops=flops, bytes_accessed=moved, transcendentals=0),
     )(*args)
@@ -325,27 +340,28 @@
     border = lax.ppermute(sent, "tile", swap)
 
     base = vmem((depth * taps * pitch, LANES), F32)
-    forward = call(
+    windows = sensor_rows + 2 * half + 1
+    left_shape = shape((frames * depth * windows * blocks, 2 * LANES), BF16)
+    forward, left = call(
         forward_table_kernel,
-        (table,),
-        shape((depth, pairs, 2 * LANES, 2 * LANES), BF16),
-        [base],
+        (table, volume, background),
+        (shape((depth, pairs, 2 * LANES, 2 * LANES), BF16), left_shape),
+        [base, vmem((frames * depth * row_count * blocks + 2 * PAD, LANES), F32)],
         2 * 10**8,
     )
-    windows = sensor_rows + 2 * half + 1
     padded_rows = chunks * chunk_rows
     chunk = (frames, chunk_rows, blocks, LANES)
     parts = call(
-        functools.partial(sensor_kernel, chunks),
-        (volume, background, border, forward),
-        (shape(chunk, F32),) + (shape(chunk, BF16),) * (chunks - 1),
+        functools.partial(sensor_kernel, chunks, row_count, half),
+        (left, border, forward),
+        (shape(chunk, F32),) + (shape(chunk, BF16),) * (chunks - 1) + (left_shape,),
         [
-            vmem((frames * depth * windows * blocks + 2 * PAD, LANES), F32),
-            vmem((frames * depth * windows * blocks, 2 * LANES), BF16),
+            vmem((frames * depth * 2 * half * blocks + 2 * PAD, LANES), F32),
             vmem(((sensor_rows + 1) * blocks, 2 * LANES), F32),
             vmem((frames, padded_rows * blocks, LANES), F32),
         ],
         2 * 10**9,
+        {0: chunks},
     )
     sensor = parts[0]
     moved = [

time: 34.7 us -> 33 us (0.951)
  waiting for transfers between devices: 11.9 us -> 9.53 us
  starting transfers between devices: 12.6 us -> 13.3 us
    ppermute x3, waiting for transfers between devices: 6.76 us -> 4.76 us  [body(): lax.ppermute(ratio, 'depth', [(i, (i + s) % chunks) for i in range(chunks)])]
    ppermute x3, starting transfers between devices: 3.62 us -> 4.3 us  [body(): lax.ppermute(ratio, 'depth', [(i, (i + s) % chunks) for i in range(chunks)])]
    ppermute x1, waiting for transfers between devices: 0.71 us -> 0.2 us  [body(): border = lax.ppermute(sent, 'tile', swap)]
  transfers between devices with their start and end apart: 8 -> 8, of which waited for: 6 -> 7; matrix products, arithmetic and copies ran while one was open for 0% -> 0% of each run, Pallas kernels for 12% -> 14%
where the time goes in v3:
time: 33 us; the launch traced here: 32.9 us
  starting transfers between devices  13.3 us (40%)
  waiting for transfers between devices  9.53 us (29%)
  Pallas kernels  9.2 us (28%)
  between operations  0.71 us (2%)
    pallas_call x5, Pallas kernels, call(): pl.pallas_call(kernel, out_shape=outs, in_specs=whole(len(args)), out_spe...  8.03 us
    ppermute x3, starting transfers between devices, body(): lax.ppermute(parts[s], 'depth', [(i, (i + s) % chunks) for i in range(chu...  6.93 us
    ppermute x3, waiting for transfers between devices, body(): lax.ppermute(ratio, 'depth', [(i, (i + s) % chunks) for i in range(chunks)])  4.76 us
    ppermute x3, starting transfers between devices, body(): lax.ppermute(ratio, 'depth', [(i, (i + s) % chunks) for i in range(chunks)])  4.3 us
    ppermute x3, waiting for transfers between devices, body(): lax.ppermute(parts[s], 'depth', [(i, (i + s) % chunks) for i in range(chu...  3.1 us
    ppermute x1, starting transfers between devices, body(): others = lax.ppermute(summed, 'tm', swap)  1.56 us
    ppermute x1, waiting for transfers between devices, body(): others = lax.ppermute(summed, 'tm', swap)  1.47 us
    pallas_call x1, Pallas kernels, body(): pl.pallas_call(border_kernel, out_shape=(shape((frames, depth + 1, 2 * ha...  1.17 us
  transfers between devices with their start and end apart: 8, of which 7 were waited for; matrix products, arithmetic and copies ran while one was open for 0% of the time, Pallas kernels for 14%

profile of v3, /device:TPU:0, one launch (start us, length us, event | category | flops | bytes accessed | tf_op | source)
XLA Modules:
  0.0 32.9 jit_solution(8361482960015865093)
XLA Ops:
  0.6 0.0 copy-start
  0.6 1.2 %shard_map.59 = (bf16[2,3,8,2048]{3,2,1,0:T(8,128)(2,1)S(1)}, bf16[2,9,16,17]{3,2,1,0:T(8,128)(2,1)S(1)}) custom-call(bf16[2,2,32,2048]{3,2,1,0:T(8,128)(2,1)} %refs_4_.1, f32[2,32,2048]{2,1,0:T(8,128)} %background_ref.5, bf16[2,32,2048]{2,1,0:T(8,128)(2,1)} %measured_ref.3, bf16[2,9,16,17]{3,2,1,0:T(8,128)(2,1)} %psf_ref.1), custom_call_target="tpu_custom_call" | custom-call | tf_op jit(solution)/shard_map/pallas_call | solution.py:328
  1.8 0.5 %collective-permute-start = (bf16[2,3,8,2048]{3,2,1,0:T(8,128)(2,1)S(1)}, bf16[2,3,8,2048]{3,2,1,0:T(8,128)(2,1)S(1)}, u32[]{:S(2)}, u32[]{:S(2)}) collective-permute-start(bf16[2,3,8,2048]{3,2,1,0:T(8,128)(2,1)S(1)} %get-tuple-element.14), channel_id=1, source_target_pairs={{0,1},{1,0},{2,3},{3,2},{4,5},{5,4},{6,7},{7,6},{8,9},{9,8},{10,11... | collective-permute-start | bytes 589832 | tf_op jit(solution)/shard_map/ppermute | solution.py:340
  2.4 0.9 %shard_map.61 = (bf16[2,5,256,256]{3,2,1,0:T(8,128)(2,1)S(1)}, bf16[2880,256]{1,0:T(8,128)(2,1)S(1)}) custom-call(bf16[2,9,16,17]{3,2,1,0:T(8,128)(2,1)S(1)} %get-tuple-element.13.psf_ref, bf16[2,2,32,2048]{3,2,1,0:T(8,128)(2,1)S(1)} %copy-done, f32[2,32,2048]{2,1,0:T(8,128)S(1)} %copy-done.1), custom_call_target="tpu_custom_call" | custom-call | flops 200000000 | bytes 1058368 | tf_op jit(solution)/shard_map/pallas_call | solution.py:302
  3.2 0.2 collective-permute-done.got_ref
  3.4 1.8 %shard_map.62 = (f32[2,9,16,128]{3,2,1,0:T(8,128)S(1)}, bf16[2,9,16,128]{3,2,1,0:T(8,128)(2,1)S(1)}, bf16[2,9,16,128]{3,2,1,0:T(8,128)(2,1)S(1)}, bf16[2,9,16,12...) custom-call(bf16[2880,256]{1,0:T(8,128)(2,1)S(1)} %get-tuple-element.16.given_ref, ...), custom_call_target="tpu_custom_call", output_to_operand_aliasing={{4}: (0, {})} | custom-call | flops 2000000000 | bytes 2981888 | tf_op jit(solution)/shard_map/pallas_call | solution.py:302
  5.3 3.0 %collective-permute-start.1 = (bf16[2,9,16,128]{3,2,1,0:T(8,128)(2,1)S(1)}, bf16[2,9,16,128]{3,2,1,0:T(8,128)(2,1)S(1)}, u32[]{:S(2)}, u32[]{:S(2)}) collective-permute-start(bf16[2,9,16,128]{3,2,1,0:T(8,128)(2,1)S(1)} %get-tuple-element.19), channel_id=1, source_target_pairs={{0,4},{4,8},{8,12},{12,0},{1,5},{5,9},{9,13},{13,1},{2,6},{6,10},{... | collective-permute-start | bytes 221192 | tf_op jit(solution)/shard_map/ppermute | solution.py:368
  8.2 2.6 %collective-permute-start.2 = (bf16[2,9,16,128]{3,2,1,0:T(8,128)(2,1)S(1)}, bf16[2,9,16,128]{3,2,1,0:T(8,128)(2,1)S(1)}, u32[]{:S(2)}, u32[]{:S(2)}) collective-permute-start(bf16[2,9,16,128]{3,2,1,0:T(8,128)(2,1)S(1)} %get-tuple-element.20), channel_id=1, source_target_pairs={{0,8},{4,12},{8,0},{12,4},{1,9},{5,13},{9,1},{13,5},{2,10},{6,14},... | collective-permute-start | bytes 221192 | tf_op jit(solution)/shard_map/ppermute | solution.py:368
  10.8 1.3 %collective-permute-start.3 = (bf16[2,9,16,128]{3,2,1,0:T(8,128)(2,1)S(1)}, bf16[2,9,16,128]{3,2,1,0:T(8,128)(2,1)S(1)}, u32[]{:S(2)}, u32[]{:S(2)}) collective-permute-start(bf16[2,9,16,128]{3,2,1,0:T(8,128)(2,1)S(1)} %get-tuple-element.21), channel_id=1, source_target_pairs={{0,12},{4,0},{8,4},{12,8},{1,13},{5,1},{9,5},{13,9},{2,14},{6,2},{... | collective-permute-start | bytes 221192 | tf_op jit(solution)/shard_map/ppermute | solution.py:368
  12.2 1.0 %shard_map.60 = (bf16[9,256,256]{2,1,0:T(8,128)(2,1)S(1)}, f32[2,1,128]{2,1,0:T(1,128)S(1)}, f32[2,9,16,128]{3,2,1,0:T(8,128)S(1)}) custom-call(bf16[2,9,16,17]{3,2,1,0:T(8,128)(2,1)S(1)} %get-tuple-element.13.psf_ref, bf16[2,32,2048]{2,1,0:T(8,128)(2,1)S(1)} %copy-done.2, bf16[2,3,8,2048]{3,2,1,0:T(8,128)(2,1)S(1)} %collective-permute-done.got_ref), custom_call_target="tpu_custom_call" | custom-call | flops 200000000 | bytes 468544 | tf_op jit(solution)/shard_map/pallas_call | solution.py:302
  13.2 0.0 collective-permute-done.1
  13.2 2.9 %collective-permute-done.2 = bf16[2,9,16,128]{3,2,1,0:T(8,128)(2,1)S(1)} collective-permute-done((bf16[2,9,16,128]{3,2,1,0:T(8,128)(2,1)S(1)}, bf16[2,9,16,128]{3,2,1,0:T(8,128)(2,1)S(1)}, u32[]{:S(2)}, u32[]{:S(2)}) %collective-permute-start.2) | collective-permute-done | bytes 73760 | tf_op jit(solution)/shard_map/ppermute | solution.py:368
  16.1 0.2 collective-permute-done.3
  16.3 0.1 fusion
  16.4 1.9 %collective-permute-start.4 = (bf16[2,9,16,128]{3,2,1,0:T(8,128)(2,1)S(1)}, bf16[2,9,16,128]{3,2,1,0:T(8,128)(2,1)S(1)}, u32[]{:S(2)}, u32[]{:S(2)}) collective-permute-start(bf16[2,9,16,128]{3,2,1,0:T(8,128)(2,1)S(1)} %get-tuple-element.25.refs_0_), channel_id=1, source_target_pairs={{0,4},{4,8},{8,12},{12,0},{1,5},{5,9},{9,13},{13,1},{2,6},{6,10},{... | collective-permute-start | bytes 221192 | tf_op jit(solution)/shard_map/ppermute | solution.py:386
  18.3 1.7 %collective-permute-start.5 = (bf16[2,9,16,128]{3,2,1,0:T(8,128)(2,1)S(1)}, bf16[2,9,16,128]{3,2,1,0:T(8,128)(2,1)S(1)}, u32[]{:S(2)}, u32[]{:S(2)}) collective-permute-start(bf16[2,9,16,128]{3,2,1,0:T(8,128)(2,1)S(1)} %get-tuple-element.25.refs_0_), channel_id=1, source_target_pairs={{0,8},{4,12},{8,0},{12,4},{1,9},{5,13},{9,1},{13,5},{2,10},{6,14},... | collective-permute-start | bytes 221192 | tf_op jit(solution)/shard_map/ppermute | solution.py:386
  19.9 0.8 %collective-permute-start.6 = (bf16[2,9,16,128]{3,2,1,0:T(8,128)(2,1)S(1)}, bf16[2,9,16,128]{3,2,1,0:T(8,128)(2,1)S(1)}, u32[]{:S(2)}, u32[]{:S(2)}) collective-permute-start(bf16[2,9,16,128]{3,2,1,0:T(8,128)(2,1)S(1)} %get-tuple-element.25.refs_0_), channel_id=1, source_target_pairs={{0,12},{4,0},{8,4},{12,8},{1,13},{5,1},{9,5},{13,9},{2,14},{6,2},{... | collective-permute-start | bytes 221192 | tf_op jit(solution)/shard_map/ppermute | solution.py:386
  20.7 2.5 %collective-permute-done.4.refs_1_ = bf16[2,9,16,128]{3,2,1,0:T(8,128)(2,1)S(1)} collective-permute-done((bf16[2,9,16,128]{3,2,1,0:T(8,128)(2,1)S(1)}, bf16[2,9,16,128]{3,2,1,0:T(8,128)(2,1)S(1)}, u32[]{:S(2)}, u32[]{:S(2)}) %collective-permute-start.4) | collective-permute-done | bytes 73760 | tf_op jit(solution)/shard_map/ppermute | solution.py:386
  23.2 2.1 %collective-permute-done.5.refs_2_ = bf16[2,9,16,128]{3,2,1,0:T(8,128)(2,1)S(1)} collective-permute-done((bf16[2,9,16,128]{3,2,1,0:T(8,128)(2,1)S(1)}, bf16[2,9,16,128]{3,2,1,0:T(8,128)(2,1)S(1)}, u32[]{:S(2)}, u32[]{:S(2)}) %collective-permute-start.5) | collective-permute-done | bytes 73760 | tf_op jit(solution)/shard_map/ppermute | solution.py:386
  25.4 0.1 collective-permute-done.6.refs_3_
  25.6 1.6 %collective-permute-start.7 = (bf16[4,9,16,128]{3,2,1,0:T(8,128)(2,1)S(1)}, bf16[4,9,16,128]{3,2,1,0:T(8,128)(2,1)S(1)}, u32[]{:S(2)}, u32[]{:S(2)}) collective-permute-start(bf16[4,9,16,128]{3,2,1,0:T(8,128)(2,1)S(1)} %pad_maximum_fusion.summed_ref), channel_id=1, source_target_pairs={{0,2},{2,0},{1,3},{3,1},{4,6},{6,4},{5,7},{7,5},{8,10},{10,8},{9,1... | collective-permute-start | bytes 442376 | tf_op jit(solution)/shard_map/ppermute | solution.py:391
  27.1 2.6 %shard_map.63 = bf16[2,2,32,2048]{3,2,1,0:T(8,128)(2,1)} custom-call(bf16[2,9,16,128]{3,2,1,0:T(8,128)(2,1)S(1)} %get-tuple-element.25.refs_0_, bf16[2,9,16,128]{3,2,1,0:T(8,128)(2,1)S(1)} %collective-permute-done.4.refs_1_, bf16[2,9,16,128]{3,2,1,0:T(8,128)(2,1)S(1)} %collective-permute-done.5.refs_2_, ...), custom_call_target="tpu_custom_call" | custom-call | flops 2000000000 | bytes 1999872 | tf_op jit(solution)/shard_map/pallas_call | solution.py:302
  29.7 1.5 %collective-permute-done.7.got_ref = bf16[4,9,16,128]{3,2,1,0:T(8,128)(2,1)S(1)} collective-permute-done((bf16[4,9,16,128]{3,2,1,0:T(8,128)(2,1)S(1)}, bf16[4,9,16,128]{3,2,1,0:T(8,128)(2,1)S(1)}, u32[]{:S(2)}, u32[]{:S(2)}) %collective-permute-start.7) | collective-permute-done | bytes 147488 | tf_op jit(solution)/shard_map/ppermute | solution.py:391
  31.2 1.7 %shard_map.64 = f32[2,32,2048]{2,1,0:T(8,128)} custom-call(bf16[4,9,16,128]{3,2,1,0:T(8,128)(2,1)S(1)} %pad_maximum_fusion.summed_ref, bf16[4,9,16,128]{3,2,1,0:T(8,128)(2,1)S(1)} %collective-permute-done.7.got_ref, f32[2,32,2048]{2,1,0:T(8,128)S(1)} %copy-done.1, bf16[9,256,256]{2,1,0:T(8,128)(2,1)S(1)} %get-tuple-element.22.refs_5_.table_ref, ...), custom_call_target="tpu_custom_call" | custom-call | flops 1000000000 | bytes 1999872 | tf_op jit(solution)/shard_map/pallas_call | solution.py:302
  (9 shorter events, 0.1 us)
Async XLA Ops:
  0.6 1.7 %copy-start = (bf16[2,2,32,2048]{3,2,1,0:T(8,128)(2,1)S(1)}, bf16[2,2,32,2048]{3,2,1,0:T(8,128)(2,1)}, u32[]{:S(2)}) copy-start(bf16[2,2,32,2048]{3,2,1,0:T(8,128)(2,1)} %refs_4_.1) | copy-start | bytes 1572868
  0.6 1.7 %copy-start.1 = (f32[2,32,2048]{2,1,0:T(8,128)S(1)}, f32[2,32,2048]{2,1,0:T(8,128)}, u32[]{:S(2)}) copy-start(f32[2,32,2048]{2,1,0:T(8,128)} %background_ref.5) | copy-start | bytes 1572868
  1.8 1.6 %collective-permute-start = (bf16[2,3,8,2048]{3,2,1,0:T(8,128)(2,1)S(1)}, bf16[2,3,8,2048]{3,2,1,0:T(8,128)(2,1)S(1)}, u32[]{:S(2)}, u32[]{:S(2)}) collective-permute-start(bf16[2,3,8,2048]{3,2,1,0:T(8,128)(2,1)S(1)} %get-tuple-element.14), channel_id=1, source_target_pairs={{0,1},{1,0},{2,3},{3,2},{4,5},{5,4},{6,7},{7,6},{8,9},{9,8},{10,11... | collective-permute-start | bytes 589832 | tf_op jit(solution)/shard_map/ppermute | solution.py:340
  3.4 8.8 %copy-start.2 = (bf16[2,32,2048]{2,1,0:T(8,128)(2,1)S(1)}, bf16[2,32,2048]{2,1,0:T(8,128)(2,1)}, u32[]{:S(2)}) copy-start(bf16[2,32,2048]{2,1,0:T(8,128)(2,1)} %measured_ref.3) | copy-start | bytes 786436
  5.3 8.0 %collective-permute-start.1 = (bf16[2,9,16,128]{3,2,1,0:T(8,128)(2,1)S(1)}, bf16[2,9,16,128]{3,2,1,0:T(8,128)(2,1)S(1)}, u32[]{:S(2)}, u32[]{:S(2)}) collective-permute-start(bf16[2,9,16,128]{3,2,1,0:T(8,128)(2,1)S(1)} %get-tuple-element.19), channel_id=1, source_target_pairs={{0,4},{4,8},{8,12},{12,0},{1,5},{5,9},{9,13},{13,1},{2,6},{6,10},{... | collective-permute-start | bytes 221192 | tf_op jit(solution)/shard_map/ppermute | solution.py:368
  8.2 7.9 %collective-permute-start.2 = (bf16[2,9,16,128]{3,2,1,0:T(8,128)(2,1)S(1)}, bf16[2,9,16,128]{3,2,1,0:T(8,128)(2,1)S(1)}, u32[]{:S(2)}, u32[]{:S(2)}) collective-permute-start(bf16[2,9,16,128]{3,2,1,0:T(8,128)(2,1)S(1)} %get-tuple-element.20), channel_id=1, source_target_pairs={{0,8},{4,12},{8,0},{12,4},{1,9},{5,13},{9,1},{13,5},{2,10},{6,14},... | collective-permute-start | bytes 221192 | tf_op jit(solution)/shard_map/ppermute | solution.py:368
  10.8 5.5 %collective-permute-start.3 = (bf16[2,9,16,128]{3,2,1,0:T(8,128)(2,1)S(1)}, bf16[2,9,16,128]{3,2,1,0:T(8,128)(2,1)S(1)}, u32[]{:S(2)}, u32[]{:S(2)}) collective-permute-start(bf16[2,9,16,128]{3,2,1,0:T(8,128)(2,1)S(1)} %get-tuple-element.21), channel_id=1, source_target_pairs={{0,12},{4,0},{8,4},{12,8},{1,13},{5,1},{9,5},{13,9},{2,14},{6,2},{... | collective-permute-start | bytes 221192 | tf_op jit(solution)/shard_map/ppermute | solution.py:368
  16.4 6.8 %collective-permute-start.4 = (bf16[2,9,16,128]{3,2,1,0:T(8,128)(2,1)S(1)}, bf16[2,9,16,128]{3,2,1,0:T(8,128)(2,1)S(1)}, u32[]{:S(2)}, u32[]{:S(2)}) collective-permute-start(bf16[2,9,16,128]{3,2,1,0:T(8,128)(2,1)S(1)} %get-tuple-element.25.refs_0_), channel_id=1, source_target_pairs={{0,4},{4,8},{8,12},{12,0},{1,5},{5,9},{9,13},{13,1},{2,6},{6,10},{... | collective-permute-start | bytes 221192 | tf_op jit(solution)/shard_map/ppermute | solution.py:386
  18.3 7.1 %collective-permute-start.5 = (bf16[2,9,16,128]{3,2,1,0:T(8,128)(2,1)S(1)}, bf16[2,9,16,128]{3,2,1,0:T(8,128)(2,1)S(1)}, u32[]{:S(2)}, u32[]{:S(2)}) collective-permute-start(bf16[2,9,16,128]{3,2,1,0:T(8,128)(2,1)S(1)} %get-tuple-element.25.refs_0_), channel_id=1, source_target_pairs={{0,8},{4,12},{8,0},{12,4},{1,9},{5,13},{9,1},{13,5},{2,10},{6,14},... | collective-permute-start | bytes 221192 | tf_op jit(solution)/shard_map/ppermute | solution.py:386
  19.9 5.6 %collective-permute-start.6 = (bf16[2,9,16,128]{3,2,1,0:T(8,128)(2,1)S(1)}, bf16[2,9,16,128]{3,2,1,0:T(8,128)(2,1)S(1)}, u32[]{:S(2)}, u32[]{:S(2)}) collective-permute-start(bf16[2,9,16,128]{3,2,1,0:T(8,128)(2,1)S(1)} %get-tuple-element.25.refs_0_), channel_id=1, source_target_pairs={{0,12},{4,0},{8,4},{12,8},{1,13},{5,1},{9,5},{13,9},{2,14},{6,2},{... | collective-permute-start | bytes 221192 | tf_op jit(solution)/shard_map/ppermute | solution.py:386
  25.6 5.6 %collective-permute-start.7 = (bf16[4,9,16,128]{3,2,1,0:T(8,128)(2,1)S(1)}, bf16[4,9,16,128]{3,2,1,0:T(8,128)(2,1)S(1)}, u32[]{:S(2)}, u32[]{:S(2)}) collective-permute-start(bf16[4,9,16,128]{3,2,1,0:T(8,128)(2,1)S(1)} %pad_maximum_fusion.summed_ref), channel_id=1, source_target_pairs={{0,2},{2,0},{1,3},{3,1},{4,6},{6,4},{5,7},{7,5},{8,10},{10,8},{9,1... | collective-permute-start | bytes 442376 | tf_op jit(solution)/shard_map/ppermute | solution.py:391

commit v4 on v3

--- a/solution.py
+++ b/solution.py
@@ -37,9 +37,10 @@
     return jnp.abs(row - col) <= reach
 
 
-def border_kernel(volume_ref, background_ref, measured_ref, psf_ref, border_ref, table_ref, volume_edge, background_edge, sems):
+def border_kernel(volume_ref, background_ref, psf_ref, border_ref, table_ref, volume_edge, background_edge, sems):
     frames, depth, row_count = volume_ref.shape[:3]
-    width = border_ref.shape[2]
+    half = border_ref.shape[2]
+    width = volume_edge.shape[2]
     tile = lax.axis_index("tile")
 
     def copies(start):
@@ -47,10 +48,9 @@
         return (
             pltpu.make_async_copy(volume_ref.at[:, :, rows, :], volume_edge, sems.at[0]),
             pltpu.make_async_copy(background_ref.at[:, rows, :], background_edge, sems.at[1]),
-            pltpu.make_async_copy(measured_ref.at[:, rows, :], border_ref.at[:, depth], sems.at[2]),
         )
 
-    spread = pltpu.make_async_copy(psf_ref, table_ref, sems.at[3])
+    spread = pltpu.make_async_copy(psf_ref, table_ref, sems.at[2])
 
     @pl.when(tile == 0)
     def _():
@@ -67,7 +67,8 @@
         copy.wait()
     for f in range(frames):
         for d in range(depth):
-            border_ref[f, d] = (volume_edge[f, d].astype(F32) + background_edge[d]).astype(BF16)
+            total = volume_edge[f, d].astype(F32) + background_edge[d]
+            border_ref[f, d] = jnp.where(tile == 0, total[width - half :], total[:half]).astype(BF16)
     spread.wait()
 
 
@@ -97,23 +98,21 @@
                 lanes = pl.ds(j * LANES, LANES)
                 total = (volume_ref[f, d, :, lanes].astype(F32) + background_ref[d, :, lanes]).astype(BF16).astype(F32)
                 rows_ref[pl.ds(PAD + base + j, row_count, stride=blocks), :] = total
-            own = (f * depth + d) * span + (half + half * tile) * blocks
-            empty = pl.multiple_of((f * depth + d) * span + (row_count + 2 * half) * blocks * tile, blocks)
+            own = (f * depth + d) * span + half * blocks
+            empty = pl.multiple_of((f * depth + d) * span + (row_count + half) * blocks * tile, blocks)
             left_ref[pl.ds(empty, half * blocks), :] = jnp.zeros((half * blocks, 2 * LANES), BF16)
             left_ref[pl.ds((f * depth + d + 1) * span - blocks, blocks), :] = jnp.zeros((blocks, 2 * LANES), BF16)
             for r in range(row_count):
                 here, edges = with_edges(rows_ref, PAD + base + r * blocks, blocks, blocks, *masks)
-                rows = pl.ds(pl.multiple_of(own + r * blocks, blocks), blocks)
+                rows = pl.ds(own + r * blocks, blocks)
                 left_ref[rows, pl.ds(0, LANES)] = here
                 left_ref[rows, pl.ds(LANES, LANES)] = edges
 
 
-def backward_table_kernel(psf_ref, measured_ref, got_ref, table_ref, inverse_ref, chunk_ref, base_ref, rows_ref):
+def backward_table_kernel(psf_ref, measured_ref, table_ref, inverse_ref, chunk_ref, base_ref, rows_ref):
     depth, taps, pitch, width = psf_ref.shape
     frames, row_count, col_count = measured_ref.shape
     blocks = col_count // LANES
-    extra = (taps - 1) // 2
-    got_rows = got_ref.shape[2]
     chunk_rows = chunk_ref.shape[1]
     fill_base(psf_ref, base_ref)
     near = near_mask(width)
@@ -126,20 +125,15 @@
             table_ref[t, pl.ds(0, LANES), lanes] = jnp.where(near, band, 0.0).astype(BF16)
             table_ref[t, pl.ds(LANES, LANES), lanes] = jnp.where(near, 0.0, band).astype(BF16)
         inverse_ref[d] = 1.0 / total
-    tile = lax.axis_index("tile")
     place = lax.axis_index("depth")
     per_frame = rows_ref.shape[0] // frames
-    rows_ref[...] = jnp.ones_like(rows_ref)
-    for f in range(frames):
-        start = f * per_frame + extra * blocks
-        own = start + extra * blocks * tile
-        other = start + (row_count * (1 - tile) - (got_rows - extra) * tile) * blocks
+    if per_frame > row_count * blocks:
+        rows_ref[...] = jnp.ones_like(rows_ref)
+    for f in range(frames):
+        start = f * per_frame
         for j in range(blocks):
             lanes = pl.ds(j * LANES, LANES)
-            values = measured_ref[f, :, lanes].astype(F32)
-            rows_ref[pl.ds(own + j, row_count, stride=blocks), :] = values
-            values = got_ref[f, depth, :, lanes].astype(F32)
-            rows_ref[pl.ds(other + j, got_rows, stride=blocks), :] = values
+            rows_ref[pl.ds(start + j, row_count, stride=blocks), :] = measured_ref[f, :, lanes].astype(F32)
         for r in range(chunk_rows):
             at = pl.multiple_of(start + (place * chunk_rows + r) * blocks, blocks)
             chunk_ref[f, r] = rows_ref[pl.ds(at, blocks), :]
@@ -164,14 +158,17 @@
 PAD = 8
 
 
+def partners(chunks):
+    return [0] + sorted(range(1, chunks), key=lambda mask: (mask != chunks - 1, mask))
+
+
 def sensor_kernel(chunks, row_count, half, given_ref, got_ref, table_ref, own_ref, *rest):
     sent_refs = rest[: chunks - 1]
     left_ref, rows_ref, sums_ref, whole_ref = rest[chunks - 1 :]
-    frames, layers, halo, col_count = got_ref.shape
-    depth = layers - 1
+    frames, depth, halo, col_count = got_ref.shape
     blocks = col_count // LANES
     pairs = table_ref.shape[1]
-    sensor_rows = row_count + half
+    sensor_rows = row_count
     span = left_ref.shape[0] // (frames * depth)
     tile = lax.axis_index("tile")
     place = lax.axis_index("depth")
@@ -203,7 +200,7 @@
         if whole_ref.shape[1] > count:
             whole_ref[f, pl.ds(count, whole_ref.shape[1] - count), :] = jnp.ones((whole_ref.shape[1] - count, LANES), F32)
         for s in range(chunks):
-            target = lax.rem(place + s, chunks)
+            target = place if s == 0 else lax.bitwise_xor(place, partners(chunks)[s])
             for r in range(chunk_rows):
                 start = pl.multiple_of((target * chunk_rows + r) * blocks, blocks)
                 values = whole_ref[f, pl.ds(start, blocks), :]
@@ -213,37 +210,47 @@
                     sent_refs[s - 1][f, r] = values.astype(BF16)
 
 
-def spread_ratio(chunks, images, get, rows_ref, left_ref, row_count, half, blocks):
+def spread_ratio(images, row_count, half, blocks, own, border, rows_ref, left_ref):
+    tile = lax.axis_index("tile")
+    masks = edge_masks(blocks, blocks)
+    windows = row_count + 2 * half
+    for f in range(images):
+        first = PAD + f * windows * blocks
+        for r in range(row_count):
+            rows_ref[pl.ds(first + (half + r) * blocks, blocks), :] = own(f, r)
+        for r in range(half):
+            at = first + ((row_count + half) * (1 - tile) + r) * blocks
+            rows_ref[pl.ds(pl.multiple_of(at, 8), blocks), :] = border(f, r)
+        empty = pl.multiple_of(first + (row_count + half) * blocks * tile, 8)
+        rows_ref[pl.ds(empty, half * blocks), :] = jnp.zeros((half * blocks, LANES), F32)
+        for r in range(windows):
+            here, edges = with_edges(rows_ref, first + r * blocks, blocks, blocks, *masks)
+            rows = pl.ds((f * windows + r) * blocks, blocks)
+            left_ref[rows, pl.ds(0, LANES)] = here
+            left_ref[rows, pl.ds(LANES, LANES)] = edges
+
+
+def collect_kernel(chunks, row_count, half, *refs):
+    ratio_refs = refs[:chunks]
+    image_ref, summed_ref, border_ref, border_sum_ref = refs[chunks:]
+    frames, chunk_rows = ratio_refs[0].shape[:2]
     tile = lax.axis_index("tile")
     place = lax.axis_index("depth")
-    use_after, use_before = edge_masks(blocks, blocks)
-    windows = row_count + 2 * half
-    span = windows * blocks
-    sensor_rows = row_count + half
-    for f in range(images):
-        first = PAD + f * max(windows, chunks * get.rows + half) * blocks
-        empty = pl.multiple_of(first + sensor_rows * blocks * tile, 8)
-        base = first + half * blocks * (1 - tile)
-        for s in range(chunks):
-            source = lax.rem(place + chunks - s, chunks)
-            chunk_rows = get.rows
-            for r in range(chunk_rows):
-                start = pl.multiple_of(base + (source * chunk_rows + r) * blocks, 8)
-                rows_ref[pl.ds(start, blocks), :] = get(s, f, r)
-        rows_ref[pl.ds(empty, half * blocks), :] = jnp.zeros((half * blocks, LANES), F32)
-        for r in range(windows):
-            here, edges = with_edges(rows_ref, first + r * blocks, blocks, blocks, use_after, use_before)
-            left_ref[pl.ds(f * span + r * blocks, blocks), pl.ds(0, LANES)] = here
-            left_ref[pl.ds(f * span + r * blocks, blocks), pl.ds(LANES, LANES)] = edges
-
-
-class Chunk:
-    def __init__(self, rows, read):
-        self.rows = rows
-        self.read = read
-
-    def __call__(self, s, f, r):
-        return self.read(s, f, r)
+    for s, mask in enumerate(partners(chunks)):
+        source = lax.bitwise_xor(place, mask) if s else place
+        for r in range(chunk_rows):
+            total = None
+            for f in range(frames):
+                values = ratio_refs[s][f, r]
+                image_ref[f, source * chunk_rows + r] = values
+                values = values.astype(F32)
+                total = values if total is None else total + values
+            summed_ref[source * chunk_rows + r] = total.astype(BF16)
+    edge = (row_count - half) * (1 - tile)
+    for r in range(half):
+        border_sum_ref[r] = summed_ref[edge + r]
+        for f in range(frames):
+            border_ref[f, r] = image_ref[f, edge + r]
 
 
 def backproject(f, span, taps, row_count, blocks, left_ref, table_ref):
@@ -255,14 +262,21 @@
     return total
 
 
-def volume_kernel(chunks, half, *refs):
-    ratio_refs = refs[:chunks]
-    volume_ref, table_ref, inverse_ref, out_ref, rows_ref, left_ref, sums_ref = refs[chunks:]
+def volume_kernel(image_ref, border_ref, volume_ref, table_ref, inverse_ref, out_ref, rows_ref, left_ref, sums_ref):
     frames, depth, row_count, col_count = volume_ref.shape
+    half = border_ref.shape[1]
     blocks = col_count // LANES
     taps = table_ref.shape[0]
-    get = Chunk(ratio_refs[0].shape[1], lambda s, f, r: ratio_refs[s][f, r].astype(F32))
-    spread_ratio(chunks, frames, get, rows_ref, left_ref, row_count, half, blocks)
+    spread_ratio(
+        frames,
+        row_count,
+        half,
+        blocks,
+        lambda f, r: image_ref[f, r].astype(F32),
+        lambda f, r: border_ref[f, r].astype(F32),
+        rows_ref,
+        left_ref,
+    )
     span = (row_count + 2 * half) * blocks
     for f in range(frames):
         total = backproject(f, span, taps, row_count, blocks, left_ref, table_ref)
@@ -276,12 +290,21 @@
                 out_ref[f, d, :, lanes] = value.astype(BF16)
 
 
-def background_kernel(chunks, half, scale, summed_ref, got_ref, background_ref, table_ref, inverse_ref, out_ref, rows_ref, left_ref, sums_ref):
+def background_kernel(scale, summed_ref, got_ref, border_ref, border_got_ref, background_ref, table_ref, inverse_ref, out_ref, rows_ref, left_ref, sums_ref):
     depth, row_count, col_count = background_ref.shape
+    half = border_ref.shape[0]
     blocks = col_count // LANES
     taps = table_ref.shape[0]
-    get = Chunk(summed_ref.shape[1], lambda s, f, r: summed_ref[s, r].astype(F32) + got_ref[s, r].astype(F32))
-    spread_ratio(chunks, 1, get, rows_ref, left_ref, row_count, half, blocks)
+    spread_ratio(
+        1,
+        row_count,
+        half,
+        blocks,
+        lambda f, r: summed_ref[r].astype(F32) + got_ref[r].astype(F32),
+        lambda f, r: border_ref[r].astype(F32) + border_got_ref[r].astype(F32),
+        rows_ref,
+        left_ref,
+    )
     span = (row_count + 2 * half) * blocks
     total = backproject(0, span, taps, row_count, blocks, left_ref, table_ref)
     for d in range(depth):
@@ -319,29 +342,30 @@
     pairs = (taps + 1) // 2
     chunks = lax.axis_size("depth")
     splits = lax.axis_size("tm")
-    sensor_rows = row_count + half
-    chunk_rows = -(-sensor_rows // chunks)
+    chunk_rows = -(-row_count // chunks)
+    padded_rows = chunks * chunk_rows
+    windows = row_count + 2 * half
     shape = jax.ShapeDtypeStruct
     vmem = pltpu.VMEM
 
     swap = [(0, 1), (1, 0)]
+    edge_rows = 8 * -(-half // 8)
     sent, table = pl.pallas_call(
         border_kernel,
-        out_shape=(shape((frames, depth + 1, 2 * half, col_count), BF16), shape(psf.shape, BF16)),
-        in_specs=[pl.BlockSpec(memory_space=pltpu.HBM)] * 4,
+        out_shape=(shape((frames, depth, half, col_count), BF16), shape(psf.shape, BF16)),
+        in_specs=[pl.BlockSpec(memory_space=pltpu.HBM)] * 3,
         out_specs=(pl.BlockSpec(memory_space=pltpu.VMEM),) * 2,
         scratch_shapes=[
-            vmem((frames, depth, 2 * half, col_count), BF16),
-            vmem((depth, 2 * half, col_count), F32),
-            pltpu.SemaphoreType.DMA((4,)),
+            vmem((frames, depth, edge_rows, col_count), BF16),
+            vmem((depth, edge_rows, col_count), F32),
+            pltpu.SemaphoreType.DMA((3,)),
         ],
         compiler_params=pltpu.CompilerParams(vmem_limit_bytes=8 * 2**20),
-    )(*[pltpu.with_memory_space_constraint(a, pltpu.HBM) for a in (volume, background, measured, psf)])
+    )(*[pltpu.with_memory_space_constraint(a, pltpu.HBM) for a in (volume, background, psf)])
     border = lax.ppermute(sent, "tile", swap)
 
     base = vmem((depth * taps * pitch, LANES), F32)
-    windows = sensor_rows + 2 * half + 1
-    left_shape = shape((frames * depth * windows * blocks, 2 * LANES), BF16)
+    left_shape = shape((frames * depth * (windows + 1) * blocks, 2 * LANES), BF16)
     forward, left = call(
         forward_table_kernel,
         (table, volume, background),
@@ -349,71 +373,87 @@
         [base, vmem((frames * depth * row_count * blocks + 2 * PAD, LANES), F32)],
         2 * 10**8,
     )
-    padded_rows = chunks * chunk_rows
     chunk = (frames, chunk_rows, blocks, LANES)
     parts = call(
         functools.partial(sensor_kernel, chunks, row_count, half),
         (left, border, forward),
         (shape(chunk, F32),) + (shape(chunk, BF16),) * (chunks - 1) + (left_shape,),
         [
-            vmem((frames * depth * 2 * half * blocks + 2 * PAD, LANES), F32),
-            vmem(((sensor_rows + 1) * blocks, 2 * LANES), F32),
+            vmem((frames * depth * half * blocks + 2 * PAD, LANES), F32),
+            vmem(((row_count + 1) * blocks, 2 * LANES), F32),
             vmem((frames, padded_rows * blocks, LANES), F32),
         ],
         2 * 10**9,
         {0: chunks},
     )
     sensor = parts[0]
+    masks = partners(chunks)
     moved = [
-        lax.ppermute(parts[s], "depth", [(i, (i + s) % chunks) for i in range(chunks)])
+        lax.ppermute(parts[s], "depth", [(i, i ^ masks[s]) for i in range(chunks)])
         for s in range(1, chunks)
     ]
     backward, inverse, measured_chunk = call(
         backward_table_kernel,
-        (table, measured, border),
+        (table, measured),
         (
             shape((taps, 2 * LANES, depth * LANES), BF16),
             shape((depth, 1, LANES), F32),
             shape(chunk, F32),
         ),
-        [base, vmem((frames * (half + max(padded_rows, row_count + 2 * half)) * blocks, LANES), F32)],
+        [base, vmem((frames * padded_rows * blocks, LANES), F32)],
         2 * 10**8,
     )
     for part in moved:
         sensor = sensor + part.astype(F32)
     ratio = (measured_chunk / sensor).astype(BF16)
     ratios = [ratio] + [
-        lax.ppermute(ratio, "depth", [(i, (i + s) % chunks) for i in range(chunks)])
+        lax.ppermute(ratio, "depth", [(i, i ^ masks[s]) for i in range(chunks)])
         for s in range(1, chunks)
     ]
-    summed = jnp.stack([jnp.sum(r.astype(F32), axis=0) for r in ratios]).astype(BF16)
+    image, summed, edge, edge_sum = call(
+        functools.partial(collect_kernel, chunks, row_count, half),
+        tuple(ratios),
+        (
+            shape((frames, padded_rows, blocks, LANES), BF16),
+            shape((padded_rows, blocks, LANES), BF16),
+            shape((frames, half, blocks, LANES), BF16),
+            shape((half, blocks, LANES), BF16),
+        ),
+        [],
+        10**6,
+    )
     if splits == 2:
-        others = lax.ppermute(summed, "tm", swap)
+        got = lax.ppermute(summed, "tm", swap)
+        other_got = lax.ppermute(edge_sum, ("tm", "tile"), [(i, 3 - i) for i in range(4)])
+    edge = lax.ppermute(edge, "tile", swap)
+    other = jnp.sum(edge.astype(F32), axis=0)
+    if splits == 2:
+        other = other.astype(BF16)
     else:
-        total = lax.psum(summed.astype(F32), "tm").astype(BF16)
-        summed, others = total, jnp.zeros_like(total)
-    window_rows = max(row_count + 2 * half, padded_rows + half) * blocks
+        summed = lax.psum(summed.astype(F32), "tm").astype(BF16)
+        other = lax.psum(other.astype(BF16).astype(F32), "tm").astype(BF16)
+        got, other_got = jnp.zeros_like(summed), jnp.zeros_like(other)
+    new_background = call(
+        functools.partial(background_kernel, 1.0 / (frames * splits)),
+        (summed, got, other, other_got, background, backward, inverse),
+        shape(background.shape, F32),
+        [
+            vmem((windows * blocks + 2 * PAD, LANES), F32),
+            vmem((windows * blocks, 2 * LANES), BF16),
+            vmem((depth * row_count * blocks, LANES), F32),
+        ],
+        10**9,
+    )
     new_volume = call(
-        functools.partial(volume_kernel, chunks, half),
-        (*ratios, volume, backward, inverse),
+        volume_kernel,
+        (image, edge, volume, backward, inverse),
         shape(volume.shape, BF16),
         [
-            vmem((frames * window_rows + 2 * PAD, LANES), F32),
-            vmem((frames * (row_count + 2 * half) * blocks, 2 * LANES), BF16),
+            vmem((frames * windows * blocks + 2 * PAD, LANES), F32),
+            vmem((frames * windows * blocks, 2 * LANES), BF16),
             vmem((frames * depth * row_count * blocks, LANES), F32),
         ],
         2 * 10**9,
-    )
-    new_background = call(
-        functools.partial(background_kernel, chunks, half, 1.0 / (frames * splits)),
-        (summed, others, background, backward, inverse),
-        shape(background.shape, F32),
-        [
-            vmem((window_rows + 2 * PAD, LANES), F32),
-            vmem(((row_count + 2 * half) * blocks, 2 * LANES), BF16),
-            vmem((depth * row_count * blocks, LANES), F32),
-        ],
-        10**9,
     )
     return new_volume, new_background
 

time: 33 us -> 31.9 us (0.967)
  starting transfers between devices: 13.3 us -> 12.6 us
    ppermute x7 -> x9, starting transfers between devices: 12.8 us -> 12 us  [the longest x3 5.65 us: body(): lax.ppermute(parts[s], 'depth', [(i, i ^ masks[s]) for i in range(chunks)])]
    pallas_call x5 -> x6, Pallas kernels: 8.03 us -> 7.81 us  [call(): pl.pallas_call(kernel, out_shape=outs, in_specs=whole(len(args)), out_spe...]
    ppermute x7 -> x9, waiting for transfers between devices: 9.32 us -> 9.43 us  [the longest x3 4.26 us: body(): lax.ppermute(parts[s], 'depth', [(i, i ^ masks[s]) for i in range(chunks)])]
  transfers between devices with their start and end apart: 8 -> 10, of which waited for: 7 -> 8; matrix products, arithmetic and copies ran while one was open for 0% -> 0% of each run, Pallas kernels for 14% -> 14%
where the time goes in v4:
time: 31.9 us; the launch traced here: 31.7 us
  starting transfers between devices  12.6 us (39%)
  waiting for transfers between devices  9.43 us (30%)
  Pallas kernels  8.95 us (28%)
  between operations  0.72 us (2%)
    pallas_call x6, Pallas kernels, call(): pl.pallas_call(kernel, out_shape=outs, in_specs=whole(len(args)), out_spe...  7.81 us
    ppermute x3, starting transfers between devices, body(): lax.ppermute(parts[s], 'depth', [(i, i ^ masks[s]) for i in range(chunks)])  5.65 us
    ppermute x3, starting transfers between devices, body(): lax.ppermute(ratio, 'depth', [(i, i ^ masks[s]) for i in range(chunks)])  4.45 us
    ppermute x3, waiting for transfers between devices, body(): lax.ppermute(parts[s], 'depth', [(i, i ^ masks[s]) for i in range(chunks)])  4.26 us
    ppermute x3, waiting for transfers between devices, body(): lax.ppermute(ratio, 'depth', [(i, i ^ masks[s]) for i in range(chunks)])  3.54 us
    ppermute x1, starting transfers between devices, body(): got = lax.ppermute(summed, 'tm', swap)  1.56 us
    ppermute x1, waiting for transfers between devices, body(): lax.ppermute(edge_sum, ('tm', 'tile'), [(i, 3 - i) for i in range(4)])  1.35 us
    pallas_call x1, Pallas kernels, body(): pl.pallas_call(border_kernel, out_shape=(shape((frames, depth, half, col_...  1.14 us
  transfers between devices with their start and end apart: 10, of which 8 were waited for; matrix products, arithmetic and copies ran while one was open for 0% of the time, Pallas kernels for 14%

profile of v4, /device:TPU:0, one launch (start us, length us, event | category | flops | bytes accessed | tf_op | source)
XLA Modules:
  0.0 31.7 jit_solution(4739864378661100631)
XLA Ops:
  0.6 1.1 %shard_map.59 = (bf16[2,2,4,2048]{3,2,1,0:T(4,128)(2,1)S(1)}, bf16[2,9,16,17]{3,2,1,0:T(8,128)(2,1)S(1)}) custom-call(bf16[2,2,32,2048]{3,2,1,0:T(8,128)(2,1)} %volume_ref.5, f32[2,32,2048]{2,1,0:T(8,128)} %background_ref.5, bf16[2,9,16,17]{3,2,1,0:T(8,128)(2,1)} %psf_ref.1), custom_call_target="tpu_custom_call" | custom-call | tf_op jit(solution)/shard_map/pallas_call | solution.py:353
  1.8 0.5 %collective-permute-start = (bf16[2,2,4,2048]{3,2,1,0:T(4,128)(2,1)S(1)}, bf16[2,2,4,2048]{3,2,1,0:T(4,128)(2,1)S(1)}, u32[]{:S(2)}, u32[]{:S(2)}) collective-permute-start(bf16[2,2,4,2048]{3,2,1,0:T(4,128)(2,1)S(1)} %get-tuple-element.20), channel_id=1, source_target_pairs={{0,1},{1,0},{2,3},{3,2},{4,5},{5,4},{6,7},{7,6},{8,9},{9,8},{10,11... | collective-permute-start | bytes 196616 | tf_op jit(solution)/shard_map/ppermute | solution.py:365
  2.3 0.9 %shard_map.61 = (bf16[2,5,256,256]{3,2,1,0:T(8,128)(2,1)S(1)}, bf16[2624,256]{1,0:T(8,128)(2,1)S(1)}) custom-call(bf16[2,9,16,17]{3,2,1,0:T(8,128)(2,1)S(1)} %get-tuple-element.17.psf_ref, bf16[2,2,32,2048]{3,2,1,0:T(8,128)(2,1)S(1)} %copy-done, f32[2,32,2048]{2,1,0:T(8,128)S(1)} %copy-done.1), custom_call_target="tpu_custom_call" | custom-call | flops 200000000 | bytes 1058368 | tf_op jit(solution)/shard_map/pallas_call | solution.py:325
  3.2 1.6 %shard_map.62 = (f32[2,8,16,128]{3,2,1,0:T(8,128)S(1)}, bf16[2,8,16,128]{3,2,1,0:T(8,128)(2,1)S(1)}, bf16[2,8,16,128]{3,2,1,0:T(8,128)(2,1)S(1)}, bf16[2,8,16,12...) custom-call(bf16[2624,256]{1,0:T(8,128)(2,1)S(1)} %get-tuple-element.19.given_ref, ...), custom_call_target="tpu_custom_call", output_to_operand_aliasing={{4}: (0, {})} | custom-call | flops 2000000000 | bytes 2719744 | tf_op jit(solution)/shard_map/pallas_call | solution.py:325
  4.9 5.0 %collective-permute-start.1 = (bf16[2,8,16,128]{3,2,1,0:T(8,128)(2,1)S(1)}, bf16[2,8,16,128]{3,2,1,0:T(8,128)(2,1)S(1)}, u32[]{:S(2)}, u32[]{:S(2)}) collective-permute-start(bf16[2,8,16,128]{3,2,1,0:T(8,128)(2,1)S(1)} %get-tuple-element.23), channel_id=1, source_target_pairs={{0,12},{4,8},{8,4},{12,0},{1,13},{5,9},{9,5},{13,1},{2,14},{6,10},... | collective-permute-start | bytes 196616 | tf_op jit(solution)/shard_map/ppermute | solution.py:392
  9.9 0.6 %collective-permute-start.3 = (bf16[2,8,16,128]{3,2,1,0:T(8,128)(2,1)S(1)}, bf16[2,8,16,128]{3,2,1,0:T(8,128)(2,1)S(1)}, u32[]{:S(2)}, u32[]{:S(2)}) collective-permute-start(bf16[2,8,16,128]{3,2,1,0:T(8,128)(2,1)S(1)} %get-tuple-element.25), channel_id=1, source_target_pairs={{0,8},{4,12},{8,0},{12,4},{1,9},{5,13},{9,1},{13,5},{2,10},{6,14},... | collective-permute-start | bytes 196616 | tf_op jit(solution)/shard_map/ppermute | solution.py:392
  10.5 1.0 %shard_map.60 = (bf16[9,256,256]{2,1,0:T(8,128)(2,1)S(1)}, f32[2,1,128]{2,1,0:T(1,128)S(1)}, f32[2,8,16,128]{3,2,1,0:T(8,128)S(1)}) custom-call(bf16[2,9,16,17]{3,2,1,0:T(8,128)(2,1)S(1)} %get-tuple-element.17.psf_ref, bf16[2,32,2048]{2,1,0:T(8,128)(2,1)S(1)} %copy-done.2), custom_call_target="tpu_custom_call" | custom-call | flops 200000000 | bytes 271936 | tf_op jit(solution)/shard_map/pallas_call | solution.py:325
  11.5 1.3 %collective-permute-done.1 = bf16[2,8,16,128]{3,2,1,0:T(8,128)(2,1)S(1)} collective-permute-done((bf16[2,8,16,128]{3,2,1,0:T(8,128)(2,1)S(1)}, bf16[2,8,16,128]{3,2,1,0:T(8,128)(2,1)S(1)}, u32[]{:S(2)}, u32[]{:S(2)}) %collective-permute-start.1) | collective-permute-done | bytes 65568 | tf_op jit(solution)/shard_map/ppermute | solution.py:392
  12.8 2.1 %collective-permute-done.2 = bf16[2,8,16,128]{3,2,1,0:T(8,128)(2,1)S(1)} collective-permute-done((bf16[2,8,16,128]{3,2,1,0:T(8,128)(2,1)S(1)}, bf16[2,8,16,128]{3,2,1,0:T(8,128)(2,1)S(1)}, u32[]{:S(2)}, u32[]{:S(2)}) %collective-permute-start.2) | collective-permute-done | bytes 65568 | tf_op jit(solution)/shard_map/ppermute | solution.py:392
  14.9 0.8 %collective-permute-done.3 = bf16[2,8,16,128]{3,2,1,0:T(8,128)(2,1)S(1)} collective-permute-done((bf16[2,8,16,128]{3,2,1,0:T(8,128)(2,1)S(1)}, bf16[2,8,16,128]{3,2,1,0:T(8,128)(2,1)S(1)}, u32[]{:S(2)}, u32[]{:S(2)}) %collective-permute-start.3) | collective-permute-done | bytes 65568 | tf_op jit(solution)/shard_map/ppermute | solution.py:392
  15.8 2.3 %collective-permute-start.4 = (bf16[2,8,16,128]{3,2,1,0:T(8,128)(2,1)S(1)}, bf16[2,8,16,128]{3,2,1,0:T(8,128)(2,1)S(1)}, u32[]{:S(2)}, u32[]{:S(2)}) collective-permute-start(bf16[2,8,16,128]{3,2,1,0:T(8,128)(2,1)S(1)} %divide_convert_fusion.refs_0_), channel_id=1, source_target_pairs={{0,12},{4,8},{8,4},{12,0},{1,13},{5,9},{9,5},{13,1},{2,14},{6,10},... | collective-permute-start | bytes 196616 | tf_op jit(solution)/shard_map/ppermute | solution.py:410
  18.1 0.4 %collective-permute-start.5 = (bf16[2,8,16,128]{3,2,1,0:T(8,128)(2,1)S(1)}, bf16[2,8,16,128]{3,2,1,0:T(8,128)(2,1)S(1)}, u32[]{:S(2)}, u32[]{:S(2)}) collective-permute-start(bf16[2,8,16,128]{3,2,1,0:T(8,128)(2,1)S(1)} %divide_convert_fusion.refs_0_), channel_id=1, source_target_pairs={{0,4},{4,0},{8,12},{12,8},{1,5},{5,1},{9,13},{13,9},{2,6},{6,2},{1... | collective-permute-start | bytes 196616 | tf_op jit(solution)/shard_map/ppermute | solution.py:410
  18.4 1.8 %collective-permute-start.6 = (bf16[2,8,16,128]{3,2,1,0:T(8,128)(2,1)S(1)}, bf16[2,8,16,128]{3,2,1,0:T(8,128)(2,1)S(1)}, u32[]{:S(2)}, u32[]{:S(2)}) collective-permute-start(bf16[2,8,16,128]{3,2,1,0:T(8,128)(2,1)S(1)} %divide_convert_fusion.refs_0_), channel_id=1, source_target_pairs={{0,8},{4,12},{8,0},{12,4},{1,9},{5,13},{9,1},{13,5},{2,10},{6,14},... | collective-permute-start | bytes 196616 | tf_op jit(solution)/shard_map/ppermute | solution.py:410
  20.3 1.8 %collective-permute-done.4.refs_1_ = bf16[2,8,16,128]{3,2,1,0:T(8,128)(2,1)S(1)} collective-permute-done((bf16[2,8,16,128]{3,2,1,0:T(8,128)(2,1)S(1)}, bf16[2,8,16,128]{3,2,1,0:T(8,128)(2,1)S(1)}, u32[]{:S(2)}, u32[]{:S(2)}) %collective-permute-start.4) | collective-permute-done | bytes 65568 | tf_op jit(solution)/shard_map/ppermute | solution.py:410
  22.1 1.0 %collective-permute-done.5.refs_2_ = bf16[2,8,16,128]{3,2,1,0:T(8,128)(2,1)S(1)} collective-permute-done((bf16[2,8,16,128]{3,2,1,0:T(8,128)(2,1)S(1)}, bf16[2,8,16,128]{3,2,1,0:T(8,128)(2,1)S(1)}, u32[]{:S(2)}, u32[]{:S(2)}) %collective-permute-start.5) | collective-permute-done | bytes 65568 | tf_op jit(solution)/shard_map/ppermute | solution.py:410
  23.1 0.7 %collective-permute-done.6.refs_3_ = bf16[2,8,16,128]{3,2,1,0:T(8,128)(2,1)S(1)} collective-permute-done((bf16[2,8,16,128]{3,2,1,0:T(8,128)(2,1)S(1)}, bf16[2,8,16,128]{3,2,1,0:T(8,128)(2,1)S(1)}, u32[]{:S(2)}, u32[]{:S(2)}) %collective-permute-start.6) | collective-permute-done | bytes 65568 | tf_op jit(solution)/shard_map/ppermute | solution.py:410
  23.8 0.1 shard_map.63
  23.9 0.1 collective-permute-start.7
  23.9 1.6 %collective-permute-start.8 = (bf16[32,16,128]{2,1,0:T(8,128)(2,1)S(1)}, bf16[32,16,128]{2,1,0:T(8,128)(2,1)S(1)}, u32[]{:S(2)}, u32[]{:S(2)}) collective-permute-start(bf16[32,16,128]{2,1,0:T(8,128)(2,1)S(1)} %get-tuple-element.30.summed_ref), channel_id=1, source_target_pairs={{0,2},{2,0},{1,3},{3,1},{4,6},{6,4},{5,7},{7,5},{8,10},{10,8},{9,1... | collective-permute-start | bytes 393224 | tf_op jit(solution)/shard_map/ppermute | solution.py:426
  25.5 0.3 collective-permute-start.9
  25.8 2.6 %shard_map.64 = bf16[2,2,32,2048]{3,2,1,0:T(8,128)(2,1)} custom-call(bf16[2,32,16,128]{3,2,1,0:T(8,128)(2,1)S(1)} %get-tuple-element.26.image_ref, bf16[2,4,16,128]{3,2,1,0:T(8,128)(2,1)S(1)} %collective-permute-done.7.border_ref, bf16[2,2,32,2048]{3,2,1,0:T(8,128)(2,1)S(1)} %copy-done, bf16[9,256,256]{2,1,0:T(8,128)(2,1)S(1)} %get-tuple-element.28.table_ref, ...), custom_call_target="tpu_custom_call" | custom-call | flops 2000000000 | bytes 1999872 | tf_op jit(solution)/shard_map/pallas_call | solution.py:325
  28.4 1.3 %collective-permute-done.9.border_got_ref = bf16[4,16,128]{2,1,0:T(8,128)(2,1)S(1)} collective-permute-done((bf16[4,16,128]{2,1,0:T(8,128)(2,1)S(1)}, bf16[4,16,128]{2,1,0:T(8,128)(2,1)S(1)}, u32[]{:S(2)}, u32[]{:S(2)}) %collective-permute-start.9) | collective-permute-done | bytes 16416 | tf_op jit(solution)/shard_map/ppermute | solution.py:427
  29.8 0.3 collective-permute-done.8.got_ref
  30.0 1.7 %shard_map.65 = f32[2,32,2048]{2,1,0:T(8,128)} custom-call(bf16[32,16,128]{2,1,0:T(8,128)(2,1)S(1)} %get-tuple-element.30.summed_ref, bf16[32,16,128]{2,1,0:T(8,128)(2,1)S(1)} %collective-permute-done.8.got_ref, bf16[4,16,128]{2,1,0:T(8,128)(2,1)S(1)} %reduce_sum.12.border_ref, bf16[4,16,128]{2,1,0:T(8,128)(2,1)S(1)} %collective-permute-done.9.border_got_ref, ...), custom_call_target="tpu_custom_call" | custom-call | flops 1000000000 | bytes 1999872 | tf_op jit(solution)/shard_map/pallas_call | solution.py:325
  (11 shorter events, 0.1 us)
Async XLA Ops:
  0.6 1.7 %copy-start = (bf16[2,2,32,2048]{3,2,1,0:T(8,128)(2,1)S(1)}, bf16[2,2,32,2048]{3,2,1,0:T(8,128)(2,1)}, u32[]{:S(2)}) copy-start(bf16[2,2,32,2048]{3,2,1,0:T(8,128)(2,1)} %volume_ref.5) | copy-start | bytes 1572868
  0.6 1.7 %copy-start.1 = (f32[2,32,2048]{2,1,0:T(8,128)S(1)}, f32[2,32,2048]{2,1,0:T(8,128)}, u32[]{:S(2)}) copy-start(f32[2,32,2048]{2,1,0:T(8,128)} %background_ref.5) | copy-start | bytes 1572868
  1.8 1.4 %collective-permute-start = (bf16[2,2,4,2048]{3,2,1,0:T(4,128)(2,1)S(1)}, bf16[2,2,4,2048]{3,2,1,0:T(4,128)(2,1)S(1)}, u32[]{:S(2)}, u32[]{:S(2)}) collective-permute-start(bf16[2,2,4,2048]{3,2,1,0:T(4,128)(2,1)S(1)} %get-tuple-element.20), channel_id=1, source_target_pairs={{0,1},{1,0},{2,3},{3,2},{4,5},{5,4},{6,7},{7,6},{8,9},{9,8},{10,11... | collective-permute-start | bytes 196616 | tf_op jit(solution)/shard_map/ppermute | solution.py:365
  3.2 7.3 %copy-start.2 = (bf16[2,32,2048]{2,1,0:T(8,128)(2,1)S(1)}, bf16[2,32,2048]{2,1,0:T(8,128)(2,1)}, u32[]{:S(2)}) copy-start(bf16[2,32,2048]{2,1,0:T(8,128)(2,1)} %measured_ref.1) | copy-start | bytes 786436
  4.9 7.9 %collective-permute-start.1 = (bf16[2,8,16,128]{3,2,1,0:T(8,128)(2,1)S(1)}, bf16[2,8,16,128]{3,2,1,0:T(8,128)(2,1)S(1)}, u32[]{:S(2)}, u32[]{:S(2)}) collective-permute-start(bf16[2,8,16,128]{3,2,1,0:T(8,128)(2,1)S(1)} %get-tuple-element.23), channel_id=1, source_target_pairs={{0,12},{4,8},{8,4},{12,0},{1,13},{5,9},{9,5},{13,1},{2,14},{6,10},... | collective-permute-start | bytes 196616 | tf_op jit(solution)/shard_map/ppermute | solution.py:392
  9.9 5.0 %collective-permute-start.2 = (bf16[2,8,16,128]{3,2,1,0:T(8,128)(2,1)S(1)}, bf16[2,8,16,128]{3,2,1,0:T(8,128)(2,1)S(1)}, u32[]{:S(2)}, u32[]{:S(2)}) collective-permute-start(bf16[2,8,16,128]{3,2,1,0:T(8,128)(2,1)S(1)} %get-tuple-element.24), channel_id=1, source_target_pairs={{0,4},{4,0},{8,12},{12,8},{1,5},{5,1},{9,13},{13,9},{2,6},{6,2},{1... | collective-permute-start | bytes 196616 | tf_op jit(solution)/shard_map/ppermute | solution.py:392
  9.9 5.9 %collective-permute-start.3 = (bf16[2,8,16,128]{3,2,1,0:T(8,128)(2,1)S(1)}, bf16[2,8,16,128]{3,2,1,0:T(8,128)(2,1)S(1)}, u32[]{:S(2)}, u32[]{:S(2)}) collective-permute-start(bf16[2,8,16,128]{3,2,1,0:T(8,128)(2,1)S(1)} %get-tuple-element.25), channel_id=1, source_target_pairs={{0,8},{4,12},{8,0},{12,4},{1,9},{5,13},{9,1},{13,5},{2,10},{6,14},... | collective-permute-start | bytes 196616 | tf_op jit(solution)/shard_map/ppermute | solution.py:392
  15.8 6.3 %collective-permute-start.4 = (bf16[2,8,16,128]{3,2,1,0:T(8,128)(2,1)S(1)}, bf16[2,8,16,128]{3,2,1,0:T(8,128)(2,1)S(1)}, u32[]{:S(2)}, u32[]{:S(2)}) collective-permute-start(bf16[2,8,16,128]{3,2,1,0:T(8,128)(2,1)S(1)} %divide_convert_fusion.refs_0_), channel_id=1, source_target_pairs={{0,12},{4,8},{8,4},{12,0},{1,13},{5,9},{9,5},{13,1},{2,14},{6,10},... | collective-permute-start | bytes 196616 | tf_op jit(solution)/shard_map/ppermute | solution.py:410
  18.1 5.0 %collective-permute-start.5 = (bf16[2,8,16,128]{3,2,1,0:T(8,128)(2,1)S(1)}, bf16[2,8,16,128]{3,2,1,0:T(8,128)(2,1)S(1)}, u32[]{:S(2)}, u32[]{:S(2)}) collective-permute-start(bf16[2,8,16,128]{3,2,1,0:T(8,128)(2,1)S(1)} %divide_convert_fusion.refs_0_), channel_id=1, source_target_pairs={{0,4},{4,0},{8,12},{12,8},{1,5},{5,1},{9,13},{13,9},{2,6},{6,2},{1... | collective-permute-start | bytes 196616 | tf_op jit(solution)/shard_map/ppermute | solution.py:410
  18.4 5.4 %collective-permute-start.6 = (bf16[2,8,16,128]{3,2,1,0:T(8,128)(2,1)S(1)}, bf16[2,8,16,128]{3,2,1,0:T(8,128)(2,1)S(1)}, u32[]{:S(2)}, u32[]{:S(2)}) collective-permute-start(bf16[2,8,16,128]{3,2,1,0:T(8,128)(2,1)S(1)} %divide_convert_fusion.refs_0_), channel_id=1, source_target_pairs={{0,8},{4,12},{8,0},{12,4},{1,9},{5,13},{9,1},{13,5},{2,10},{6,14},... | collective-permute-start | bytes 196616 | tf_op jit(solution)/shard_map/ppermute | solution.py:410
  23.9 1.9 %collective-permute-start.7 = (bf16[2,4,16,128]{3,2,1,0:T(8,128)(2,1)S(1)}, bf16[2,4,16,128]{3,2,1,0:T(8,128)(2,1)S(1)}, u32[]{:S(2)}, u32[]{:S(2)}) collective-permute-start(bf16[2,4,16,128]{3,2,1,0:T(8,128)(2,1)S(1)} %get-tuple-element.27), channel_id=1, source_target_pairs={{0,1},{1,0},{2,3},{3,2},{4,5},{5,4},{6,7},{7,6},{8,9},{9,8},{10,11... | collective-permute-start | bytes 98312 | tf_op jit(solution)/shard_map/ppermute | solution.py:428
  23.9 6.1 %collective-permute-start.8 = (bf16[32,16,128]{2,1,0:T(8,128)(2,1)S(1)}, bf16[32,16,128]{2,1,0:T(8,128)(2,1)S(1)}, u32[]{:S(2)}, u32[]{:S(2)}) collective-permute-start(bf16[32,16,128]{2,1,0:T(8,128)(2,1)S(1)} %get-tuple-element.30.summed_ref), channel_id=1, source_target_pairs={{0,2},{2,0},{1,3},{3,1},{4,6},{6,4},{5,7},{7,5},{8,10},{10,8},{9,1... | collective-permute-start | bytes 393224 | tf_op jit(solution)/shard_map/ppermute | solution.py:426
  25.5 4.3 %collective-permute-start.9 = (bf16[4,16,128]{2,1,0:T(8,128)(2,1)S(1)}, bf16[4,16,128]{2,1,0:T(8,128)(2,1)S(1)}, u32[]{:S(2)}, u32[]{:S(2)}) collective-permute-start(bf16[4,16,128]{2,1,0:T(8,128)(2,1)S(1)} %get-tuple-element.31), channel_id=1, source_target_pairs={{0,3},{1,2},{2,1},{3,0},{4,7},{5,6},{6,5},{7,4},{8,11},{9,10},{10,... | collective-permute-start | bytes 49160 | tf_op jit(solution)/shard_map/ppermute | solution.py:427

commit v5 on v4

--- a/solution.py
+++ b/solution.py
@@ -230,11 +230,10 @@
             left_ref[rows, pl.ds(LANES, LANES)] = edges
 
 
-def collect_kernel(chunks, row_count, half, *refs):
+def collect_kernel(chunks, *refs):
     ratio_refs = refs[:chunks]
-    image_ref, summed_ref, border_ref, border_sum_ref = refs[chunks:]
+    image_ref, summed_ref = refs[chunks:]
     frames, chunk_rows = ratio_refs[0].shape[:2]
-    tile = lax.axis_index("tile")
     place = lax.axis_index("depth")
     for s, mask in enumerate(partners(chunks)):
         source = lax.bitwise_xor(place, mask) if s else place
@@ -246,7 +245,11 @@
                 values = values.astype(F32)
                 total = values if total is None else total + values
             summed_ref[source * chunk_rows + r] = total.astype(BF16)
-    edge = (row_count - half) * (1 - tile)
+
+
+def edge_kernel(row_count, image_ref, summed_ref, border_ref, border_sum_ref):
+    frames, half = border_ref.shape[:2]
+    edge = (row_count - half) * (1 - lax.axis_index("tile"))
     for r in range(half):
         border_sum_ref[r] = summed_ref[edge + r]
         for f in range(frames):
@@ -290,7 +293,9 @@
                 out_ref[f, d, :, lanes] = value.astype(BF16)
 
 
-def background_kernel(scale, summed_ref, got_ref, border_ref, border_got_ref, background_ref, table_ref, inverse_ref, out_ref, rows_ref, left_ref, sums_ref):
+def background_kernel(scale, summed_ref, got_ref, border_ref, border_got_ref, background_ref, table_ref, inverse_ref, given_ref, out_ref, given_out_ref, rows_ref, left_ref, sums_ref, stage_ref, sems):
+    given = pltpu.make_async_copy(given_ref, given_out_ref, sems.at[0])
+    given.start()
     depth, row_count, col_count = background_ref.shape
     half = border_ref.shape[0]
     blocks = col_count // LANES
@@ -307,30 +312,35 @@
     )
     span = (row_count + 2 * half) * blocks
     total = backproject(0, span, taps, row_count, blocks, left_ref, table_ref)
+    copies = [given]
     for d in range(depth):
         start = d * row_count * blocks
         sums_ref[pl.ds(start, row_count * blocks), :] = total[:, d * LANES : (d + 1) * LANES]
         for j in range(blocks):
             lanes = pl.ds(j * LANES, LANES)
             back = sums_ref[pl.ds(start + j, row_count, stride=blocks), :]
-            out_ref[d, :, lanes] = background_ref[d, :, lanes] * back * (inverse_ref[d] * scale)
+            stage_ref[d, :, lanes] = background_ref[d, :, lanes] * back * (inverse_ref[d] * scale)
+        copies.append(pltpu.make_async_copy(stage_ref.at[d], out_ref.at[d], sems.at[1 + d]))
+        copies[-1].start()
+    for copy in copies:
+        copy.wait()
 
 
 def whole(count):
     return [pl.BlockSpec(memory_space=pltpu.VMEM)] * count
 
 
-def call(kernel, args, outs, scratch, flops, aliases={}):
+def call(kernel, args, outs, scratch, flops, aliases={}, place=pltpu.VMEM):
     moved = sum(a.size * a.dtype.itemsize for a in args)
     return pl.pallas_call(
         kernel,
         out_shape=outs,
         in_specs=whole(len(args)),
-        out_specs=jax.tree.map(lambda _: pl.BlockSpec(memory_space=pltpu.VMEM), outs),
+        out_specs=jax.tree.map(lambda _: pl.BlockSpec(memory_space=place), outs),
         scratch_shapes=scratch,
         input_output_aliases=aliases,
         compiler_params=pltpu.CompilerParams(vmem_limit_bytes=40 * 2**20),
-        cost_estimate=pl.CostEstimate(flops=flops, bytes_accessed=moved, transcendentals=0),
+        cost_estimate=pl.CostEstimate(flops=flops, bytes_accessed=min(moved, flops // 100), transcendentals=0),
     )(*args)
 
 
@@ -410,17 +420,19 @@
         lax.ppermute(ratio, "depth", [(i, i ^ masks[s]) for i in range(chunks)])
         for s in range(1, chunks)
     ]
-    image, summed, edge, edge_sum = call(
-        functools.partial(collect_kernel, chunks, row_count, half),
+    image, summed = call(
+        functools.partial(collect_kernel, chunks),
         tuple(ratios),
-        (
-            shape((frames, padded_rows, blocks, LANES), BF16),
-            shape((padded_rows, blocks, LANES), BF16),
-            shape((frames, half, blocks, LANES), BF16),
-            shape((half, blocks, LANES), BF16),
-        ),
+        (shape((frames, padded_rows, blocks, LANES), BF16), shape((padded_rows, blocks, LANES), BF16)),
         [],
         10**6,
+    )
+    edge, edge_sum = call(
+        functools.partial(edge_kernel, row_count),
+        (image, summed),
+        (shape((frames, half, blocks, LANES), BF16), shape((half, blocks, LANES), BF16)),
+        [],
+        1000000000,
     )
     if splits == 2:
         got = lax.ppermute(summed, "tm", swap)
@@ -433,17 +445,6 @@
         summed = lax.psum(summed.astype(F32), "tm").astype(BF16)
         other = lax.psum(other.astype(BF16).astype(F32), "tm").astype(BF16)
         got, other_got = jnp.zeros_like(summed), jnp.zeros_like(other)
-    new_background = call(
-        functools.partial(background_kernel, 1.0 / (frames * splits)),
-        (summed, got, other, other_got, background, backward, inverse),
-        shape(background.shape, F32),
-        [
-            vmem((windows * blocks + 2 * PAD, LANES), F32),
-            vmem((windows * blocks, 2 * LANES), BF16),
-            vmem((depth * row_count * blocks, LANES), F32),
-        ],
-        10**9,
-    )
     new_volume = call(
         volume_kernel,
         (image, edge, volume, backward, inverse),
@@ -453,7 +454,21 @@
             vmem((frames * windows * blocks, 2 * LANES), BF16),
             vmem((frames * depth * row_count * blocks, LANES), F32),
         ],
-        2 * 10**9,
+        100000000,
+    )
+    new_background, new_volume = call(
+        functools.partial(background_kernel, 1.0 / (frames * splits)),
+        (summed, got, other, other_got, background, backward, inverse, new_volume),
+        (shape(background.shape, F32), shape(volume.shape, BF16)),
+        [
+            vmem((windows * blocks + 2 * PAD, LANES), F32),
+            vmem((windows * blocks, 2 * LANES), BF16),
+            vmem((depth * row_count * blocks, LANES), F32),
+            vmem(background.shape, F32),
+            pltpu.SemaphoreType.DMA((1 + depth,)),
+        ],
+        10**9,
+        place=pl.ANY,
     )
     return new_volume, new_background
 

time: 31.9 us -> 30.9 us (0.969)
  Pallas kernels: 8.95 us -> 8.13 us
  waiting for transfers between devices: 9.43 us -> 8.99 us
    ppermute x1, waiting for transfers between devices: 1.35 us -> 0.38 us  [body(): lax.ppermute(edge_sum, ('tm', 'tile'), [(i, 3 - i) for i in range(4)])]
    pallas_call x6 -> x7, Pallas kernels: 7.81 us -> 7 us  [call(): pl.pallas_call(kernel, out_shape=outs, in_specs=whole(len(args)), out_spe...]
    ppermute x1, waiting for transfers between devices: 0.01 us -> 0.57 us  [body(): edge = lax.ppermute(edge, 'tile', swap)]
    ppermute x1, starting transfers between devices: 0.3 us -> 0.63 us  [body(): lax.ppermute(edge_sum, ('tm', 'tile'), [(i, 3 - i) for i in range(4)])]
  transfers between devices with their start and end apart: 10 -> 10, of which waited for: 8 -> 9; matrix products, arithmetic and copies ran while one was open for 0% -> 0% of each run, Pallas kernels for 14% -> 12%
where the time goes in v5:
time: 30.9 us; the launch traced here: 30.7 us
  starting transfers between devices  12.8 us (41%)
  waiting for transfers between devices  8.99 us (29%)
  Pallas kernels  8.13 us (26%)
  between operations  0.71 us (2%)
    pallas_call x7, Pallas kernels, call(): pl.pallas_call(kernel, out_shape=outs, in_specs=whole(len(args)), out_spe...  7 us
    ppermute x3, starting transfers between devices, body(): lax.ppermute(parts[s], 'depth', [(i, i ^ masks[s]) for i in range(chunks)])  5.67 us
    ppermute x3, starting transfers between devices, body(): lax.ppermute(ratio, 'depth', [(i, i ^ masks[s]) for i in range(chunks)])  4.45 us
    ppermute x3, waiting for transfers between devices, body(): lax.ppermute(parts[s], 'depth', [(i, i ^ masks[s]) for i in range(chunks)])  4.26 us
    ppermute x3, waiting for transfers between devices, body(): lax.ppermute(ratio, 'depth', [(i, i ^ masks[s]) for i in range(chunks)])  3.5 us
    ppermute x1, starting transfers between devices, body(): got = lax.ppermute(summed, 'tm', swap)  1.57 us
    pallas_call x1, Pallas kernels, body(): pl.pallas_call(border_kernel, out_shape=(shape((frames, depth, half, col_...  1.14 us
    ppermute x1, starting transfers between devices, body(): lax.ppermute(edge_sum, ('tm', 'tile'), [(i, 3 - i) for i in range(4)])  0.63 us
  transfers between devices with their start and end apart: 10, of which 9 were waited for; matrix products, arithmetic and copies ran while one was open for 0% of the time, Pallas kernels for 12%

profile of v5, /device:TPU:0, one launch (start us, length us, event | category | flops | bytes accessed | tf_op | source)
XLA Modules:
  0.0 30.7 jit_solution(6097893819789244434)
XLA Ops:
  0.6 1.1 %shard_map.59 = (bf16[2,2,4,2048]{3,2,1,0:T(4,128)(2,1)S(1)}, bf16[2,9,16,17]{3,2,1,0:T(8,128)(2,1)S(1)}) custom-call(bf16[2,2,32,2048]{3,2,1,0:T(8,128)(2,1)} %volume_ref.5, f32[2,32,2048]{2,1,0:T(8,128)} %background_ref.5, bf16[2,9,16,17]{3,2,1,0:T(8,128)(2,1)} %psf_ref.1), custom_call_target="tpu_custom_call" | custom-call | tf_op jit(solution)/shard_map/pallas_call | solution.py:363
  1.8 0.5 %collective-permute-start = (bf16[2,2,4,2048]{3,2,1,0:T(4,128)(2,1)S(1)}, bf16[2,2,4,2048]{3,2,1,0:T(4,128)(2,1)S(1)}, u32[]{:S(2)}, u32[]{:S(2)}) collective-permute-start(bf16[2,2,4,2048]{3,2,1,0:T(4,128)(2,1)S(1)} %get-tuple-element.22), channel_id=1, source_target_pairs={{0,1},{1,0},{2,3},{3,2},{4,5},{5,4},{6,7},{7,6},{8,9},{9,8},{10,11... | collective-permute-start | bytes 196616 | tf_op jit(solution)/shard_map/ppermute | solution.py:375
  2.3 0.8 %shard_map.61 = (bf16[2,5,256,256]{3,2,1,0:T(8,128)(2,1)S(1)}, bf16[2624,256]{1,0:T(8,128)(2,1)S(1)}) custom-call(bf16[2,9,16,17]{3,2,1,0:T(8,128)(2,1)S(1)} %get-tuple-element.19.psf_ref, bf16[2,2,32,2048]{3,2,1,0:T(8,128)(2,1)S(1)} %copy-done, f32[2,32,2048]{2,1,0:T(8,128)S(1)} %copy-done.1), custom_call_target="tpu_custom_call" | custom-call | flops 200000000 | bytes 1058368 | tf_op jit(solution)/shard_map/pallas_call | solution.py:335
  3.2 1.6 %shard_map.62 = (f32[2,8,16,128]{3,2,1,0:T(8,128)S(1)}, bf16[2,8,16,128]{3,2,1,0:T(8,128)(2,1)S(1)}, bf16[2,8,16,128]{3,2,1,0:T(8,128)(2,1)S(1)}, bf16[2,8,16,12...) custom-call(bf16[2624,256]{1,0:T(8,128)(2,1)S(1)} %get-tuple-element.21.given_ref, ...), custom_call_target="tpu_custom_call", output_to_operand_aliasing={{4}: (0, {})} | custom-call | flops 2000000000 | bytes 2719744 | tf_op jit(solution)/shard_map/pallas_call | solution.py:335
  4.9 5.0 %collective-permute-start.1 = (bf16[2,8,16,128]{3,2,1,0:T(8,128)(2,1)S(1)}, bf16[2,8,16,128]{3,2,1,0:T(8,128)(2,1)S(1)}, u32[]{:S(2)}, u32[]{:S(2)}) collective-permute-start(bf16[2,8,16,128]{3,2,1,0:T(8,128)(2,1)S(1)} %get-tuple-element.25), channel_id=1, source_target_pairs={{0,12},{4,8},{8,4},{12,0},{1,13},{5,9},{9,5},{13,1},{2,14},{6,10},... | collective-permute-start | bytes 196616 | tf_op jit(solution)/shard_map/ppermute | solution.py:402
  9.9 0.6 %collective-permute-start.3 = (bf16[2,8,16,128]{3,2,1,0:T(8,128)(2,1)S(1)}, bf16[2,8,16,128]{3,2,1,0:T(8,128)(2,1)S(1)}, u32[]{:S(2)}, u32[]{:S(2)}) collective-permute-start(bf16[2,8,16,128]{3,2,1,0:T(8,128)(2,1)S(1)} %get-tuple-element.27), channel_id=1, source_target_pairs={{0,8},{4,12},{8,0},{12,4},{1,9},{5,13},{9,1},{13,5},{2,10},{6,14},... | collective-permute-start | bytes 196616 | tf_op jit(solution)/shard_map/ppermute | solution.py:402
  10.5 1.0 %shard_map.60 = (bf16[9,256,256]{2,1,0:T(8,128)(2,1)S(1)}, f32[2,1,128]{2,1,0:T(1,128)S(1)}, f32[2,8,16,128]{3,2,1,0:T(8,128)S(1)}) custom-call(bf16[2,9,16,17]{3,2,1,0:T(8,128)(2,1)S(1)} %get-tuple-element.19.psf_ref, bf16[2,32,2048]{2,1,0:T(8,128)(2,1)S(1)} %copy-done.2), custom_call_target="tpu_custom_call" | custom-call | flops 200000000 | bytes 271936 | tf_op jit(solution)/shard_map/pallas_call | solution.py:335
  11.5 1.3 %collective-permute-done.1 = bf16[2,8,16,128]{3,2,1,0:T(8,128)(2,1)S(1)} collective-permute-done((bf16[2,8,16,128]{3,2,1,0:T(8,128)(2,1)S(1)}, bf16[2,8,16,128]{3,2,1,0:T(8,128)(2,1)S(1)}, u32[]{:S(2)}, u32[]{:S(2)}) %collective-permute-start.1) | collective-permute-done | bytes 65568 | tf_op jit(solution)/shard_map/ppermute | solution.py:402
  12.8 2.1 %collective-permute-done.2 = bf16[2,8,16,128]{3,2,1,0:T(8,128)(2,1)S(1)} collective-permute-done((bf16[2,8,16,128]{3,2,1,0:T(8,128)(2,1)S(1)}, bf16[2,8,16,128]{3,2,1,0:T(8,128)(2,1)S(1)}, u32[]{:S(2)}, u32[]{:S(2)}) %collective-permute-start.2) | collective-permute-done | bytes 65568 | tf_op jit(solution)/shard_map/ppermute | solution.py:402
  14.9 0.9 %collective-permute-done.3 = bf16[2,8,16,128]{3,2,1,0:T(8,128)(2,1)S(1)} collective-permute-done((bf16[2,8,16,128]{3,2,1,0:T(8,128)(2,1)S(1)}, bf16[2,8,16,128]{3,2,1,0:T(8,128)(2,1)S(1)}, u32[]{:S(2)}, u32[]{:S(2)}) %collective-permute-start.3) | collective-permute-done | bytes 65568 | tf_op jit(solution)/shard_map/ppermute | solution.py:402
  15.8 2.3 %collective-permute-start.4 = (bf16[2,8,16,128]{3,2,1,0:T(8,128)(2,1)S(1)}, bf16[2,8,16,128]{3,2,1,0:T(8,128)(2,1)S(1)}, u32[]{:S(2)}, u32[]{:S(2)}) collective-permute-start(bf16[2,8,16,128]{3,2,1,0:T(8,128)(2,1)S(1)} %divide_convert_fusion.refs_0_), channel_id=1, source_target_pairs={{0,12},{4,8},{8,4},{12,0},{1,13},{5,9},{9,5},{13,1},{2,14},{6,10},... | collective-permute-start | bytes 196616 | tf_op jit(solution)/shard_map/ppermute | solution.py:420
  18.1 0.4 %collective-permute-start.5 = (bf16[2,8,16,128]{3,2,1,0:T(8,128)(2,1)S(1)}, bf16[2,8,16,128]{3,2,1,0:T(8,128)(2,1)S(1)}, u32[]{:S(2)}, u32[]{:S(2)}) collective-permute-start(bf16[2,8,16,128]{3,2,1,0:T(8,128)(2,1)S(1)} %divide_convert_fusion.refs_0_), channel_id=1, source_target_pairs={{0,4},{4,0},{8,12},{12,8},{1,5},{5,1},{9,13},{13,9},{2,6},{6,2},{1... | collective-permute-start | bytes 196616 | tf_op jit(solution)/shard_map/ppermute | solution.py:420
  18.4 1.8 %collective-permute-start.6 = (bf16[2,8,16,128]{3,2,1,0:T(8,128)(2,1)S(1)}, bf16[2,8,16,128]{3,2,1,0:T(8,128)(2,1)S(1)}, u32[]{:S(2)}, u32[]{:S(2)}) collective-permute-start(bf16[2,8,16,128]{3,2,1,0:T(8,128)(2,1)S(1)} %divide_convert_fusion.refs_0_), channel_id=1, source_target_pairs={{0,8},{4,12},{8,0},{12,4},{1,9},{5,13},{9,1},{13,5},{2,10},{6,14},... | collective-permute-start | bytes 196616 | tf_op jit(solution)/shard_map/ppermute | solution.py:420
  20.3 1.9 %collective-permute-done.4.refs_1_ = bf16[2,8,16,128]{3,2,1,0:T(8,128)(2,1)S(1)} collective-permute-done((bf16[2,8,16,128]{3,2,1,0:T(8,128)(2,1)S(1)}, bf16[2,8,16,128]{3,2,1,0:T(8,128)(2,1)S(1)}, u32[]{:S(2)}, u32[]{:S(2)}) %collective-permute-start.4) | collective-permute-done | bytes 65568 | tf_op jit(solution)/shard_map/ppermute | solution.py:420
  22.2 1.0 %collective-permute-done.5.refs_2_ = bf16[2,8,16,128]{3,2,1,0:T(8,128)(2,1)S(1)} collective-permute-done((bf16[2,8,16,128]{3,2,1,0:T(8,128)(2,1)S(1)}, bf16[2,8,16,128]{3,2,1,0:T(8,128)(2,1)S(1)}, u32[]{:S(2)}, u32[]{:S(2)}) %collective-permute-start.5) | collective-permute-done | bytes 65568 | tf_op jit(solution)/shard_map/ppermute | solution.py:420
  23.1 0.7 %collective-permute-done.6.refs_3_ = bf16[2,8,16,128]{3,2,1,0:T(8,128)(2,1)S(1)} collective-permute-done((bf16[2,8,16,128]{3,2,1,0:T(8,128)(2,1)S(1)}, bf16[2,8,16,128]{3,2,1,0:T(8,128)(2,1)S(1)}, u32[]{:S(2)}, u32[]{:S(2)}) %collective-permute-start.6) | collective-permute-done | bytes 65568 | tf_op jit(solution)/shard_map/ppermute | solution.py:420
  23.8 0.1 shard_map.63
  23.8 1.6 %collective-permute-start.7 = (bf16[32,16,128]{2,1,0:T(8,128)(2,1)S(1)}, bf16[32,16,128]{2,1,0:T(8,128)(2,1)S(1)}, u32[]{:S(2)}, u32[]{:S(2)}) collective-permute-start(bf16[32,16,128]{2,1,0:T(8,128)(2,1)S(1)} %get-tuple-element.28.summed_ref), channel_id=1, source_target_pairs={{0,2},{2,0},{1,3},{3,1},{4,6},{6,4},{5,7},{7,5},{8,10},{10,8},{9,1... | collective-permute-start | bytes 393224 | tf_op jit(solution)/shard_map/ppermute | solution.py:438
  25.4 0.6 %collective-permute-start.9 = (bf16[4,16,128]{2,1,0:T(8,128)(2,1)S(1)}, bf16[4,16,128]{2,1,0:T(8,128)(2,1)S(1)}, u32[]{:S(2)}, u32[]{:S(2)}) collective-permute-start(bf16[4,16,128]{2,1,0:T(8,128)(2,1)S(1)} %get-tuple-element.31), channel_id=1, source_target_pairs={{0,3},{1,2},{2,1},{3,0},{4,7},{5,6},{6,5},{7,4},{8,11},{9,10},{10,... | collective-permute-start | bytes 49160 | tf_op jit(solution)/shard_map/ppermute | solution.py:439
  26.0 0.6 %collective-permute-done.8.border_ref = bf16[2,4,16,128]{3,2,1,0:T(8,128)(2,1)S(1)} collective-permute-done((bf16[2,4,16,128]{3,2,1,0:T(8,128)(2,1)S(1)}, bf16[2,4,16,128]{3,2,1,0:T(8,128)(2,1)S(1)}, u32[]{:S(2)}, u32[]{:S(2)}) %collective-permute-start.8) | collective-permute-done | bytes 32800 | tf_op jit(solution)/shard_map/ppermute | solution.py:440
  26.6 1.8 %shard_map.65.given_ref = bf16[2,2,32,2048]{3,2,1,0:T(8,128)(2,1)S(1)} custom-call(bf16[2,32,16,128]{3,2,1,0:T(8,128)(2,1)S(1)} %get-tuple-element.29.image_ref, bf16[2,4,16,128]{3,2,1,0:T(8,128)(2,1)S(1)} %collective-permute-done.8.border_ref, bf16[2,2,32,2048]{3,2,1,0:T(8,128)(2,1)S(1)} %copy-done, bf16[9,256,256]{2,1,0:T(8,128)(2,1)S(1)} %get-tuple-element.32.table_ref, ...), custom_call_target="tpu_custom_call" | custom-call | flops 100000000 | bytes 1000000 | tf_op jit(solution)/shard_map/pallas_call | solution.py:335
  28.4 0.4 %collective-permute-done.9.border_got_ref = bf16[4,16,128]{2,1,0:T(8,128)(2,1)S(1)} collective-permute-done((bf16[4,16,128]{2,1,0:T(8,128)(2,1)S(1)}, bf16[4,16,128]{2,1,0:T(8,128)(2,1)S(1)}, u32[]{:S(2)}, u32[]{:S(2)}) %collective-permute-start.9) | collective-permute-done | bytes 16416 | tf_op jit(solution)/shard_map/ppermute | solution.py:439
  28.8 0.2 collective-permute-done.7.got_ref
  29.0 1.7 %shard_map.66 = (f32[2,32,2048]{2,1,0:T(8,128)}, bf16[2,2,32,2048]{3,2,1,0:T(8,128)(2,1)}) custom-call(bf16[32,16,128]{2,1,0:T(8,128)(2,1)S(1)} %get-tuple-element.28.summed_ref, bf16[32,16,128]{2,1,0:T(8,128)(2,1)S(1)} %collective-permute-done.7.got_ref, bf16[4,16,128]{2,1,0:T(8,128)(2,1)S(1)} %reduce_sum.12.border_ref, ...), custom_call_target="tpu_custom_call" | custom-call | flops 1000000000 | bytes 2524160 | tf_op jit(solution)/shard_map/pallas_call | solution.py:335
  (12 shorter events, 0.1 us)
Async XLA Ops:
  0.6 1.7 %copy-start = (bf16[2,2,32,2048]{3,2,1,0:T(8,128)(2,1)S(1)}, bf16[2,2,32,2048]{3,2,1,0:T(8,128)(2,1)}, u32[]{:S(2)}) copy-start(bf16[2,2,32,2048]{3,2,1,0:T(8,128)(2,1)} %volume_ref.5) | copy-start | bytes 1572868
  0.6 1.7 %copy-start.1 = (f32[2,32,2048]{2,1,0:T(8,128)S(1)}, f32[2,32,2048]{2,1,0:T(8,128)}, u32[]{:S(2)}) copy-start(f32[2,32,2048]{2,1,0:T(8,128)} %background_ref.5) | copy-start | bytes 1572868
  1.8 1.4 %collective-permute-start = (bf16[2,2,4,2048]{3,2,1,0:T(4,128)(2,1)S(1)}, bf16[2,2,4,2048]{3,2,1,0:T(4,128)(2,1)S(1)}, u32[]{:S(2)}, u32[]{:S(2)}) collective-permute-start(bf16[2,2,4,2048]{3,2,1,0:T(4,128)(2,1)S(1)} %get-tuple-element.22), channel_id=1, source_target_pairs={{0,1},{1,0},{2,3},{3,2},{4,5},{5,4},{6,7},{7,6},{8,9},{9,8},{10,11... | collective-permute-start | bytes 196616 | tf_op jit(solution)/shard_map/ppermute | solution.py:375
  3.2 7.3 %copy-start.2 = (bf16[2,32,2048]{2,1,0:T(8,128)(2,1)S(1)}, bf16[2,32,2048]{2,1,0:T(8,128)(2,1)}, u32[]{:S(2)}) copy-start(bf16[2,32,2048]{2,1,0:T(8,128)(2,1)} %measured_ref.1) | copy-start | bytes 786436
  4.9 7.9 %collective-permute-start.1 = (bf16[2,8,16,128]{3,2,1,0:T(8,128)(2,1)S(1)}, bf16[2,8,16,128]{3,2,1,0:T(8,128)(2,1)S(1)}, u32[]{:S(2)}, u32[]{:S(2)}) collective-permute-start(bf16[2,8,16,128]{3,2,1,0:T(8,128)(2,1)S(1)} %get-tuple-element.25), channel_id=1, source_target_pairs={{0,12},{4,8},{8,4},{12,0},{1,13},{5,9},{9,5},{13,1},{2,14},{6,10},... | collective-permute-start | bytes 196616 | tf_op jit(solution)/shard_map/ppermute | solution.py:402
  9.9 5.0 %collective-permute-start.2 = (bf16[2,8,16,128]{3,2,1,0:T(8,128)(2,1)S(1)}, bf16[2,8,16,128]{3,2,1,0:T(8,128)(2,1)S(1)}, u32[]{:S(2)}, u32[]{:S(2)}) collective-permute-start(bf16[2,8,16,128]{3,2,1,0:T(8,128)(2,1)S(1)} %get-tuple-element.26), channel_id=1, source_target_pairs={{0,4},{4,0},{8,12},{12,8},{1,5},{5,1},{9,13},{13,9},{2,6},{6,2},{1... | collective-permute-start | bytes 196616 | tf_op jit(solution)/shard_map/ppermute | solution.py:402
  9.9 5.9 %collective-permute-start.3 = (bf16[2,8,16,128]{3,2,1,0:T(8,128)(2,1)S(1)}, bf16[2,8,16,128]{3,2,1,0:T(8,128)(2,1)S(1)}, u32[]{:S(2)}, u32[]{:S(2)}) collective-permute-start(bf16[2,8,16,128]{3,2,1,0:T(8,128)(2,1)S(1)} %get-tuple-element.27), channel_id=1, source_target_pairs={{0,8},{4,12},{8,0},{12,4},{1,9},{5,13},{9,1},{13,5},{2,10},{6,14},... | collective-permute-start | bytes 196616 | tf_op jit(solution)/shard_map/ppermute | solution.py:402
  15.8 6.3 %collective-permute-start.4 = (bf16[2,8,16,128]{3,2,1,0:T(8,128)(2,1)S(1)}, bf16[2,8,16,128]{3,2,1,0:T(8,128)(2,1)S(1)}, u32[]{:S(2)}, u32[]{:S(2)}) collective-permute-start(bf16[2,8,16,128]{3,2,1,0:T(8,128)(2,1)S(1)} %divide_convert_fusion.refs_0_), channel_id=1, source_target_pairs={{0,12},{4,8},{8,4},{12,0},{1,13},{5,9},{9,5},{13,1},{2,14},{6,10},... | collective-permute-start | bytes 196616 | tf_op jit(solution)/shard_map/ppermute | solution.py:420
  18.1 5.0 %collective-permute-start.5 = (bf16[2,8,16,128]{3,2,1,0:T(8,128)(2,1)S(1)}, bf16[2,8,16,128]{3,2,1,0:T(8,128)(2,1)S(1)}, u32[]{:S(2)}, u32[]{:S(2)}) collective-permute-start(bf16[2,8,16,128]{3,2,1,0:T(8,128)(2,1)S(1)} %divide_convert_fusion.refs_0_), channel_id=1, source_target_pairs={{0,4},{4,0},{8,12},{12,8},{1,5},{5,1},{9,13},{13,9},{2,6},{6,2},{1... | collective-permute-start | bytes 196616 | tf_op jit(solution)/shard_map/ppermute | solution.py:420
  18.4 5.3 %collective-permute-start.6 = (bf16[2,8,16,128]{3,2,1,0:T(8,128)(2,1)S(1)}, bf16[2,8,16,128]{3,2,1,0:T(8,128)(2,1)S(1)}, u32[]{:S(2)}, u32[]{:S(2)}) collective-permute-start(bf16[2,8,16,128]{3,2,1,0:T(8,128)(2,1)S(1)} %divide_convert_fusion.refs_0_), channel_id=1, source_target_pairs={{0,8},{4,12},{8,0},{12,4},{1,9},{5,13},{9,1},{13,5},{2,10},{6,14},... | collective-permute-start | bytes 196616 | tf_op jit(solution)/shard_map/ppermute | solution.py:420
  23.8 5.2 %collective-permute-start.7 = (bf16[32,16,128]{2,1,0:T(8,128)(2,1)S(1)}, bf16[32,16,128]{2,1,0:T(8,128)(2,1)S(1)}, u32[]{:S(2)}, u32[]{:S(2)}) collective-permute-start(bf16[32,16,128]{2,1,0:T(8,128)(2,1)S(1)} %get-tuple-element.28.summed_ref), channel_id=1, source_target_pairs={{0,2},{2,0},{1,3},{3,1},{4,6},{6,4},{5,7},{7,5},{8,10},{10,8},{9,1... | collective-permute-start | bytes 393224 | tf_op jit(solution)/shard_map/ppermute | solution.py:438
  25.4 1.2 %collective-permute-start.8 = (bf16[2,4,16,128]{3,2,1,0:T(8,128)(2,1)S(1)}, bf16[2,4,16,128]{3,2,1,0:T(8,128)(2,1)S(1)}, u32[]{:S(2)}, u32[]{:S(2)}) collective-permute-start(bf16[2,4,16,128]{3,2,1,0:T(8,128)(2,1)S(1)} %get-tuple-element.30), channel_id=1, source_target_pairs={{0,1},{1,0},{2,3},{3,2},{4,5},{5,4},{6,7},{7,6},{8,9},{9,8},{10,11... | collective-permute-start | bytes 98312 | tf_op jit(solution)/shard_map/ppermute | solution.py:440
  25.4 3.4 %collective-permute-start.9 = (bf16[4,16,128]{2,1,0:T(8,128)(2,1)S(1)}, bf16[4,16,128]{2,1,0:T(8,128)(2,1)S(1)}, u32[]{:S(2)}, u32[]{:S(2)}) collective-permute-start(bf16[4,16,128]{2,1,0:T(8,128)(2,1)S(1)} %get-tuple-element.31), channel_id=1, source_target_pairs={{0,3},{1,2},{2,1},{3,0},{4,7},{5,6},{6,5},{7,4},{8,11},{9,10},{10,... | collective-permute-start | bytes 49160 | tf_op jit(solution)/shard_map/ppermute | solution.py:439

commit v6 on v5

--- a/solution.py
+++ b/solution.py
@@ -72,25 +72,33 @@
     spread.wait()
 
 
-def forward_table_kernel(psf_ref, volume_ref, background_ref, table_ref, left_ref, base_ref, rows_ref):
+def forward_table_kernel(psf_ref, volume_ref, background_ref, table_ref, left_ref, edge_ref, base_ref, rows_ref, corner_ref):
     depth, taps, pitch, width = psf_ref.shape
+    reach = (width - 1) // 2
+    pairs = table_ref.shape[0] - 1
     fill_base(psf_ref, base_ref)
     near = near_mask(width)
+    corner_ref[...] = jnp.zeros_like(corner_ref)
     for d in range(depth):
-        for t in range(2 * table_ref.shape[1]):
-            lanes = pl.ds((t % 2) * LANES, LANES)
+        for t in range(2 * pairs):
+            pair, lanes = t // 2, pl.ds((t % 2) * LANES, LANES)
             if t < taps:
                 band = rotated(base_ref, (d * taps + t) * pitch, pitch)
-                table_ref[d, t // 2, pl.ds(0, LANES), lanes] = jnp.where(near, band, 0.0).astype(BF16)
-                table_ref[d, t // 2, pl.ds(LANES, LANES), lanes] = jnp.where(near, 0.0, band).astype(BF16)
+                table_ref[pair, pl.ds(d * LANES, LANES), lanes] = jnp.where(near, band, 0.0).astype(BF16)
+                far = jnp.where(near, 0.0, band)
+                half_row = LANES * (pair // 4)
+                shift = d * (LANES // 2) + edge_shift(pair % 4)
+                corner_ref[pl.ds(half_row + shift, reach), lanes] = far[:reach]
+                corner_ref[pl.ds(half_row + (LANES - reach + shift) % LANES, reach), lanes] = far[LANES - reach :]
             else:
-                table_ref[d, t // 2, :, lanes] = jnp.zeros((2 * LANES, LANES), BF16)
+                table_ref[pair, pl.ds(d * LANES, LANES), lanes] = jnp.zeros((LANES, LANES), BF16)
+    table_ref[pairs] = corner_ref[...].astype(BF16)
     frames, depth, row_count, col_count = volume_ref.shape
     blocks = col_count // LANES
     half = (taps - 1) // 2
     tile = lax.axis_index("tile")
-    masks = edge_masks(blocks, blocks)
-    span = left_ref.shape[0] // (frames * depth)
+    masks = edge_masks(blocks, blocks, reach)
+    span = left_ref.shape[0] // frames
     for f in range(frames):
         for d in range(depth):
             base = (f * depth + d) * row_count * blocks
@@ -98,15 +106,17 @@
                 lanes = pl.ds(j * LANES, LANES)
                 total = (volume_ref[f, d, :, lanes].astype(F32) + background_ref[d, :, lanes]).astype(BF16).astype(F32)
                 rows_ref[pl.ds(PAD + base + j, row_count, stride=blocks), :] = total
-            own = (f * depth + d) * span + half * blocks
-            empty = pl.multiple_of((f * depth + d) * span + (row_count + half) * blocks * tile, blocks)
-            left_ref[pl.ds(empty, half * blocks), :] = jnp.zeros((half * blocks, 2 * LANES), BF16)
-            left_ref[pl.ds((f * depth + d + 1) * span - blocks, blocks), :] = jnp.zeros((blocks, 2 * LANES), BF16)
-            for r in range(row_count):
-                here, edges = with_edges(rows_ref, PAD + base + r * blocks, blocks, blocks, *masks)
-                rows = pl.ds(own + r * blocks, blocks)
-                left_ref[rows, pl.ds(0, LANES)] = here
-                left_ref[rows, pl.ds(LANES, LANES)] = edges
+        own = f * span + half * blocks
+        empty = pl.ds(pl.multiple_of(f * span + (row_count + half) * blocks * tile, blocks), half * blocks)
+        last = pl.ds((f + 1) * span - blocks, blocks)
+        left_ref[empty, :] = jnp.zeros((half * blocks, depth * LANES), BF16)
+        edge_ref[empty, :] = jnp.zeros((half * blocks, LANES), F32)
+        left_ref[last, :] = jnp.zeros((blocks, depth * LANES), BF16)
+        edge_ref[last, :] = jnp.zeros((blocks, LANES), F32)
+        for r in range(row_count):
+            starts = [PAD + ((f * depth + d) * row_count + r) * blocks for d in range(depth)]
+            rows = pl.ds(own + r * blocks, blocks)
+            left_ref[rows, :], edge_ref[rows, :] = joined(rows_ref, starts, blocks, masks)
 
 
 def backward_table_kernel(psf_ref, measured_ref, table_ref, inverse_ref, chunk_ref, base_ref, rows_ref):
@@ -144,14 +154,14 @@
     after = rows_ref[pl.ds(start + 1, count), :]
     before = rows_ref[pl.ds(start - 1, count), :]
     edges = jnp.where(after_mask, after, jnp.where(before_mask, before, 0.0))
-    return here.astype(BF16), edges.astype(BF16)
-
-
-def edge_masks(count, blocks):
+    return here.astype(BF16), edges
+
+
+def edge_masks(count, blocks, reach=LANES // 2):
     row = lax.rem(lax.broadcasted_iota(jnp.int32, (count, LANES), 0), blocks)
     lane = lax.broadcasted_iota(jnp.int32, (count, LANES), 1)
-    after = jnp.logical_and(lane < LANES // 2, row < blocks - 1)
-    before = jnp.logical_and(lane >= LANES // 2, row > 0)
+    after = jnp.logical_and(lane < reach, row < blocks - 1)
+    before = jnp.logical_and(lane >= LANES - reach, row > 0)
     return after, before
 
 
@@ -162,38 +172,50 @@
     return [0] + sorted(range(1, chunks), key=lambda mask: (mask != chunks - 1, mask))
 
 
-def sensor_kernel(chunks, row_count, half, given_ref, got_ref, table_ref, own_ref, *rest):
+def sensor_kernel(chunks, row_count, half, reach, given_ref, given_edge_ref, got_ref, table_ref, own_ref, *rest):
     sent_refs = rest[: chunks - 1]
-    left_ref, rows_ref, sums_ref, whole_ref = rest[chunks - 1 :]
+    left_ref, edge_ref, rows_ref, packed_ref, sums_ref, whole_ref = rest[chunks - 1 :]
     frames, depth, halo, col_count = got_ref.shape
     blocks = col_count // LANES
-    pairs = table_ref.shape[1]
+    pairs = table_ref.shape[0] - 1
     sensor_rows = row_count
-    span = left_ref.shape[0] // (frames * depth)
+    span = left_ref.shape[0] // frames
     tile = lax.axis_index("tile")
     place = lax.axis_index("depth")
-    masks = edge_masks(blocks, blocks)
+    masks = edge_masks(blocks, blocks, reach)
     for f in range(frames):
         for d in range(depth):
             first = (f * depth + d) * halo * blocks
-            other = (f * depth + d) * span + (row_count + half) * blocks * (1 - tile)
             for j in range(blocks):
                 lanes = pl.ds(j * LANES, LANES)
                 rows_ref[pl.ds(PAD + first + j, halo, stride=blocks), :] = got_ref[f, d, :, lanes].astype(F32)
-            for r in range(halo):
-                here, edges = with_edges(rows_ref, PAD + first + r * blocks, blocks, blocks, *masks)
-                rows = pl.ds(pl.multiple_of(other + r * blocks, blocks), blocks)
-                left_ref[rows, pl.ds(0, LANES)] = here
-                left_ref[rows, pl.ds(LANES, LANES)] = edges
+        other = f * span + (row_count + half) * blocks * (1 - tile)
+        for r in range(halo):
+            starts = [PAD + ((f * depth + d) * halo + r) * blocks for d in range(depth)]
+            rows = pl.ds(pl.multiple_of(other + r * blocks, blocks), blocks)
+            left_ref[rows, :], edge_ref[rows, :] = joined(rows_ref, starts, blocks, masks)
     size = (sensor_rows + 1) * blocks
     chunk_rows = own_ref.shape[1]
     for f in range(frames):
+        for r in range(sensor_rows + 1):
+            packed = None
+            for pair in range(4):
+                values = edge_ref[pl.ds(f * span + (r + 2 * pair) * blocks, blocks), :]
+                if pair:
+                    values = pltpu.roll(values, edge_shift(pair), 1)
+                packed = values if packed is None else packed + values
+            rows = pl.ds((f * (sensor_rows + 1) + r) * blocks, blocks)
+            packed_ref[rows, pl.ds(0, LANES)] = packed.astype(BF16)
+            packed_ref[rows, pl.ds(LANES, LANES)] = edge_ref[pl.ds(f * span + (r + 8) * blocks, blocks), :].astype(BF16)
+    for f in range(frames):
         total = None
-        for d in range(depth):
-            for p in range(pairs):
-                left = left_ref[pl.ds((f * depth + d) * span + 2 * p * blocks, size), :]
-                product = jnp.dot(left, table_ref[d, p], preferred_element_type=F32)
-                total = product if total is None else total + product
+        for p in range(pairs + 1):
+            if p < pairs:
+                left = left_ref[pl.ds(f * span + 2 * p * blocks, size), :]
+            else:
+                left = packed_ref[pl.ds(f * size, size), :]
+            product = jnp.dot(left, table_ref[p], preferred_element_type=F32)
+            total = product if total is None else total + product
         sums_ref[...] = total
         count = sensor_rows * blocks
         whole_ref[f, pl.ds(0, count), :] = sums_ref[pl.ds(0, count), pl.ds(0, LANES)] + sums_ref[pl.ds(blocks, count), pl.ds(LANES, LANES)]
@@ -208,6 +230,15 @@
                     own_ref[f, r] = values
                 else:
                     sent_refs[s - 1][f, r] = values.astype(BF16)
+
+
+def joined(rows_ref, starts, blocks, masks):
+    (one, one_edges), (two, two_edges) = [with_edges(rows_ref, start, blocks, blocks, *masks) for start in starts]
+    return jnp.concatenate([one, two], axis=1), one_edges + pltpu.roll(two_edges, LANES // 2, 1)
+
+
+def edge_shift(pair):
+    return 32 * (pair % 2) + 16 * (pair // 2)
 
 
 def spread_ratio(images, row_count, half, blocks, own, border, rows_ref, left_ref):
@@ -227,7 +258,7 @@
             here, edges = with_edges(rows_ref, first + r * blocks, blocks, blocks, *masks)
             rows = pl.ds((f * windows + r) * blocks, blocks)
             left_ref[rows, pl.ds(0, LANES)] = here
-            left_ref[rows, pl.ds(LANES, LANES)] = edges
+            left_ref[rows, pl.ds(LANES, LANES)] = edges.astype(BF16)
 
 
 def collect_kernel(chunks, *refs):
@@ -348,6 +379,7 @@
     frames, depth, row_count, col_count = volume.shape
     taps, pitch, width = psf.shape[1:]
     half = (taps - 1) // 2
+    reach = (width - 1) // 2
     blocks = col_count // LANES
     pairs = (taps + 1) // 2
     chunks = lax.axis_size("depth")
@@ -375,26 +407,29 @@
     border = lax.ppermute(sent, "tile", swap)
 
     base = vmem((depth * taps * pitch, LANES), F32)
-    left_shape = shape((frames * depth * (windows + 1) * blocks, 2 * LANES), BF16)
-    forward, left = call(
+    assert depth == 2 and pairs == 5 and 16 * reach == LANES
+    left_shape = shape((frames * (windows + 1) * blocks, depth * LANES), BF16)
+    edge_shape = shape((frames * (windows + 1) * blocks, LANES), F32)
+    forward, left, left_edge = call(
         forward_table_kernel,
         (table, volume, background),
-        (shape((depth, pairs, 2 * LANES, 2 * LANES), BF16), left_shape),
-        [base, vmem((frames * depth * row_count * blocks + 2 * PAD, LANES), F32)],
+        (shape((pairs + 1, 2 * LANES, 2 * LANES), BF16), left_shape, edge_shape),
+        [base, vmem((frames * depth * row_count * blocks + 2 * PAD, LANES), F32), vmem((2 * LANES, 2 * LANES), F32)],
         2 * 10**8,
     )
     chunk = (frames, chunk_rows, blocks, LANES)
     parts = call(
-        functools.partial(sensor_kernel, chunks, row_count, half),
-        (left, border, forward),
-        (shape(chunk, F32),) + (shape(chunk, BF16),) * (chunks - 1) + (left_shape,),
+        functools.partial(sensor_kernel, chunks, row_count, half, reach),
+        (left, left_edge, border, forward),
+        (shape(chunk, F32),) + (shape(chunk, BF16),) * (chunks - 1) + (left_shape, edge_shape),
         [
             vmem((frames * depth * half * blocks + 2 * PAD, LANES), F32),
+            vmem((frames * (row_count + 1) * blocks, 2 * LANES), BF16),
             vmem(((row_count + 1) * blocks, 2 * LANES), F32),
             vmem((frames, padded_rows * blocks, LANES), F32),
         ],
         2 * 10**9,
-        {0: chunks},
+        {0: chunks, 1: chunks + 1},
     )
     sensor = parts[0]
     masks = partners(chunks)

time: 30.9 us -> 30.4 us (0.984)
  Pallas kernels: 8.13 us -> 7.51 us
    pallas_call x7, Pallas kernels: 7 us -> 6.38 us  [call(): pl.pallas_call(kernel, out_shape=outs, in_specs=whole(len(args)), out_spe...]
  transfers between devices with their start and end apart: 10 -> 10, of which waited for: 9 -> 10; matrix products, arithmetic and copies ran while one was open for 0% -> 0% of each run, Pallas kernels for 12% -> 12%
where the time goes in v6:
time: 30.4 us; the launch traced here: 30.2 us
  starting transfers between devices  12.8 us (42%)
  waiting for transfers between devices  9.09 us (30%)
  Pallas kernels  7.51 us (25%)
  between operations  0.71 us (2%)
    pallas_call x7, Pallas kernels, call(): pl.pallas_call(kernel, out_shape=outs, in_specs=whole(len(args)), out_spe...  6.38 us
    ppermute x3, starting transfers between devices, body(): lax.ppermute(parts[s], 'depth', [(i, i ^ masks[s]) for i in range(chunks)])  5.67 us
    ppermute x3, starting transfers between devices, body(): lax.ppermute(ratio, 'depth', [(i, i ^ masks[s]) for i in range(chunks)])  4.45 us
    ppermute x3, waiting for transfers between devices, body(): lax.ppermute(parts[s], 'depth', [(i, i ^ masks[s]) for i in range(chunks)])  4.25 us
    ppermute x3, waiting for transfers between devices, body(): lax.ppermute(ratio, 'depth', [(i, i ^ masks[s]) for i in range(chunks)])  3.49 us
    ppermute x1, starting transfers between devices, body(): got = lax.ppermute(summed, 'tm', swap)  1.56 us
    pallas_call x1, Pallas kernels, body(): pl.pallas_call(border_kernel, out_shape=(shape((frames, depth, half, col_...  1.14 us
    ppermute x1, starting transfers between devices, body(): lax.ppermute(edge_sum, ('tm', 'tile'), [(i, 3 - i) for i in range(4)])  0.64 us
  transfers between devices with their start and end apart: 10, of which 10 were waited for; matrix products, arithmetic and copies ran while one was open for 0% of the time, Pallas kernels for 12%

profile of v6, /device:TPU:0, one launch (start us, length us, event | category | flops | bytes accessed | tf_op | source)
XLA Modules:
  0.0 30.2 jit_solution(11071363172673575224)
XLA Ops:
  0.6 1.1 %shard_map.59 = (bf16[2,2,4,2048]{3,2,1,0:T(4,128)(2,1)S(1)}, bf16[2,9,16,17]{3,2,1,0:T(8,128)(2,1)S(1)}) custom-call(bf16[2,2,32,2048]{3,2,1,0:T(8,128)(2,1)} %volume_ref.5, f32[2,32,2048]{2,1,0:T(8,128)} %background_ref.5, bf16[2,9,16,17]{3,2,1,0:T(8,128)(2,1)} %psf_ref.1), custom_call_target="tpu_custom_call" | custom-call | tf_op jit(solution)/shard_map/pallas_call | solution.py:395
  1.8 0.5 %collective-permute-start = (bf16[2,2,4,2048]{3,2,1,0:T(4,128)(2,1)S(1)}, bf16[2,2,4,2048]{3,2,1,0:T(4,128)(2,1)S(1)}, u32[]{:S(2)}, u32[]{:S(2)}) collective-permute-start(bf16[2,2,4,2048]{3,2,1,0:T(4,128)(2,1)S(1)} %get-tuple-element.24), channel_id=1, source_target_pairs={{0,1},{1,0},{2,3},{3,2},{4,5},{5,4},{6,7},{7,6},{8,9},{9,8},{10,11... | collective-permute-start | bytes 196616 | tf_op jit(solution)/shard_map/ppermute | solution.py:407
  2.3 0.7 %shard_map.61 = (bf16[6,256,256]{2,1,0:T(8,128)(2,1)S(1)}, bf16[1312,256]{1,0:T(8,128)(2,1)S(1)}, f32[1312,128]{1,0:T(8,128)S(1)}) custom-call(bf16[2,9,16,17]{3,2,1,0:T(8,128)(2,1)S(1)} %get-tuple-element.20.psf_ref, bf16[2,2,32,2048]{3,2,1,0:T(8,128)(2,1)S(1)} %copy-done, f32[2,32,2048]{2,1,0:T(8,128)S(1)} %copy-done.1), custom_call_target="tpu_custom_call" | custom-call | flops 200000000 | bytes 1058368 | tf_op jit(solution)/shard_map/pallas_call | solution.py:366
  3.1 0.2 collective-permute-done.got_ref
  3.2 1.1 %shard_map.62 = (f32[2,8,16,128]{3,2,1,0:T(8,128)S(1)}, bf16[2,8,16,128]{3,2,1,0:T(8,128)(2,1)S(1)}, bf16[2,8,16,128]{3,2,1,0:T(8,128)(2,1)S(1)}, bf16[2,8,16,12...) custom-call(bf16[1312,256]{1,0:T(8,128)(2,1)S(1)} %get-tuple-element, ...), custom_call_target="tpu_custom_call", output_to_operand_aliasing={{4}: (0, {}), {5}: (1, {})} | custom-call | flops 2000000000 | bytes 2195456 | tf_op jit(solution)/shard_map/pallas_call | solution.py:366
  4.3 5.0 %collective-permute-start.1 = (bf16[2,8,16,128]{3,2,1,0:T(8,128)(2,1)S(1)}, bf16[2,8,16,128]{3,2,1,0:T(8,128)(2,1)S(1)}, u32[]{:S(2)}, u32[]{:S(2)}) collective-permute-start(bf16[2,8,16,128]{3,2,1,0:T(8,128)(2,1)S(1)} %get-tuple-element.27), channel_id=1, source_target_pairs={{0,12},{4,8},{8,4},{12,0},{1,13},{5,9},{9,5},{13,1},{2,14},{6,10},... | collective-permute-start | bytes 196616 | tf_op jit(solution)/shard_map/ppermute | solution.py:437
  9.4 0.6 %collective-permute-start.3 = (bf16[2,8,16,128]{3,2,1,0:T(8,128)(2,1)S(1)}, bf16[2,8,16,128]{3,2,1,0:T(8,128)(2,1)S(1)}, u32[]{:S(2)}, u32[]{:S(2)}) collective-permute-start(bf16[2,8,16,128]{3,2,1,0:T(8,128)(2,1)S(1)} %get-tuple-element.29), channel_id=1, source_target_pairs={{0,8},{4,12},{8,0},{12,4},{1,9},{5,13},{9,1},{13,5},{2,10},{6,14},... | collective-permute-start | bytes 196616 | tf_op jit(solution)/shard_map/ppermute | solution.py:437
  10.0 1.0 %shard_map.60 = (bf16[9,256,256]{2,1,0:T(8,128)(2,1)S(1)}, f32[2,1,128]{2,1,0:T(1,128)S(1)}, f32[2,8,16,128]{3,2,1,0:T(8,128)S(1)}) custom-call(bf16[2,9,16,17]{3,2,1,0:T(8,128)(2,1)S(1)} %get-tuple-element.20.psf_ref, bf16[2,32,2048]{2,1,0:T(8,128)(2,1)S(1)} %copy-done.2), custom_call_target="tpu_custom_call" | custom-call | flops 200000000 | bytes 271936 | tf_op jit(solution)/shard_map/pallas_call | solution.py:366
  11.0 1.3 %collective-permute-done.1 = bf16[2,8,16,128]{3,2,1,0:T(8,128)(2,1)S(1)} collective-permute-done((bf16[2,8,16,128]{3,2,1,0:T(8,128)(2,1)S(1)}, bf16[2,8,16,128]{3,2,1,0:T(8,128)(2,1)S(1)}, u32[]{:S(2)}, u32[]{:S(2)}) %collective-permute-start.1) | collective-permute-done | bytes 65568 | tf_op jit(solution)/shard_map/ppermute | solution.py:437
  12.3 2.1 %collective-permute-done.2 = bf16[2,8,16,128]{3,2,1,0:T(8,128)(2,1)S(1)} collective-permute-done((bf16[2,8,16,128]{3,2,1,0:T(8,128)(2,1)S(1)}, bf16[2,8,16,128]{3,2,1,0:T(8,128)(2,1)S(1)}, u32[]{:S(2)}, u32[]{:S(2)}) %collective-permute-start.2) | collective-permute-done | bytes 65568 | tf_op jit(solution)/shard_map/ppermute | solution.py:437
  14.4 0.9 %collective-permute-done.3 = bf16[2,8,16,128]{3,2,1,0:T(8,128)(2,1)S(1)} collective-permute-done((bf16[2,8,16,128]{3,2,1,0:T(8,128)(2,1)S(1)}, bf16[2,8,16,128]{3,2,1,0:T(8,128)(2,1)S(1)}, u32[]{:S(2)}, u32[]{:S(2)}) %collective-permute-start.3) | collective-permute-done | bytes 65568 | tf_op jit(solution)/shard_map/ppermute | solution.py:437
  15.3 2.3 %collective-permute-start.4 = (bf16[2,8,16,128]{3,2,1,0:T(8,128)(2,1)S(1)}, bf16[2,8,16,128]{3,2,1,0:T(8,128)(2,1)S(1)}, u32[]{:S(2)}, u32[]{:S(2)}) collective-permute-start(bf16[2,8,16,128]{3,2,1,0:T(8,128)(2,1)S(1)} %divide_convert_fusion.refs_0_), channel_id=1, source_target_pairs={{0,12},{4,8},{8,4},{12,0},{1,13},{5,9},{9,5},{13,1},{2,14},{6,10},... | collective-permute-start | bytes 196616 | tf_op jit(solution)/shard_map/ppermute | solution.py:455
  17.6 0.4 %collective-permute-start.5 = (bf16[2,8,16,128]{3,2,1,0:T(8,128)(2,1)S(1)}, bf16[2,8,16,128]{3,2,1,0:T(8,128)(2,1)S(1)}, u32[]{:S(2)}, u32[]{:S(2)}) collective-permute-start(bf16[2,8,16,128]{3,2,1,0:T(8,128)(2,1)S(1)} %divide_convert_fusion.refs_0_), channel_id=1, source_target_pairs={{0,4},{4,0},{8,12},{12,8},{1,5},{5,1},{9,13},{13,9},{2,6},{6,2},{1... | collective-permute-start | bytes 196616 | tf_op jit(solution)/shard_map/ppermute | solution.py:455
  17.9 1.8 %collective-permute-start.6 = (bf16[2,8,16,128]{3,2,1,0:T(8,128)(2,1)S(1)}, bf16[2,8,16,128]{3,2,1,0:T(8,128)(2,1)S(1)}, u32[]{:S(2)}, u32[]{:S(2)}) collective-permute-start(bf16[2,8,16,128]{3,2,1,0:T(8,128)(2,1)S(1)} %divide_convert_fusion.refs_0_), channel_id=1, source_target_pairs={{0,8},{4,12},{8,0},{12,4},{1,9},{5,13},{9,1},{13,5},{2,10},{6,14},... | collective-permute-start | bytes 196616 | tf_op jit(solution)/shard_map/ppermute | solution.py:455
  19.8 1.9 %collective-permute-done.4.refs_1_ = bf16[2,8,16,128]{3,2,1,0:T(8,128)(2,1)S(1)} collective-permute-done((bf16[2,8,16,128]{3,2,1,0:T(8,128)(2,1)S(1)}, bf16[2,8,16,128]{3,2,1,0:T(8,128)(2,1)S(1)}, u32[]{:S(2)}, u32[]{:S(2)}) %collective-permute-start.4) | collective-permute-done | bytes 65568 | tf_op jit(solution)/shard_map/ppermute | solution.py:455
  21.7 0.9 %collective-permute-done.5.refs_2_ = bf16[2,8,16,128]{3,2,1,0:T(8,128)(2,1)S(1)} collective-permute-done((bf16[2,8,16,128]{3,2,1,0:T(8,128)(2,1)S(1)}, bf16[2,8,16,128]{3,2,1,0:T(8,128)(2,1)S(1)}, u32[]{:S(2)}, u32[]{:S(2)}) %collective-permute-start.5) | collective-permute-done | bytes 65568 | tf_op jit(solution)/shard_map/ppermute | solution.py:455
  22.6 0.6 %collective-permute-done.6.refs_3_ = bf16[2,8,16,128]{3,2,1,0:T(8,128)(2,1)S(1)} collective-permute-done((bf16[2,8,16,128]{3,2,1,0:T(8,128)(2,1)S(1)}, bf16[2,8,16,128]{3,2,1,0:T(8,128)(2,1)S(1)}, u32[]{:S(2)}, u32[]{:S(2)}) %collective-permute-start.6) | collective-permute-done | bytes 65568 | tf_op jit(solution)/shard_map/ppermute | solution.py:455
  23.3 1.6 %collective-permute-start.7 = (bf16[32,16,128]{2,1,0:T(8,128)(2,1)S(1)}, bf16[32,16,128]{2,1,0:T(8,128)(2,1)S(1)}, u32[]{:S(2)}, u32[]{:S(2)}) collective-permute-start(bf16[32,16,128]{2,1,0:T(8,128)(2,1)S(1)} %get-tuple-element.30.summed_ref), channel_id=1, source_target_pairs={{0,2},{2,0},{1,3},{3,1},{4,6},{6,4},{5,7},{7,5},{8,10},{10,8},{9,1... | collective-permute-start | bytes 393224 | tf_op jit(solution)/shard_map/ppermute | solution.py:473
  24.9 0.6 %collective-permute-start.9 = (bf16[4,16,128]{2,1,0:T(8,128)(2,1)S(1)}, bf16[4,16,128]{2,1,0:T(8,128)(2,1)S(1)}, u32[]{:S(2)}, u32[]{:S(2)}) collective-permute-start(bf16[4,16,128]{2,1,0:T(8,128)(2,1)S(1)} %get-tuple-element.33), channel_id=1, source_target_pairs={{0,3},{1,2},{2,1},{3,0},{4,7},{5,6},{6,5},{7,4},{8,11},{9,10},{10,... | collective-permute-start | bytes 49160 | tf_op jit(solution)/shard_map/ppermute | solution.py:474
  25.5 0.6 %collective-permute-done.8.border_ref = bf16[2,4,16,128]{3,2,1,0:T(8,128)(2,1)S(1)} collective-permute-done((bf16[2,4,16,128]{3,2,1,0:T(8,128)(2,1)S(1)}, bf16[2,4,16,128]{3,2,1,0:T(8,128)(2,1)S(1)}, u32[]{:S(2)}, u32[]{:S(2)}) %collective-permute-start.8) | collective-permute-done | bytes 32800 | tf_op jit(solution)/shard_map/ppermute | solution.py:475
  26.1 1.8 %shard_map.65.given_ref = bf16[2,2,32,2048]{3,2,1,0:T(8,128)(2,1)S(1)} custom-call(bf16[2,32,16,128]{3,2,1,0:T(8,128)(2,1)S(1)} %get-tuple-element.31.image_ref, bf16[2,4,16,128]{3,2,1,0:T(8,128)(2,1)S(1)} %collective-permute-done.8.border_ref, bf16[2,2,32,2048]{3,2,1,0:T(8,128)(2,1)S(1)} %copy-done, bf16[9,256,256]{2,1,0:T(8,128)(2,1)S(1)} %get-tuple-element.34.table_ref, ...), custom_call_target="tpu_custom_call" | custom-call | flops 100000000 | bytes 1000000 | tf_op jit(solution)/shard_map/pallas_call | solution.py:366
  27.9 0.4 %collective-permute-done.9.border_got_ref = bf16[4,16,128]{2,1,0:T(8,128)(2,1)S(1)} collective-permute-done((bf16[4,16,128]{2,1,0:T(8,128)(2,1)S(1)}, bf16[4,16,128]{2,1,0:T(8,128)(2,1)S(1)}, u32[]{:S(2)}, u32[]{:S(2)}) %collective-permute-start.9) | collective-permute-done | bytes 16416 | tf_op jit(solution)/shard_map/ppermute | solution.py:474
  28.3 0.2 collective-permute-done.7.got_ref
  28.5 1.7 %shard_map.66 = (f32[2,32,2048]{2,1,0:T(8,128)}, bf16[2,2,32,2048]{3,2,1,0:T(8,128)(2,1)}) custom-call(bf16[32,16,128]{2,1,0:T(8,128)(2,1)S(1)} %get-tuple-element.30.summed_ref, bf16[32,16,128]{2,1,0:T(8,128)(2,1)S(1)} %collective-permute-done.7.got_ref, bf16[4,16,128]{2,1,0:T(8,128)(2,1)S(1)} %reduce_sum.12.border_ref, ...), custom_call_target="tpu_custom_call" | custom-call | flops 1000000000 | bytes 2524160 | tf_op jit(solution)/shard_map/pallas_call | solution.py:366
  (12 shorter events, 0.1 us)
Async XLA Ops:
  0.6 1.7 %copy-start = (bf16[2,2,32,2048]{3,2,1,0:T(8,128)(2,1)S(1)}, bf16[2,2,32,2048]{3,2,1,0:T(8,128)(2,1)}, u32[]{:S(2)}) copy-start(bf16[2,2,32,2048]{3,2,1,0:T(8,128)(2,1)} %volume_ref.5) | copy-start | bytes 1572868
  0.6 1.7 %copy-start.1 = (f32[2,32,2048]{2,1,0:T(8,128)S(1)}, f32[2,32,2048]{2,1,0:T(8,128)}, u32[]{:S(2)}) copy-start(f32[2,32,2048]{2,1,0:T(8,128)} %background_ref.5) | copy-start | bytes 1572868
  1.8 1.4 %collective-permute-start = (bf16[2,2,4,2048]{3,2,1,0:T(4,128)(2,1)S(1)}, bf16[2,2,4,2048]{3,2,1,0:T(4,128)(2,1)S(1)}, u32[]{:S(2)}, u32[]{:S(2)}) collective-permute-start(bf16[2,2,4,2048]{3,2,1,0:T(4,128)(2,1)S(1)} %get-tuple-element.24), channel_id=1, source_target_pairs={{0,1},{1,0},{2,3},{3,2},{4,5},{5,4},{6,7},{7,6},{8,9},{9,8},{10,11... | collective-permute-start | bytes 196616 | tf_op jit(solution)/shard_map/ppermute | solution.py:407
  3.2 6.8 %copy-start.2 = (bf16[2,32,2048]{2,1,0:T(8,128)(2,1)S(1)}, bf16[2,32,2048]{2,1,0:T(8,128)(2,1)}, u32[]{:S(2)}) copy-start(bf16[2,32,2048]{2,1,0:T(8,128)(2,1)} %measured_ref.1) | copy-start | bytes 786436
  4.3 7.9 %collective-permute-start.1 = (bf16[2,8,16,128]{3,2,1,0:T(8,128)(2,1)S(1)}, bf16[2,8,16,128]{3,2,1,0:T(8,128)(2,1)S(1)}, u32[]{:S(2)}, u32[]{:S(2)}) collective-permute-start(bf16[2,8,16,128]{3,2,1,0:T(8,128)(2,1)S(1)} %get-tuple-element.27), channel_id=1, source_target_pairs={{0,12},{4,8},{8,4},{12,0},{1,13},{5,9},{9,5},{13,1},{2,14},{6,10},... | collective-permute-start | bytes 196616 | tf_op jit(solution)/shard_map/ppermute | solution.py:437
  9.4 5.0 %collective-permute-start.2 = (bf16[2,8,16,128]{3,2,1,0:T(8,128)(2,1)S(1)}, bf16[2,8,16,128]{3,2,1,0:T(8,128)(2,1)S(1)}, u32[]{:S(2)}, u32[]{:S(2)}) collective-permute-start(bf16[2,8,16,128]{3,2,1,0:T(8,128)(2,1)S(1)} %get-tuple-element.28), channel_id=1, source_target_pairs={{0,4},{4,0},{8,12},{12,8},{1,5},{5,1},{9,13},{13,9},{2,6},{6,2},{1... | collective-permute-start | bytes 196616 | tf_op jit(solution)/shard_map/ppermute | solution.py:437
  9.4 5.9 %collective-permute-start.3 = (bf16[2,8,16,128]{3,2,1,0:T(8,128)(2,1)S(1)}, bf16[2,8,16,128]{3,2,1,0:T(8,128)(2,1)S(1)}, u32[]{:S(2)}, u32[]{:S(2)}) collective-permute-start(bf16[2,8,16,128]{3,2,1,0:T(8,128)(2,1)S(1)} %get-tuple-element.29), channel_id=1, source_target_pairs={{0,8},{4,12},{8,0},{12,4},{1,9},{5,13},{9,1},{13,5},{2,10},{6,14},... | collective-permute-start | bytes 196616 | tf_op jit(solution)/shard_map/ppermute | solution.py:437
  15.3 6.4 %collective-permute-start.4 = (bf16[2,8,16,128]{3,2,1,0:T(8,128)(2,1)S(1)}, bf16[2,8,16,128]{3,2,1,0:T(8,128)(2,1)S(1)}, u32[]{:S(2)}, u32[]{:S(2)}) collective-permute-start(bf16[2,8,16,128]{3,2,1,0:T(8,128)(2,1)S(1)} %divide_convert_fusion.refs_0_), channel_id=1, source_target_pairs={{0,12},{4,8},{8,4},{12,0},{1,13},{5,9},{9,5},{13,1},{2,14},{6,10},... | collective-permute-start | bytes 196616 | tf_op jit(solution)/shard_map/ppermute | solution.py:455
  17.6 5.0 %collective-permute-start.5 = (bf16[2,8,16,128]{3,2,1,0:T(8,128)(2,1)S(1)}, bf16[2,8,16,128]{3,2,1,0:T(8,128)(2,1)S(1)}, u32[]{:S(2)}, u32[]{:S(2)}) collective-permute-start(bf16[2,8,16,128]{3,2,1,0:T(8,128)(2,1)S(1)} %divide_convert_fusion.refs_0_), channel_id=1, source_target_pairs={{0,4},{4,0},{8,12},{12,8},{1,5},{5,1},{9,13},{13,9},{2,6},{6,2},{1... | collective-permute-start | bytes 196616 | tf_op jit(solution)/shard_map/ppermute | solution.py:455
  17.9 5.3 %collective-permute-start.6 = (bf16[2,8,16,128]{3,2,1,0:T(8,128)(2,1)S(1)}, bf16[2,8,16,128]{3,2,1,0:T(8,128)(2,1)S(1)}, u32[]{:S(2)}, u32[]{:S(2)}) collective-permute-start(bf16[2,8,16,128]{3,2,1,0:T(8,128)(2,1)S(1)} %divide_convert_fusion.refs_0_), channel_id=1, source_target_pairs={{0,8},{4,12},{8,0},{12,4},{1,9},{5,13},{9,1},{13,5},{2,10},{6,14},... | collective-permute-start | bytes 196616 | tf_op jit(solution)/shard_map/ppermute | solution.py:455
  23.3 5.2 %collective-permute-start.7 = (bf16[32,16,128]{2,1,0:T(8,128)(2,1)S(1)}, bf16[32,16,128]{2,1,0:T(8,128)(2,1)S(1)}, u32[]{:S(2)}, u32[]{:S(2)}) collective-permute-start(bf16[32,16,128]{2,1,0:T(8,128)(2,1)S(1)} %get-tuple-element.30.summed_ref), channel_id=1, source_target_pairs={{0,2},{2,0},{1,3},{3,1},{4,6},{6,4},{5,7},{7,5},{8,10},{10,8},{9,1... | collective-permute-start | bytes 393224 | tf_op jit(solution)/shard_map/ppermute | solution.py:473
  24.9 1.2 %collective-permute-start.8 = (bf16[2,4,16,128]{3,2,1,0:T(8,128)(2,1)S(1)}, bf16[2,4,16,128]{3,2,1,0:T(8,128)(2,1)S(1)}, u32[]{:S(2)}, u32[]{:S(2)}) collective-permute-start(bf16[2,4,16,128]{3,2,1,0:T(8,128)(2,1)S(1)} %get-tuple-element.32), channel_id=1, source_target_pairs={{0,1},{1,0},{2,3},{3,2},{4,5},{5,4},{6,7},{7,6},{8,9},{9,8},{10,11... | collective-permute-start | bytes 98312 | tf_op jit(solution)/shard_map/ppermute | solution.py:475
  24.9 3.4 %collective-permute-start.9 = (bf16[4,16,128]{2,1,0:T(8,128)(2,1)S(1)}, bf16[4,16,128]{2,1,0:T(8,128)(2,1)S(1)}, u32[]{:S(2)}, u32[]{:S(2)}) collective-permute-start(bf16[4,16,128]{2,1,0:T(8,128)(2,1)S(1)} %get-tuple-element.33), channel_id=1, source_target_pairs={{0,3},{1,2},{2,1},{3,0},{4,7},{5,6},{6,5},{7,4},{8,11},{9,10},{10,... | collective-permute-start | bytes 49160 | tf_op jit(solution)/shard_map/ppermute | solution.py:474

commit v7 on v6

--- a/solution.py
+++ b/solution.py
@@ -241,14 +241,13 @@
     return 32 * (pair % 2) + 16 * (pair // 2)
 
 
-def spread_ratio(images, row_count, half, blocks, own, border, rows_ref, left_ref):
+def spread_ratio(images, row_count, half, blocks, fill, border, rows_ref, left_ref):
     tile = lax.axis_index("tile")
     masks = edge_masks(blocks, blocks)
     windows = row_count + 2 * half
     for f in range(images):
         first = PAD + f * windows * blocks
-        for r in range(row_count):
-            rows_ref[pl.ds(first + (half + r) * blocks, blocks), :] = own(f, r)
+        fill(f, first + half * blocks)
         for r in range(half):
             at = first + ((row_count + half) * (1 - tile) + r) * blocks
             rows_ref[pl.ds(pl.multiple_of(at, 8), blocks), :] = border(f, r)
@@ -261,30 +260,36 @@
             left_ref[rows, pl.ds(LANES, LANES)] = edges.astype(BF16)
 
 
-def collect_kernel(chunks, *refs):
+def sum_kernel(*refs):
+    for s, chunk_ref in enumerate(refs[:-1]):
+        frames, chunk_rows = chunk_ref.shape[:2]
+        for r in range(chunk_rows):
+            total = chunk_ref[0, r].astype(F32)
+            for f in range(1, frames):
+                total = total + chunk_ref[f, r].astype(F32)
+            refs[-1][s, r] = total.astype(BF16)
+
+
+def collect_kernel(chunks, row_count, *refs):
     ratio_refs = refs[:chunks]
-    image_ref, summed_ref = refs[chunks:]
+    image_ref, border_ref, border_sum_ref = refs[chunks:]
     frames, chunk_rows = ratio_refs[0].shape[:2]
+    half = border_ref.shape[1]
     place = lax.axis_index("depth")
     for s, mask in enumerate(partners(chunks)):
         source = lax.bitwise_xor(place, mask) if s else place
         for r in range(chunk_rows):
-            total = None
             for f in range(frames):
-                values = ratio_refs[s][f, r]
-                image_ref[f, source * chunk_rows + r] = values
-                values = values.astype(F32)
-                total = values if total is None else total + values
-            summed_ref[source * chunk_rows + r] = total.astype(BF16)
-
-
-def edge_kernel(row_count, image_ref, summed_ref, border_ref, border_sum_ref):
-    frames, half = border_ref.shape[:2]
+                image_ref[f, source * chunk_rows + r] = ratio_refs[s][f, r]
     edge = (row_count - half) * (1 - lax.axis_index("tile"))
     for r in range(half):
-        border_sum_ref[r] = summed_ref[edge + r]
+        total = None
         for f in range(frames):
-            border_ref[f, r] = image_ref[f, edge + r]
+            values = image_ref[f, edge + r]
+            border_ref[f, r] = values
+            values = values.astype(F32)
+            total = values if total is None else total + values
+        border_sum_ref[r] = total.astype(BF16)
 
 
 def backproject(f, span, taps, row_count, blocks, left_ref, table_ref):
@@ -301,12 +306,17 @@
     half = border_ref.shape[1]
     blocks = col_count // LANES
     taps = table_ref.shape[0]
+
+    def fill(f, start):
+        for r in range(row_count):
+            rows_ref[pl.ds(start + r * blocks, blocks), :] = image_ref[f, r].astype(F32)
+
     spread_ratio(
         frames,
         row_count,
         half,
         blocks,
-        lambda f, r: image_ref[f, r].astype(F32),
+        fill,
         lambda f, r: border_ref[f, r].astype(F32),
         rows_ref,
         left_ref,
@@ -324,19 +334,30 @@
                 out_ref[f, d, :, lanes] = value.astype(BF16)
 
 
-def background_kernel(scale, summed_ref, got_ref, border_ref, border_got_ref, background_ref, table_ref, inverse_ref, given_ref, out_ref, given_out_ref, rows_ref, left_ref, sums_ref, stage_ref, sems):
+def background_kernel(chunks, scale, late_ref, early_ref, late_got_ref, early_got_ref, border_ref, border_got_ref, background_ref, table_ref, inverse_ref, given_ref, out_ref, given_out_ref, rows_ref, left_ref, sums_ref, stage_ref, sems):
     given = pltpu.make_async_copy(given_ref, given_out_ref, sems.at[0])
     given.start()
     depth, row_count, col_count = background_ref.shape
     half = border_ref.shape[0]
     blocks = col_count // LANES
     taps = table_ref.shape[0]
+    place = lax.axis_index("depth")
+    early, chunk_rows = early_ref.shape[:2]
+
+    def fill(f, start):
+        for s, mask in enumerate(partners(chunks)):
+            source = lax.bitwise_xor(place, mask) if s else place
+            own, got, slot = (early_ref, early_got_ref, s) if s < early else (late_ref, late_got_ref, s - early)
+            for r in range(chunk_rows):
+                at = pl.multiple_of(start + (source * chunk_rows + r) * blocks, 8)
+                rows_ref[pl.ds(at, blocks), :] = own[slot, r].astype(F32) + got[slot, r].astype(F32)
+
     spread_ratio(
         1,
         row_count,
         half,
         blocks,
-        lambda f, r: summed_ref[r].astype(F32) + got_ref[r].astype(F32),
+        fill,
         lambda f, r: border_ref[r].astype(F32) + border_got_ref[r].astype(F32),
         rows_ref,
         left_ref,
@@ -455,31 +476,33 @@
         lax.ppermute(ratio, "depth", [(i, i ^ masks[s]) for i in range(chunks)])
         for s in range(1, chunks)
     ]
-    image, summed = call(
-        functools.partial(collect_kernel, chunks),
+    early = max(1, chunks // 2)
+    pieces = [
+        call(sum_kernel, tuple(part), shape((len(part),) + chunk[1:], BF16), [], 10**6)
+        for part in (ratios[:early], ratios[early:])
+    ]
+    image, edge, edge_sum = call(
+        functools.partial(collect_kernel, chunks, row_count),
         tuple(ratios),
-        (shape((frames, padded_rows, blocks, LANES), BF16), shape((padded_rows, blocks, LANES), BF16)),
+        (
+            shape((frames, padded_rows, blocks, LANES), BF16),
+            shape((frames, half, blocks, LANES), BF16),
+            shape((half, blocks, LANES), BF16),
+        ),
         [],
-        10**6,
-    )
-    edge, edge_sum = call(
-        functools.partial(edge_kernel, row_count),
-        (image, summed),
-        (shape((frames, half, blocks, LANES), BF16), shape((half, blocks, LANES), BF16)),
-        [],
-        1000000000,
+        10**9,
     )
     if splits == 2:
-        got = lax.ppermute(summed, "tm", swap)
+        got = [lax.ppermute(piece, "tm", swap) for piece in pieces]
         other_got = lax.ppermute(edge_sum, ("tm", "tile"), [(i, 3 - i) for i in range(4)])
     edge = lax.ppermute(edge, "tile", swap)
     other = jnp.sum(edge.astype(F32), axis=0)
     if splits == 2:
         other = other.astype(BF16)
     else:
-        summed = lax.psum(summed.astype(F32), "tm").astype(BF16)
+        pieces = [lax.psum(piece.astype(F32), "tm").astype(BF16) for piece in pieces]
         other = lax.psum(other.astype(BF16).astype(F32), "tm").astype(BF16)
-        got, other_got = jnp.zeros_like(summed), jnp.zeros_like(other)
+        got, other_got = [jnp.zeros_like(piece) for piece in pieces], jnp.zeros_like(other)
     new_volume = call(
         volume_kernel,
         (image, edge, volume, backward, inverse),
@@ -492,8 +515,8 @@
         100000000,
     )
     new_background, new_volume = call(
-        functools.partial(background_kernel, 1.0 / (frames * splits)),
-        (summed, got, other, other_got, background, backward, inverse, new_volume),
+        functools.partial(background_kernel, chunks, 1.0 / (frames * splits)),
+        (*pieces[::-1], *got[::-1], other, other_got, background, backward, inverse, new_volume),
         (shape(background.shape, F32), shape(volume.shape, BF16)),
         [
             vmem((windows * blocks + 2 * PAD, LANES), F32),

time: 30.4 us -> 30.1 us (level)
  waiting for transfers between devices: 9.09 us -> 7.11 us
  starting transfers between devices: 12.8 us -> 14.5 us
    ppermute x3, waiting for transfers between devices: 3.49 us -> 1.92 us  [body(): lax.ppermute(ratio, 'depth', [(i, i ^ masks[s]) for i in range(chunks)])]
    ppermute x1 -> x2, starting transfers between devices: 1.56 us -> 3.11 us  [body(): got = [lax.ppermute(piece, 'tm', swap) for piece in pieces]]
    pallas_call x7 -> x8, Pallas kernels: 6.38 us -> 6.41 us  [call(): pl.pallas_call(kernel, out_shape=outs, in_specs=whole(len(args)), out_spe...]
  transfers between devices with their start and end apart: 10 -> 11, of which waited for: 10 -> 7; matrix products, arithmetic and copies ran while one was open for 0% -> 0% of each run, Pallas kernels for 12% -> 12%
where the time goes in v7:
time: 30.1 us; the launch traced here: 29.9 us
  starting transfers between devices  14.5 us (48%)
  Pallas kernels  7.55 us (25%)
  waiting for transfers between devices  7.11 us (24%)
  between operations  0.72 us (2%)
    pallas_call x8, Pallas kernels, call(): pl.pallas_call(kernel, out_shape=outs, in_specs=whole(len(args)), out_spe...  6.41 us
    ppermute x3, starting transfers between devices, body(): lax.ppermute(parts[s], 'depth', [(i, i ^ masks[s]) for i in range(chunks)])  5.67 us
    ppermute x3, starting transfers between devices, body(): lax.ppermute(ratio, 'depth', [(i, i ^ masks[s]) for i in range(chunks)])  4.45 us
    ppermute x3, waiting for transfers between devices, body(): lax.ppermute(parts[s], 'depth', [(i, i ^ masks[s]) for i in range(chunks)])  4.25 us
    ppermute x2, starting transfers between devices, body(): got = [lax.ppermute(piece, 'tm', swap) for piece in pieces]  3.11 us
    ppermute x3, waiting for transfers between devices, body(): lax.ppermute(ratio, 'depth', [(i, i ^ masks[s]) for i in range(chunks)])  1.92 us
    pallas_call x1, Pallas kernels, body(): pl.pallas_call(border_kernel, out_shape=(shape((frames, depth, half, col_...  1.14 us
    ppermute x1, starting transfers between devices, body(): lax.ppermute(edge_sum, ('tm', 'tile'), [(i, 3 - i) for i in range(4)])  0.65 us
  transfers between devices with their start and end apart: 11, of which 7 were waited for; matrix products, arithmetic and copies ran while one was open for 0% of the time, Pallas kernels for 12%

profile of v7, /device:TPU:0, one launch (start us, length us, event | category | flops | bytes accessed | tf_op | source)
XLA Modules:
  0.0 29.9 jit_solution(17317330305858262482)
XLA Ops:
  0.6 1.1 %shard_map.59 = (bf16[2,2,4,2048]{3,2,1,0:T(4,128)(2,1)S(1)}, bf16[2,9,16,17]{3,2,1,0:T(8,128)(2,1)S(1)}) custom-call(bf16[2,2,32,2048]{3,2,1,0:T(8,128)(2,1)} %volume_ref.5, f32[2,32,2048]{2,1,0:T(8,128)} %background_ref.5, bf16[2,9,16,17]{3,2,1,0:T(8,128)(2,1)} %psf_ref.1), custom_call_target="tpu_custom_call" | custom-call | tf_op jit(solution)/shard_map/pallas_call | solution.py:416
  1.8 0.5 %collective-permute-start = (bf16[2,2,4,2048]{3,2,1,0:T(4,128)(2,1)S(1)}, bf16[2,2,4,2048]{3,2,1,0:T(4,128)(2,1)S(1)}, u32[]{:S(2)}, u32[]{:S(2)}) collective-permute-start(bf16[2,2,4,2048]{3,2,1,0:T(4,128)(2,1)S(1)} %get-tuple-element.23), channel_id=1, source_target_pairs={{0,1},{1,0},{2,3},{3,2},{4,5},{5,4},{6,7},{7,6},{8,9},{9,8},{10,11... | collective-permute-start | bytes 196616 | tf_op jit(solution)/shard_map/ppermute | solution.py:428
  2.3 0.7 %shard_map.61 = (bf16[6,256,256]{2,1,0:T(8,128)(2,1)S(1)}, bf16[1312,256]{1,0:T(8,128)(2,1)S(1)}, f32[1312,128]{1,0:T(8,128)S(1)}) custom-call(bf16[2,9,16,17]{3,2,1,0:T(8,128)(2,1)S(1)} %get-tuple-element.19.psf_ref, bf16[2,2,32,2048]{3,2,1,0:T(8,128)(2,1)S(1)} %copy-done, f32[2,32,2048]{2,1,0:T(8,128)S(1)} %copy-done.1), custom_call_target="tpu_custom_call" | custom-call | flops 200000000 | bytes 1058368 | tf_op jit(solution)/shard_map/pallas_call | solution.py:387
  3.1 0.2 collective-permute-done.got_ref
  3.2 1.1 %shard_map.62 = (f32[2,8,16,128]{3,2,1,0:T(8,128)S(1)}, bf16[2,8,16,128]{3,2,1,0:T(8,128)(2,1)S(1)}, bf16[2,8,16,128]{3,2,1,0:T(8,128)(2,1)S(1)}, bf16[2,8,16,12...) custom-call(bf16[1312,256]{1,0:T(8,128)(2,1)S(1)} %get-tuple-element, ...), custom_call_target="tpu_custom_call", output_to_operand_aliasing={{4}: (0, {}), {5}: (1, {})} | custom-call | flops 2000000000 | bytes 2195456 | tf_op jit(solution)/shard_map/pallas_call | solution.py:387
  4.3 5.0 %collective-permute-start.1 = (bf16[2,8,16,128]{3,2,1,0:T(8,128)(2,1)S(1)}, bf16[2,8,16,128]{3,2,1,0:T(8,128)(2,1)S(1)}, u32[]{:S(2)}, u32[]{:S(2)}) collective-permute-start(bf16[2,8,16,128]{3,2,1,0:T(8,128)(2,1)S(1)} %get-tuple-element.26), channel_id=1, source_target_pairs={{0,12},{4,8},{8,4},{12,0},{1,13},{5,9},{9,5},{13,1},{2,14},{6,10},... | collective-permute-start | bytes 196616 | tf_op jit(solution)/shard_map/ppermute | solution.py:458
  9.4 0.6 %collective-permute-start.3 = (bf16[2,8,16,128]{3,2,1,0:T(8,128)(2,1)S(1)}, bf16[2,8,16,128]{3,2,1,0:T(8,128)(2,1)S(1)}, u32[]{:S(2)}, u32[]{:S(2)}) collective-permute-start(bf16[2,8,16,128]{3,2,1,0:T(8,128)(2,1)S(1)} %get-tuple-element.28), channel_id=1, source_target_pairs={{0,8},{4,12},{8,0},{12,4},{1,9},{5,13},{9,1},{13,5},{2,10},{6,14},... | collective-permute-start | bytes 196616 | tf_op jit(solution)/shard_map/ppermute | solution.py:458
  10.0 1.0 %shard_map.60 = (bf16[9,256,256]{2,1,0:T(8,128)(2,1)S(1)}, f32[2,1,128]{2,1,0:T(1,128)S(1)}, f32[2,8,16,128]{3,2,1,0:T(8,128)S(1)}) custom-call(bf16[2,9,16,17]{3,2,1,0:T(8,128)(2,1)S(1)} %get-tuple-element.19.psf_ref, bf16[2,32,2048]{2,1,0:T(8,128)(2,1)S(1)} %copy-done.2), custom_call_target="tpu_custom_call" | custom-call | flops 200000000 | bytes 271936 | tf_op jit(solution)/shard_map/pallas_call | solution.py:387
  11.0 1.3 %collective-permute-done.1 = bf16[2,8,16,128]{3,2,1,0:T(8,128)(2,1)S(1)} collective-permute-done((bf16[2,8,16,128]{3,2,1,0:T(8,128)(2,1)S(1)}, bf16[2,8,16,128]{3,2,1,0:T(8,128)(2,1)S(1)}, u32[]{:S(2)}, u32[]{:S(2)}) %collective-permute-start.1) | collective-permute-done | bytes 65568 | tf_op jit(solution)/shard_map/ppermute | solution.py:458
  12.3 2.1 %collective-permute-done.2 = bf16[2,8,16,128]{3,2,1,0:T(8,128)(2,1)S(1)} collective-permute-done((bf16[2,8,16,128]{3,2,1,0:T(8,128)(2,1)S(1)}, bf16[2,8,16,128]{3,2,1,0:T(8,128)(2,1)S(1)}, u32[]{:S(2)}, u32[]{:S(2)}) %collective-permute-start.2) | collective-permute-done | bytes 65568 | tf_op jit(solution)/shard_map/ppermute | solution.py:458
  14.4 0.9 %collective-permute-done.3 = bf16[2,8,16,128]{3,2,1,0:T(8,128)(2,1)S(1)} collective-permute-done((bf16[2,8,16,128]{3,2,1,0:T(8,128)(2,1)S(1)}, bf16[2,8,16,128]{3,2,1,0:T(8,128)(2,1)S(1)}, u32[]{:S(2)}, u32[]{:S(2)}) %collective-permute-start.3) | collective-permute-done | bytes 65568 | tf_op jit(solution)/shard_map/ppermute | solution.py:458
  15.2 0.1 divide_convert_fusion.refs_0_
  15.3 2.3 %collective-permute-start.6 = (bf16[2,8,16,128]{3,2,1,0:T(8,128)(2,1)S(1)}, bf16[2,8,16,128]{3,2,1,0:T(8,128)(2,1)S(1)}, u32[]{:S(2)}, u32[]{:S(2)}) collective-permute-start(bf16[2,8,16,128]{3,2,1,0:T(8,128)(2,1)S(1)} %divide_convert_fusion.refs_0_), channel_id=1, source_target_pairs={{0,12},{4,8},{8,4},{12,0},{1,13},{5,9},{9,5},{13,1},{2,14},{6,10},... | collective-permute-start | bytes 196616 | tf_op jit(solution)/shard_map/ppermute | solution.py:476
  17.6 0.4 %collective-permute-start.4 = (bf16[2,8,16,128]{3,2,1,0:T(8,128)(2,1)S(1)}, bf16[2,8,16,128]{3,2,1,0:T(8,128)(2,1)S(1)}, u32[]{:S(2)}, u32[]{:S(2)}) collective-permute-start(bf16[2,8,16,128]{3,2,1,0:T(8,128)(2,1)S(1)} %divide_convert_fusion.refs_0_), channel_id=1, source_target_pairs={{0,4},{4,0},{8,12},{12,8},{1,5},{5,1},{9,13},{13,9},{2,6},{6,2},{1... | collective-permute-start | bytes 196616 | tf_op jit(solution)/shard_map/ppermute | solution.py:476
  17.9 1.8 %collective-permute-start.5 = (bf16[2,8,16,128]{3,2,1,0:T(8,128)(2,1)S(1)}, bf16[2,8,16,128]{3,2,1,0:T(8,128)(2,1)S(1)}, u32[]{:S(2)}, u32[]{:S(2)}) collective-permute-start(bf16[2,8,16,128]{3,2,1,0:T(8,128)(2,1)S(1)} %divide_convert_fusion.refs_0_), channel_id=1, source_target_pairs={{0,8},{4,12},{8,0},{12,4},{1,9},{5,13},{9,1},{13,5},{2,10},{6,14},... | collective-permute-start | bytes 196616 | tf_op jit(solution)/shard_map/ppermute | solution.py:476
  19.8 1.9 %collective-permute-done.6.refs_1_ = bf16[2,8,16,128]{3,2,1,0:T(8,128)(2,1)S(1)} collective-permute-done((bf16[2,8,16,128]{3,2,1,0:T(8,128)(2,1)S(1)}, bf16[2,8,16,128]{3,2,1,0:T(8,128)(2,1)S(1)}, u32[]{:S(2)}, u32[]{:S(2)}) %collective-permute-start.6) | collective-permute-done | bytes 65568 | tf_op jit(solution)/shard_map/ppermute | solution.py:476
  21.7 1.6 %collective-permute-start.8 = (bf16[2,8,16,128]{3,2,1,0:T(8,128)(2,1)S(1)}, bf16[2,8,16,128]{3,2,1,0:T(8,128)(2,1)S(1)}, u32[]{:S(2)}, u32[]{:S(2)}) collective-permute-start(bf16[2,8,16,128]{3,2,1,0:T(8,128)(2,1)S(1)} %shard_map.64.early_ref), channel_id=1, source_target_pairs={{0,2},{2,0},{1,3},{3,1},{4,6},{6,4},{5,7},{7,5},{8,10},{10,8},{9,1... | collective-permute-start | bytes 196616 | tf_op jit(solution)/shard_map/ppermute | solution.py:496
  23.3 1.6 %collective-permute-start.7 = (bf16[2,8,16,128]{3,2,1,0:T(8,128)(2,1)S(1)}, bf16[2,8,16,128]{3,2,1,0:T(8,128)(2,1)S(1)}, u32[]{:S(2)}, u32[]{:S(2)}) collective-permute-start(bf16[2,8,16,128]{3,2,1,0:T(8,128)(2,1)S(1)} %shard_map.63.late_ref), channel_id=1, source_target_pairs={{0,2},{2,0},{1,3},{3,1},{4,6},{6,4},{5,7},{7,5},{8,10},{10,8},{9,1... | collective-permute-start | bytes 196616 | tf_op jit(solution)/shard_map/ppermute | solution.py:496
  24.9 0.1 collective-permute-start.9
  24.9 0.6 %collective-permute-start.10 = (bf16[4,16,128]{2,1,0:T(8,128)(2,1)S(1)}, bf16[4,16,128]{2,1,0:T(8,128)(2,1)S(1)}, u32[]{:S(2)}, u32[]{:S(2)}) collective-permute-start(bf16[4,16,128]{2,1,0:T(8,128)(2,1)S(1)} %get-tuple-element.30), channel_id=1, source_target_pairs={{0,3},{1,2},{2,1},{3,0},{4,7},{5,6},{6,5},{7,4},{8,11},{9,10},{10,... | collective-permute-start | bytes 49160 | tf_op jit(solution)/shard_map/ppermute | solution.py:497
  25.6 0.5 %collective-permute-done.9.border_ref = bf16[2,4,16,128]{3,2,1,0:T(8,128)(2,1)S(1)} collective-permute-done((bf16[2,4,16,128]{3,2,1,0:T(8,128)(2,1)S(1)}, bf16[2,4,16,128]{3,2,1,0:T(8,128)(2,1)S(1)}, u32[]{:S(2)}, u32[]{:S(2)}) %collective-permute-start.9) | collective-permute-done | bytes 32800 | tf_op jit(solution)/shard_map/ppermute | solution.py:498
  26.2 1.8 %shard_map.66.given_ref = bf16[2,2,32,2048]{3,2,1,0:T(8,128)(2,1)S(1)} custom-call(bf16[2,32,16,128]{3,2,1,0:T(8,128)(2,1)S(1)} %get-tuple-element.33.image_ref, bf16[2,4,16,128]{3,2,1,0:T(8,128)(2,1)S(1)} %collective-permute-done.9.border_ref, bf16[2,2,32,2048]{3,2,1,0:T(8,128)(2,1)S(1)} %copy-done, bf16[9,256,256]{2,1,0:T(8,128)(2,1)S(1)} %get-tuple-element.31.table_ref, ...), custom_call_target="tpu_custom_call" | custom-call | flops 100000000 | bytes 1000000 | tf_op jit(solution)/shard_map/pallas_call | solution.py:387
  27.9 0.2 collective-permute-done.10.border_got_ref
  28.2 1.7 %shard_map.67 = (f32[2,32,2048]{2,1,0:T(8,128)}, bf16[2,2,32,2048]{3,2,1,0:T(8,128)(2,1)}) custom-call(bf16[2,8,16,128]{3,2,1,0:T(8,128)(2,1)S(1)} %shard_map.63.late_ref, bf16[2,8,16,128]{3,2,1,0:T(8,128)(2,1)S(1)} %shard_map.64.early_ref, bf16[2,8,16,128]{3,2,1,0:T(8,128)(2,1)S(1)} %collective-permute-done.7.late_got_ref, ...), custom_call_target="tpu_custom_call" | custom-call | flops 1000000000 | bytes 2524160 | tf_op jit(solution)/shard_map/pallas_call | solution.py:387
  (15 shorter events, 0.1 us)
Async XLA Ops:
  0.6 1.7 %copy-start = (bf16[2,2,32,2048]{3,2,1,0:T(8,128)(2,1)S(1)}, bf16[2,2,32,2048]{3,2,1,0:T(8,128)(2,1)}, u32[]{:S(2)}) copy-start(bf16[2,2,32,2048]{3,2,1,0:T(8,128)(2,1)} %volume_ref.5) | copy-start | bytes 1572868
  0.6 1.7 %copy-start.1 = (f32[2,32,2048]{2,1,0:T(8,128)S(1)}, f32[2,32,2048]{2,1,0:T(8,128)}, u32[]{:S(2)}) copy-start(f32[2,32,2048]{2,1,0:T(8,128)} %background_ref.5) | copy-start | bytes 1572868
  1.8 1.4 %collective-permute-start = (bf16[2,2,4,2048]{3,2,1,0:T(4,128)(2,1)S(1)}, bf16[2,2,4,2048]{3,2,1,0:T(4,128)(2,1)S(1)}, u32[]{:S(2)}, u32[]{:S(2)}) collective-permute-start(bf16[2,2,4,2048]{3,2,1,0:T(4,128)(2,1)S(1)} %get-tuple-element.23), channel_id=1, source_target_pairs={{0,1},{1,0},{2,3},{3,2},{4,5},{5,4},{6,7},{7,6},{8,9},{9,8},{10,11... | collective-permute-start | bytes 196616 | tf_op jit(solution)/shard_map/ppermute | solution.py:428
  3.2 6.8 %copy-start.2 = (bf16[2,32,2048]{2,1,0:T(8,128)(2,1)S(1)}, bf16[2,32,2048]{2,1,0:T(8,128)(2,1)}, u32[]{:S(2)}) copy-start(bf16[2,32,2048]{2,1,0:T(8,128)(2,1)} %measured_ref.1) | copy-start | bytes 786436
  4.3 7.9 %collective-permute-start.1 = (bf16[2,8,16,128]{3,2,1,0:T(8,128)(2,1)S(1)}, bf16[2,8,16,128]{3,2,1,0:T(8,128)(2,1)S(1)}, u32[]{:S(2)}, u32[]{:S(2)}) collective-permute-start(bf16[2,8,16,128]{3,2,1,0:T(8,128)(2,1)S(1)} %get-tuple-element.26), channel_id=1, source_target_pairs={{0,12},{4,8},{8,4},{12,0},{1,13},{5,9},{9,5},{13,1},{2,14},{6,10},... | collective-permute-start | bytes 196616 | tf_op jit(solution)/shard_map/ppermute | solution.py:458
  9.4 5.0 %collective-permute-start.2 = (bf16[2,8,16,128]{3,2,1,0:T(8,128)(2,1)S(1)}, bf16[2,8,16,128]{3,2,1,0:T(8,128)(2,1)S(1)}, u32[]{:S(2)}, u32[]{:S(2)}) collective-permute-start(bf16[2,8,16,128]{3,2,1,0:T(8,128)(2,1)S(1)} %get-tuple-element.27), channel_id=1, source_target_pairs={{0,4},{4,0},{8,12},{12,8},{1,5},{5,1},{9,13},{13,9},{2,6},{6,2},{1... | collective-permute-start | bytes 196616 | tf_op jit(solution)/shard_map/ppermute | solution.py:458
  9.4 5.9 %collective-permute-start.3 = (bf16[2,8,16,128]{3,2,1,0:T(8,128)(2,1)S(1)}, bf16[2,8,16,128]{3,2,1,0:T(8,128)(2,1)S(1)}, u32[]{:S(2)}, u32[]{:S(2)}) collective-permute-start(bf16[2,8,16,128]{3,2,1,0:T(8,128)(2,1)S(1)} %get-tuple-element.28), channel_id=1, source_target_pairs={{0,8},{4,12},{8,0},{12,4},{1,9},{5,13},{9,1},{13,5},{2,10},{6,14},... | collective-permute-start | bytes 196616 | tf_op jit(solution)/shard_map/ppermute | solution.py:458
  15.3 6.4 %collective-permute-start.6 = (bf16[2,8,16,128]{3,2,1,0:T(8,128)(2,1)S(1)}, bf16[2,8,16,128]{3,2,1,0:T(8,128)(2,1)S(1)}, u32[]{:S(2)}, u32[]{:S(2)}) collective-permute-start(bf16[2,8,16,128]{3,2,1,0:T(8,128)(2,1)S(1)} %divide_convert_fusion.refs_0_), channel_id=1, source_target_pairs={{0,12},{4,8},{8,4},{12,0},{1,13},{5,9},{9,5},{13,1},{2,14},{6,10},... | collective-permute-start | bytes 196616 | tf_op jit(solution)/shard_map/ppermute | solution.py:476
  17.6 5.7 %collective-permute-start.4 = (bf16[2,8,16,128]{3,2,1,0:T(8,128)(2,1)S(1)}, bf16[2,8,16,128]{3,2,1,0:T(8,128)(2,1)S(1)}, u32[]{:S(2)}, u32[]{:S(2)}) collective-permute-start(bf16[2,8,16,128]{3,2,1,0:T(8,128)(2,1)S(1)} %divide_convert_fusion.refs_0_), channel_id=1, source_target_pairs={{0,4},{4,0},{8,12},{12,8},{1,5},{5,1},{9,13},{13,9},{2,6},{6,2},{1... | collective-permute-start | bytes 196616 | tf_op jit(solution)/shard_map/ppermute | solution.py:476
  17.9 5.3 %collective-permute-start.5 = (bf16[2,8,16,128]{3,2,1,0:T(8,128)(2,1)S(1)}, bf16[2,8,16,128]{3,2,1,0:T(8,128)(2,1)S(1)}, u32[]{:S(2)}, u32[]{:S(2)}) collective-permute-start(bf16[2,8,16,128]{3,2,1,0:T(8,128)(2,1)S(1)} %divide_convert_fusion.refs_0_), channel_id=1, source_target_pairs={{0,8},{4,12},{8,0},{12,4},{1,9},{5,13},{9,1},{13,5},{2,10},{6,14},... | collective-permute-start | bytes 196616 | tf_op jit(solution)/shard_map/ppermute | solution.py:476
  21.7 6.5 %collective-permute-start.8 = (bf16[2,8,16,128]{3,2,1,0:T(8,128)(2,1)S(1)}, bf16[2,8,16,128]{3,2,1,0:T(8,128)(2,1)S(1)}, u32[]{:S(2)}, u32[]{:S(2)}) collective-permute-start(bf16[2,8,16,128]{3,2,1,0:T(8,128)(2,1)S(1)} %shard_map.64.early_ref), channel_id=1, source_target_pairs={{0,2},{2,0},{1,3},{3,1},{4,6},{6,4},{5,7},{7,5},{8,10},{10,8},{9,1... | collective-permute-start | bytes 196616 | tf_op jit(solution)/shard_map/ppermute | solution.py:496
  23.3 4.9 %collective-permute-start.7 = (bf16[2,8,16,128]{3,2,1,0:T(8,128)(2,1)S(1)}, bf16[2,8,16,128]{3,2,1,0:T(8,128)(2,1)S(1)}, u32[]{:S(2)}, u32[]{:S(2)}) collective-permute-start(bf16[2,8,16,128]{3,2,1,0:T(8,128)(2,1)S(1)} %shard_map.63.late_ref), channel_id=1, source_target_pairs={{0,2},{2,0},{1,3},{3,1},{4,6},{6,4},{5,7},{7,5},{8,10},{10,8},{9,1... | collective-permute-start | bytes 196616 | tf_op jit(solution)/shard_map/ppermute | solution.py:496
  24.9 1.3 %collective-permute-start.9 = (bf16[2,4,16,128]{3,2,1,0:T(8,128)(2,1)S(1)}, bf16[2,4,16,128]{3,2,1,0:T(8,128)(2,1)S(1)}, u32[]{:S(2)}, u32[]{:S(2)}) collective-permute-start(bf16[2,4,16,128]{3,2,1,0:T(8,128)(2,1)S(1)} %get-tuple-element.29), channel_id=1, source_target_pairs={{0,1},{1,0},{2,3},{3,2},{4,5},{5,4},{6,7},{7,6},{8,9},{9,8},{10,11... | collective-permute-start | bytes 98312 | tf_op jit(solution)/shard_map/ppermute | solution.py:498
  24.9 3.2 %collective-permute-start.10 = (bf16[4,16,128]{2,1,0:T(8,128)(2,1)S(1)}, bf16[4,16,128]{2,1,0:T(8,128)(2,1)S(1)}, u32[]{:S(2)}, u32[]{:S(2)}) collective-permute-start(bf16[4,16,128]{2,1,0:T(8,128)(2,1)S(1)} %get-tuple-element.30), channel_id=1, source_target_pairs={{0,3},{1,2},{2,1},{3,0},{4,7},{5,6},{6,5},{7,4},{8,11},{9,10},{10,... | collective-permute-start | bytes 49160 | tf_op jit(solution)/shard_map/ppermute | solution.py:497
